TPU v7x, 256 devices: a whole 4x4x8 slice. The times are simulated.
256 devices in a mesh: ctx: 32 (over z, x), head: 8 (over y, core).
Axes of the slice: x: 4, y: 4, z: 8, core: 2. Of those that a mesh axis runs over, the one named last changes fastest.
Arguments:
- tokens: bfloat16 [131072, 1024], P(('ctx', 'head')), may hold values from -16 to 16
- w_query: bfloat16 [1024, 1024], replicated, may hold values from -0.4375 to 0.4375
- w_key: bfloat16 [1024, 1024], replicated, may hold values from -0.1875 to 0.1875
- w_value: bfloat16 [1024, 1024], replicated, may hold values from -0.1875 to 0.1875
- w_out: bfloat16 [1024, 1024], replicated, may hold values from -0.1875 to 0.1875
- random_tiles: int32 [1024, 12], replicated, may hold values from 2 to 1023, as said below
- random_count: int32 [1024], replicated, may hold values from 1 to 12, as said below
Outputs:
- sublayer_out: bfloat16 [131072, 1024], P(('ctx', 'head'))
Inputs may be any that keep to these rules, and one draw needn't show every extreme that they name: `random_tiles`: entry [t, j] names a tile of the sequence (tiles of ctx shard c are c * 32 to (c + 1) * 32 - 1). Entries j < random_count[t] are live: distinct within a row, never one of the first 2 tiles, and never on query tile t's own ctx shard; later entries are padding, drawn in the same way. The live entries of the 32 query tiles of one ctx shard name at most 3 distinct tiles on any one ctx shard, and in every draw some ctx shard names exactly 3 on each of the 31 other shards. `random_count`: number of live entries in each row of random_tiles; in every draw all counts of some ctx shard equal 12.
All inputs are finite; a program needn't handle non-finite values.
Results may differ from a plain program's by a relative error of at most 0.011.
Values may be sent and summed in bfloat16 or wider, within the bound.
No kernel may reach another device: no remote copies, remote signals or barrier semaphores. Data moves between devices by JAX's collectives and lax.ppermute only.
A program may use at most 128 MiB of HBM per device.

v0:
```python
import math

import jax
import jax.numpy as jnp
from jax import lax
from jax.sharding import PartitionSpec as P

HEADS = 16
HEAD_DIM = 64
TILE = 128
GLOBALS = 2
RANDOM = 12
CAP = 3


def padded_2(x, sides, width):
    for axis, dim in sides:
        size, length = (lax.axis_size(axis), x.shape[dim])
        up = [(i, (i + 1) % size) for i in range(size - 1)]
        down = [(j, i) for i, j in up]
        last = lax.slice_in_dim(x, length - width, length, axis=dim)
        initial = lax.slice_in_dim(x, 0, width, axis=dim)
        before = lax.ppermute(last, axis, up)
        after = lax.ppermute(initial, axis, down)
        x = jnp.concatenate([before, x, after], axis=dim)
    return x


def from_root(value, axis, source):
    kept = jnp.where(lax.axis_index(axis) == source, value, 0).astype(value.dtype)
    return lax.psum(kept, axis)


def fetch_requested(packed, random_tiles, random_count, shard_index, ctx_count, tiles_here):
    tiles_total = random_tiles.shape[0]
    lane_count = packed.shape[1]
    live_all = (jnp.arange(RANDOM)[None, :] < random_count[:, None]).astype(jnp.int32)
    owners = (jnp.arange(tiles_total, dtype=jnp.int32) // tiles_here)[:, None]
    flat_index = (owners * tiles_total + random_tiles).reshape(-1)
    wanted = (
        jnp.zeros((ctx_count * tiles_total,), jnp.int32).at[flat_index].max(live_all.reshape(-1))
    )
    wanted = wanted.reshape(ctx_count, tiles_total)
    owned = lax.dynamic_slice_in_dim(wanted, shard_index * tiles_here, tiles_here, 1)
    ranking = jnp.cumsum(owned, axis=1) - 1
    select = (owned[:, None, :] > 0) & (ranking[:, None, :] == jnp.arange(CAP)[None, :, None])
    outgoing = jnp.einsum(
        "dck,kx->dcx",
        select.astype(jnp.bfloat16),
        packed.reshape(tiles_here, TILE * lane_count),
        preferred_element_type=jnp.float32,
    ).astype(jnp.bfloat16)
    incoming = lax.all_to_all(outgoing, "ctx", split_axis=0, concat_axis=0, tiled=True)
    needed_here = lax.dynamic_index_in_dim(wanted, shard_index, 0, keepdims=False).reshape(
        ctx_count, tiles_here
    )
    before = (jnp.cumsum(needed_here, axis=1) - needed_here).reshape(-1)
    my_tiles = lax.dynamic_slice_in_dim(random_tiles, shard_index * tiles_here, tiles_here, 0)
    my_count = lax.dynamic_slice_in_dim(random_count, shard_index * tiles_here, tiles_here, 0)
    live_slots = jnp.arange(RANDOM)[None, :] < my_count[:, None]
    slot_index = my_tiles // tiles_here * CAP + before[my_tiles]
    slot_index = jnp.where(live_slots, slot_index, 0)
    return incoming.reshape(ctx_count * CAP, TILE, lane_count)[slot_index]


def body(tokens, w_query, w_key, w_value, w_out, random_tiles, random_count):
    head_count = lax.axis_size("head")
    ctx_count = lax.axis_size("ctx")
    local_heads = HEADS // head_count
    half_lanes = local_heads * HEAD_DIM
    queries = jnp.dot(tokens, w_query, preferred_element_type=jnp.float32).astype(jnp.bfloat16)
    key_rows = jnp.dot(tokens, w_key, preferred_element_type=jnp.float32).astype(jnp.bfloat16)
    value_rows = jnp.dot(tokens, w_value, preferred_element_type=jnp.float32).astype(jnp.bfloat16)
    queries, key_rows, value_rows = (
        lax.all_to_all(queries, "head", split_axis=1, concat_axis=0, tiled=True),
        lax.all_to_all(key_rows, "head", split_axis=1, concat_axis=0, tiled=True),
        lax.all_to_all(value_rows, "head", split_axis=1, concat_axis=0, tiled=True),
    )
    span_rows = queries.shape[0]
    tiles_here = span_rows // TILE
    tiles_total = tiles_here * ctx_count
    packed = jnp.concatenate([key_rows, value_rows], axis=1)
    lane_count = packed.shape[1]
    padded = padded_2(packed, (("ctx", 0),), TILE)
    global_kv = from_root(packed[: GLOBALS * TILE], "ctx", 0)
    shard_index = lax.axis_index("ctx")
    first_tile = shard_index * tiles_here
    my_count = lax.dynamic_slice_in_dim(random_count, first_tile, tiles_here, 0)
    live_slots = jnp.arange(RANDOM)[None, :] < my_count[:, None]
    picked = fetch_requested(packed, random_tiles, random_count, shard_index, ctx_count, tiles_here)
    windows = jnp.stack(
        [
            padded[offset * TILE : offset * TILE + span_rows].reshape(tiles_here, TILE, lane_count)
            for offset in range(3)
        ],
        axis=1,
    )
    tile_global = first_tile + jnp.arange(tiles_here, dtype=jnp.int32)
    window_ids = tile_global[:, None] - 1 + jnp.arange(3, dtype=jnp.int32)[None, :]
    window_ok = (window_ids >= GLOBALS) & (window_ids < tiles_total)
    group_size = math.gcd(tiles_here, 4)
    blocks = tiles_here // group_size
    score_scale = HEAD_DIM ** (-0.5)
    query_groups = queries.reshape(blocks, group_size, TILE, local_heads, HEAD_DIM)
    window_groups = windows.reshape(blocks, group_size, 3 * TILE, lane_count)
    random_groups = picked.reshape(blocks, group_size, RANDOM * TILE, lane_count)
    window_flags = window_ok.reshape(blocks, group_size, 3)
    random_flags = live_slots.reshape(blocks, group_size, RANDOM)

    def attend(inputs):
        query_block, window_block, random_block, window_mask, random_mask = inputs
        global_block = jnp.broadcast_to(global_kv[None], (group_size,) + global_kv.shape)
        kv_block = jnp.concatenate([window_block, global_block, random_block], axis=1)
        key_block = kv_block[..., :half_lanes].reshape(group_size, -1, local_heads, HEAD_DIM)
        value_block = kv_block[..., half_lanes:].reshape(group_size, -1, local_heads, HEAD_DIM)
        key_ok = jnp.concatenate(
            [
                jnp.repeat(window_mask, TILE, axis=1),
                jnp.ones((group_size, GLOBALS * TILE), jnp.bool_),
                jnp.repeat(random_mask, TILE, axis=1),
            ],
            axis=1,
        )
        scores = (
            jnp.einsum(
                "tqhd,tkhd->thqk", query_block, key_block, preferred_element_type=jnp.float32
            )
            * score_scale
        )
        scores = jnp.where(key_ok[:, None, None, :], scores, -1e30)
        maxima = jnp.max(scores, axis=-1, keepdims=True)
        weights = jnp.exp(scores - maxima)
        totals = jnp.sum(weights, axis=-1, keepdims=True)
        blended = jnp.einsum(
            "thqk,tkhd->tqhd",
            weights.astype(jnp.bfloat16),
            value_block,
            preferred_element_type=jnp.float32,
        )
        return (blended / jnp.transpose(totals, (0, 2, 1, 3))).astype(jnp.bfloat16)

    attended = lax.map(
        attend, (query_groups, window_groups, random_groups, window_flags, random_flags)
    )
    attended = attended.reshape(span_rows, half_lanes)
    returned = lax.all_to_all(attended, "head", split_axis=0, concat_axis=1, tiled=True)
    return jnp.dot(returned, w_out, preferred_element_type=jnp.float32).astype(jnp.bfloat16)


def solution(mesh):
    return jax.shard_map(
        body,
        mesh=mesh,
        in_specs=(P(("ctx", "head"), None), P(), P(), P(), P(), P(), P()),
        out_specs=P(("ctx", "head"), None),
        check_vma=False,
    )
```

profile of v0, /device:TPU:1, one launch (start us, length us, event | category | flops | bytes accessed | tf_op | source)
XLA Modules:
  0.0 622.0 jit_solution(13592844951943769095)
XLA Ops:
  11.8 6.7 %all-to-all-start = ((bf16[512,8,128]{2,0,1:T(8,128)(2,1)}), bf16[512,8,128]{2,0,1:T(8,128)(2,1)S(1)}, u32[]{:S(2)}, u32[]{:S(2)}) async-start(bf16[512,8,128]{2,0,1:T(8,128)(2,1)} %bitcast.80), calls=%async_computation | async-start | bytes 2097152 | tf_op jit(solution)/shard_map/all_to_all | solution.py:76
  23.2 10.3 %all-to-all-done = bf16[512,8,128]{2,0,1:T(8,128)(2,1)S(1)} async-done(((bf16[512,8,128]{2,0,1:T(8,128)(2,1)}), bf16[512,8,128]{2,0,1:T(8,128)(2,1)S(1)}, u32[]{:S(2)}, u32[]{:S(2)}) %all-to-all-start) | async-done | bytes 1048608 | tf_op jit(solution)/shard_map/all_to_all | solution.py:76
  33.4 4.4 all-to-all-start.1
  38.5 85.2 %scatter_custom_fusion = s32[32768]{0:T(1024)S(1)} fusion(s32[12288]{0:T(1024)S(1)} %bitcast.127, s32[12288]{0:T(1024)S(1)} %reshape.177, s32[]{:T(128)} %copy.88), kind=kCustom, calls=%fused_computation.57 | custom fusion | flops 12288 | bytes 131076 | tf_op jit(solution)/shard_map/scatter-max | solution.py:41
  129.1 4.8 all-to-all-start.3
  139.3 3.9 collective-permute-done.1
  143.2 6.2 %pad_maximum_fusion.2 = (bf16[4096,256]{0,1:T(8,128)(2,1)}, bf16[4096,256]{0,1:T(8,128)(2,1)}, bf16[4096,256]{0,1:T(8,128)(2,1)}) fusion(bf16[4096,128]{0,1:T(8,128)(2,1)S(1)} %copy.33, bf16[4096,128]{0,1:T(8,128)(2,1)S(1)} %copy.32, bf16[128,256]{0,1:T(8,128)(2,1)S(1)} %collective-permute-done.1, bf16[128,256]{0,1:T(8,128)(2,1)S(1)} %collective-permute-done), kind=kLoop, calls=%fused_computation.34 | loop fusion | flops 16777216 | bytes 8519680 | tf_op jit(solution)/shard_map/concatenate | solution.py:82
  149.5 4.1 copy.38
  153.5 4.2 reshape.186
  157.7 6.0 convolution_convert_fusion
  163.8 11.4 %copy.39 = bf16[32,3,32768]{2,1,0:T(4,128)(2,1)} copy(bf16[32,3,32768]{2,0,1:T(8,128)(2,1)} %convolution_convert_fusion) | data formatting | bytes 12582912 | tf_op jit(solution)/shard_map/convert_element_type | solution.py:52
  175.2 12.8 %all-to-all-start.2 = ((bf16[32,3,32768]{2,1,0:T(4,128)(2,1)}), bf16[32,3,32768]{2,1,0:T(4,128)(2,1)}, u32[]{:S(2)}, u32[]{:S(2)}) async-start(bf16[32,3,32768]{2,1,0:T(4,128)(2,1)} %copy.39), calls=%async_computation.2 | async-start | bytes 16777216 | tf_op jit(solution)/shard_map/all_to_all | solution.py:53
  195.4 4.2 copy.34
  199.6 4.1 copy.35
  209.9 169.2 %all-to-all-done.2 = bf16[32,3,32768]{2,1,0:T(4,128)(2,1)} async-done(((bf16[32,3,32768]{2,1,0:T(4,128)(2,1)}), bf16[32,3,32768]{2,1,0:T(4,128)(2,1)}, u32[]{:S(2)}, u32[]{:S(2)}) %all-to-all-start.2) | async-done | bytes 6291488 | tf_op jit(solution)/shard_map/all_to_all | solution.py:53
  379.1 15.3 %reshape.151 = bf16[96,128,256]{2,1,0:T(8,128)(2,1)} reshape(bf16[32,3,32768]{2,1,0:T(4,128)(2,1)} %all-to-all-done.2) | data formatting | bytes 12582912 | tf_op jit(solution)/shard_map/reshape | solution.py:63
  394.4 15.5 %gather_fusion.1 = bf16[384,128,256]{2,1,0:T(8,128)(2,1)} fusion(bf16[96,128,256]{2,1,0:T(8,128)(2,1)} %reshape.151, s32[1024]{0:T(1024)S(1)} %pad_clamp_fusion), kind=kCustom, calls=%fused_computation.1 | custom fusion | bytes 50333184 | tf_op jit(solution)/shard_map/gather | solution.py:63
  410.0 179.5 %while.10 = (s32[]{:T(128)}, bf16[8,4,128,2,64]{2,1,4,3,0:T(4,128)(2,1)}, bf16[8,4,384,256]{3,2,1,0:T(8,128)(2,1)}, bf16[256,256]{0,1:T(8,128)(2,1)}, bf16[8,4,1...) while((s32[]{:T(128)}, ...), condition=%wide.region_7.8_spmd, body=%wide.region_4.7_spmd.sunk | while | flops 608451584 | bytes 75717248 | solution.py:142
  410.0 3.7 constant_dynamic-slice_fusion.11
  413.7 3.2 copy.75
  432.4 3.7 constant_dynamic-slice_fusion.11
  436.1 3.2 copy.75
  454.9 3.7 constant_dynamic-slice_fusion.11
  458.6 3.2 copy.75
  477.3 3.7 constant_dynamic-slice_fusion.11
  481.0 3.2 copy.75
  499.7 3.7 constant_dynamic-slice_fusion.11
  522.2 3.7 constant_dynamic-slice_fusion.11
  544.6 3.7 constant_dynamic-slice_fusion.11
  567.0 3.7 constant_dynamic-slice_fusion.11
  591.1 20.2 %all_to_all.78 = bf16[8,512,128]{1,2,0:T(8,128)(2,1)S(1)} all-to-all(bf16[8,512,128]{1,2,0:T(8,128)(2,1)S(1)} %all_to_all.69), channel_id=1, replica_groups=mesh['ctx'=32,'head'=8] {'head'}, dimensions={0} | all-to-all | bytes 2097152 | tf_op jit(solution)/shard_map/all_to_all | solution.py:146
  611.3 3.9 convolution_convert_fusion.1
  (257 shorter events, 172.7 us)
Async XLA Ops:
  6.5 1.6 copy-start
  6.5 11.9 %copy-start.6 = (s32[1024,12]{0,1:T(8,128)S(1)}, s32[1024,12]{0,1:T(8,128)}, u32[]{:S(2)}) copy-start(s32[1024,12]{0,1:T(8,128)} %param.14) | copy-start | bytes 147460
  10.6 8.5 %copy-start.8 = (bf16[512,1024]{1,0:T(8,128)(2,1)S(1)}, bf16[512,1024]{1,0:T(8,128)(2,1)}, u32[]{:S(2)}) copy-start(bf16[512,1024]{1,0:T(8,128)(2,1)} %param.9) | copy-start | bytes 3145732
  11.8 21.7 %all-to-all-start = ((bf16[512,8,128]{2,0,1:T(8,128)(2,1)}), bf16[512,8,128]{2,0,1:T(8,128)(2,1)S(1)}, u32[]{:S(2)}, u32[]{:S(2)}) async-start(bf16[512,8,128]{2,0,1:T(8,128)(2,1)} %bitcast.80), calls=%async_computation | async-start | bytes 2097152 | tf_op jit(solution)/shard_map/all_to_all | solution.py:76
  19.1 18.8 %copy-start.7 = (s32[1024]{0:T(1024)S(1)}, s32[1024]{0:T(1024)}, u32[]{:S(2)}) copy-start(s32[1024]{0:T(1024)} %param.15) | copy-start | bytes 12292
  33.4 95.6 %all-to-all-start.1 = ((bf16[512,8,128]{2,0,1:T(8,128)(2,1)}), bf16[512,8,128]{2,0,1:T(8,128)(2,1)S(1)}, u32[]{:S(2)}, u32[]{:S(2)}) async-start(bf16[512,8,128]{2,0,1:T(8,128)(2,1)} %bitcast.79), calls=%async_computation.1 | async-start | bytes 2097152 | tf_op jit(solution)/shard_map/all_to_all | solution.py:77
  129.1 4.8 copy-start.3
  129.1 46.1 %all-to-all-start.3 = ((bf16[512,8,128]{0,2,1:T(8,128)(2,1)}), bf16[512,8,128]{0,2,1:T(8,128)(2,1)}, u32[]{:S(2)}, u32[]{:S(2)}) async-start(bf16[512,8,128]{0,2,1:T(8,128)(2,1)} %bitcast.123), calls=%async_computation.3 | async-start | bytes 2097152 | tf_op jit(solution)/shard_map/all_to_all | solution.py:75
  135.4 3.9 collective-permute-start
  137.8 5.4 collective-permute-start.1
  175.2 203.9 %all-to-all-start.2 = ((bf16[32,3,32768]{2,1,0:T(4,128)(2,1)}), bf16[32,3,32768]{2,1,0:T(4,128)(2,1)}, u32[]{:S(2)}, u32[]{:S(2)}) async-start(bf16[32,3,32768]{2,1,0:T(4,128)(2,1)} %copy.39), calls=%async_computation.2 | async-start | bytes 16777216 | tf_op jit(solution)/shard_map/all_to_all | solution.py:53
  188.0 222.0 %all-reduce.2.cloned.1.call-start = ((), (), s32[]{:S(2)}) async-start(), calls=%async_computation.5 | async-start | bytes 262144 | tf_op jit(solution)/shard_map/psum | solution.py:31
  195.4 8.2 %copy-start.4 = (bf16[512,8,128]{2,0,1:T(8,128)(2,1)S(1)}, bf16[512,8,128]{2,0,1:T(8,128)(2,1)}, u32[]{:S(2)}) copy-start(bf16[512,8,128]{2,0,1:T(8,128)(2,1)} %copy-done.3) | copy-start | bytes 3145732
  413.7 7.6 %copy-start.5 = (bf16[256,256]{0,1:T(8,128)(2,1)S(1)}, bf16[256,256]{0,1:T(8,128)(2,1)}, u32[]{:S(2)}) copy-start(bf16[256,256]{0,1:T(8,128)(2,1)} %get-tuple-element.175) | copy-start | bytes 393220 | tf_op jit(solution)/shard_map/while
  427.2 2.0 copy-start.2
  436.1 7.6 %copy-start.5 = (bf16[256,256]{0,1:T(8,128)(2,1)S(1)}, bf16[256,256]{0,1:T(8,128)(2,1)}, u32[]{:S(2)}) copy-start(bf16[256,256]{0,1:T(8,128)(2,1)} %get-tuple-element.175) | copy-start | bytes 393220 | tf_op jit(solution)/shard_map/while
  449.6 2.0 copy-start.2
  458.6 7.6 %copy-start.5 = (bf16[256,256]{0,1:T(8,128)(2,1)S(1)}, bf16[256,256]{0,1:T(8,128)(2,1)}, u32[]{:S(2)}) copy-start(bf16[256,256]{0,1:T(8,128)(2,1)} %get-tuple-element.175) | copy-start | bytes 393220 | tf_op jit(solution)/shard_map/while
  472.1 2.0 copy-start.2
  481.0 7.6 %copy-start.5 = (bf16[256,256]{0,1:T(8,128)(2,1)S(1)}, bf16[256,256]{0,1:T(8,128)(2,1)}, u32[]{:S(2)}) copy-start(bf16[256,256]{0,1:T(8,128)(2,1)} %get-tuple-element.175) | copy-start | bytes 393220 | tf_op jit(solution)/shard_map/while
  494.5 2.0 copy-start.2
  503.4 7.6 %copy-start.5 = (bf16[256,256]{0,1:T(8,128)(2,1)S(1)}, bf16[256,256]{0,1:T(8,128)(2,1)}, u32[]{:S(2)}) copy-start(bf16[256,256]{0,1:T(8,128)(2,1)} %get-tuple-element.175) | copy-start | bytes 393220 | tf_op jit(solution)/shard_map/while
  516.9 2.0 copy-start.2
  525.9 7.6 %copy-start.5 = (bf16[256,256]{0,1:T(8,128)(2,1)S(1)}, bf16[256,256]{0,1:T(8,128)(2,1)}, u32[]{:S(2)}) copy-start(bf16[256,256]{0,1:T(8,128)(2,1)} %get-tuple-element.175) | copy-start | bytes 393220 | tf_op jit(solution)/shard_map/while
  539.4 2.0 copy-start.2
  548.3 7.6 %copy-start.5 = (bf16[256,256]{0,1:T(8,128)(2,1)S(1)}, bf16[256,256]{0,1:T(8,128)(2,1)}, u32[]{:S(2)}) copy-start(bf16[256,256]{0,1:T(8,128)(2,1)} %get-tuple-element.175) | copy-start | bytes 393220 | tf_op jit(solution)/shard_map/while
  561.8 2.0 copy-start.2
  570.7 7.6 %copy-start.5 = (bf16[256,256]{0,1:T(8,128)(2,1)S(1)}, bf16[256,256]{0,1:T(8,128)(2,1)}, u32[]{:S(2)}) copy-start(bf16[256,256]{0,1:T(8,128)(2,1)} %get-tuple-element.175) | copy-start | bytes 393220 | tf_op jit(solution)/shard_map/while
  584.2 2.0 copy-start.2
  589.5 25.7 %copy-start.1 = (bf16[1024,1024]{1,0:T(8,128)(2,1)S(1)}, bf16[1024,1024]{1,0:T(8,128)(2,1)}, u32[]{:S(2)}) copy-start(bf16[1024,1024]{1,0:T(8,128)(2,1)} %param.11) | copy-start | bytes 6291460
Sparse Core Ops, SparseCore 0:
  193.4 202.0 all-reduce.1
where the time goes:
time: 625 us; the launch traced here: 622 us
  local copies, waits for them, and re-layouts  198 us (32%)
  waiting for transfers between devices  183 us (29%)
  other arithmetic  124 us (20%)
  matrix products  49.5 us (8%)
  starting transfers between devices  32.9 us (5%)
  blocking collectives  20.2 us (3%)
  between operations  13.7 us (2%)
    all_to_all x1, waiting for transfers between devices, fetch_requested(): lax.all_to_all(outgoing, 'ctx', split_axis=0, concat_axis=0, tiled=True)  169 us
    dynamic_slice x40, local copies, waits for them, and re-layouts, body(): lax.map(attend, (query_groups, window_groups, random_groups, window_flags...  97.8 us
    another operation x1, other arithmetic, fetch_requested(): jnp.zeros((ctx_count * tiles_total,), jnp.int32).at[flat_index]  85.2 us
    all_to_all x1, blocking collectives, body(): lax.all_to_all(attended, 'head', split_axis=0, concat_axis=1, tiled=True)  20.2 us
    dot_general x8, matrix products, attend(): jnp.einsum('thqk,tkhd->tqhd', weights.astype(jnp.bfloat16), value_block,...  19.4 us
    reduce_sum x8, other arithmetic, attend(): totals = jnp.sum(weights, axis=-1, keepdims=True)  16.1 us
    gather x1, local copies, waits for them, and re-layouts, fetch_requested(): return incoming.reshape(ctx_count * CAP, TILE, lane_count)[slot_index]  15.5 us
    reshape x1, local copies, waits for them, and re-layouts, fetch_requested(): return incoming.reshape(ctx_count * CAP, TILE, lane_count)[slot_index]  15.3 us
  transfers between devices with their start and end apart: 7, of which 3 were waited for; matrix products, arithmetic and copies ran while one was open for 29% of the time, Pallas kernels for 0%

commit v1 on v0

v1 whole, which is shorter than its diff:
```python
import jax
import jax.numpy as jnp
from jax import lax
from jax.experimental import pallas as pl
from jax.experimental.pallas import tpu as pltpu
from jax.sharding import PartitionSpec as P

HEADS = 16
HEAD_DIM = 64
TILE = 128
GLOBALS = 2
RANDOM = 12
CAP = 3
LOG2E = 1.4426950408889634
SCALE = HEAD_DIM ** (-0.5) * LOG2E
NEG = -1e30


def project_kv_kernel(x_ref, wk_ref, wv_ref, o_ref):
    w = jnp.concatenate([wk_ref[...], wv_ref[...]], axis=1)
    o_ref[0] = jnp.dot(x_ref[...], w, preferred_element_type=jnp.float32).astype(jnp.bfloat16)


def project_kv(x, w_key, w_value, groups):
    rows, width = x.shape
    lanes = w_key.shape[1] // groups
    w_spec = pl.BlockSpec((width, lanes), lambda h: (0, h))
    return pl.pallas_call(
        project_kv_kernel,
        grid=(groups,),
        in_specs=[pl.BlockSpec((rows, width), lambda h: (0, 0)), w_spec, w_spec],
        out_specs=pl.BlockSpec((1, rows, 2 * lanes), lambda h: (h, 0, 0)),
        out_shape=jax.ShapeDtypeStruct((groups, rows, 2 * lanes), jnp.bfloat16),
        cost_estimate=pl.CostEstimate(
            flops=4 * rows * width * w_key.shape[1],
            transcendentals=0,
            bytes_accessed=4 * width * w_key.shape[1] + 6 * rows * width,
        ),
        name="project_kv",
    )(x, w_key, w_value)


def project_q_kernel(x_ref, wa_ref, wb_ref, o_ref):
    lanes = wa_ref.shape[1]
    w = jnp.concatenate([wa_ref[...], wb_ref[...]], axis=1)
    r = jnp.dot(x_ref[...], w, preferred_element_type=jnp.float32).astype(jnp.bfloat16)
    o_ref[0] = r[:, :lanes]
    o_ref[1] = r[:, lanes:]


def project_q(x, w_query, groups):
    rows, width = x.shape
    lanes = w_query.shape[1] // groups
    return pl.pallas_call(
        project_q_kernel,
        grid=(groups // 2,),
        in_specs=[
            pl.BlockSpec((rows, width), lambda h: (0, 0)),
            pl.BlockSpec((width, lanes), lambda h: (0, 2 * h)),
            pl.BlockSpec((width, lanes), lambda h: (0, 2 * h + 1)),
        ],
        out_specs=pl.BlockSpec((2, rows, lanes), lambda h: (h, 0, 0)),
        out_shape=jax.ShapeDtypeStruct((groups, rows, lanes), jnp.bfloat16),
        cost_estimate=pl.CostEstimate(
            flops=2 * rows * width * w_query.shape[1],
            transcendentals=0,
            bytes_accessed=2 * width * w_query.shape[1] + 4 * rows * width,
        ),
        name="project_q",
    )(x, w_query, w_query)


def pick_kernel(index_ref, x_ref, *o_refs):
    count = x_ref.shape[0]

    def step(d, carry):
        for s, o_ref in enumerate(o_refs):
            o_ref[d] = x_ref[index_ref[s * count + d]]
        return carry

    lax.fori_loop(0, count, step, 0)


def pick_tiles(index, x, dests):
    whole = pl.BlockSpec(x.shape, lambda i, idx: (0, 0, 0))
    out = (dests,) + x.shape[1:]
    return pl.pallas_call(
        pick_kernel,
        grid_spec=pltpu.PrefetchScalarGridSpec(
            num_scalar_prefetch=1,
            grid=(1,),
            in_specs=[whole],
            out_specs=[pl.BlockSpec(out, lambda i, idx: (0, 0, 0))] * CAP,
        ),
        out_shape=[jax.ShapeDtypeStruct(out, x.dtype)] * CAP,
        cost_estimate=pl.CostEstimate(flops=0, transcendentals=0, bytes_accessed=4 * x.size * 2),
        name="pick_tiles",
    )(index, x)


def split_heads(q):
    first = lax.broadcasted_iota(jnp.int32, q.shape, 1) < HEAD_DIM
    zero = jnp.zeros_like(q)
    return jnp.concatenate([jnp.where(first, q, zero), jnp.where(first, zero, q)], axis=0)


def join_heads(both):
    half = both.shape[0] // 2
    shape = (half, 2 * HEAD_DIM)
    first = lax.broadcasted_iota(jnp.int32, shape, 1) < HEAD_DIM
    return jnp.where(
        first, jnp.broadcast_to(both[:half], shape), jnp.broadcast_to(both[half:], shape)
    )


def score(q2, keys):
    return lax.dot_general(q2, keys, (((1,), (1,)), ((), ())), preferred_element_type=jnp.float32)


def local_kernel(shard_ref, q_ref, kv_ref, before_ref, after_ref, global_ref, m_ref, l_ref, a_ref, pad_ref):
    tiles_here = kv_ref.shape[0] // TILE
    lanes = q_ref.shape[1]
    step = pl.program_id(0)
    per_step = q_ref.shape[0] // TILE

    @pl.when(step == 0)
    def _():
        pad_ref[0:TILE] = before_ref[...]
        pad_ref[TILE : TILE + kv_ref.shape[0]] = kv_ref[...]
        pad_ref[TILE + kv_ref.shape[0] :] = after_ref[...]

    tiles_total = shard_ref[1]
    for i in range(per_step):
        t = step * per_step + i
        rows = pl.ds(i * TILE, TILE)
        q2 = split_heads(q_ref[rows, :])
        window = pad_ref[pl.ds(pl.multiple_of(t * TILE, TILE), 3 * TILE), :]
        first_id = shard_ref[0] * tiles_here + t - 1
        position = lax.broadcasted_iota(jnp.int32, (2 * TILE, 3 * TILE), 1)
        ok = (position >= (GLOBALS - first_id) * TILE) & (
            position < (tiles_total - first_id) * TILE
        )
        s_window = jnp.where(ok, score(q2, window[:, :lanes]), NEG)
        s_global = score(q2, global_ref[:, :lanes])
        top = jnp.maximum(
            jnp.max(s_window, axis=1, keepdims=True), jnp.max(s_global, axis=1, keepdims=True)
        )
        p_window = jnp.exp2((s_window - top) * SCALE)
        p_global = jnp.exp2((s_global - top) * SCALE)
        total = jnp.sum(p_window, axis=1, keepdims=True) + jnp.sum(p_global, axis=1, keepdims=True)
        acc = jnp.dot(
            p_window.astype(jnp.bfloat16), window[:, lanes:], preferred_element_type=jnp.float32
        ) + jnp.dot(
            p_global.astype(jnp.bfloat16), global_ref[:, lanes:], preferred_element_type=jnp.float32
        )
        m_ref[rows, :] = join_heads(top)
        l_ref[rows, :] = join_heads(total)
        a_ref[rows, :] = join_heads(acc)


def local_attention(shard, q, kv, before, after, global_kv, per_step=2):
    rows, lanes = q.shape
    block = pl.BlockSpec((per_step * TILE, lanes), lambda i, s: (i, 0))
    fixed = lambda a: pl.BlockSpec(a.shape, lambda i, s: (0, 0))
    out = jax.ShapeDtypeStruct((rows, lanes), jnp.float32)
    keys = (3 + GLOBALS) * TILE
    return pl.pallas_call(
        local_kernel,
        grid_spec=pltpu.PrefetchScalarGridSpec(
            num_scalar_prefetch=1,
            grid=(rows // (per_step * TILE),),
            in_specs=[block, fixed(kv), fixed(before), fixed(after), fixed(global_kv)],
            out_specs=[block] * 3,
            scratch_shapes=[pltpu.VMEM((rows + 2 * TILE, 2 * lanes), jnp.bfloat16)],
        ),
        out_shape=[out] * 3,
        cost_estimate=pl.CostEstimate(
            flops=8 * rows * keys * lanes,
            transcendentals=2 * rows * keys,
            bytes_accessed=rows * lanes * 20,
        ),
        name="local_attention",
    )(shard, q, kv, before, after, global_kv)


def random_kernel(index_ref, count_ref, q_ref, kv0_ref, kv1_ref, kv2_ref, m_ref, l_ref, a_ref, o_ref, kv_ref):
    lanes = q_ref.shape[1]
    step = pl.program_id(0)
    per_step = q_ref.shape[0] // TILE
    parts = kv0_ref.shape[0]
    shards = kv0_ref.shape[1]
    part_rows = kv0_ref.shape[2]

    @pl.when(step == 0)
    def _():
        for s, ref in enumerate((kv0_ref, kv1_ref, kv2_ref)):
            for j in range(parts):
                kv_ref[s * shards : (s + 1) * shards, j * part_rows : (j + 1) * part_rows, :] = ref[j]

    for i in range(per_step):
        t = step * per_step + i
        rows = pl.ds(i * TILE, TILE)
        q2 = split_heads(q_ref[rows, :])
        count = count_ref[t]
        at = [index_ref[t * RANDOM + j] for j in range(RANDOM)]
        scores = []
        top = None
        for j in range(RANDOM):
            bias = jnp.where(j < count, 0.0, NEG).astype(jnp.float32)
            s = score(q2, kv_ref[at[j], :, :lanes]) + bias
            scores.append(s)
            top = s if top is None else jnp.maximum(top, s)
        m_old = m_ref[rows, :]
        m_old = jnp.concatenate([m_old[:, :1], m_old[:, HEAD_DIM : HEAD_DIM + 1]], axis=0)
        m_new = jnp.maximum(jnp.max(top, axis=1, keepdims=True), m_old)
        alpha = jnp.exp2((m_old - m_new) * SCALE)
        total = None
        acc = None
        for j in range(0, RANDOM, 2):
            p0 = jnp.exp2((scores[j] - m_new) * SCALE)
            p1 = jnp.exp2((scores[j + 1] - m_new) * SCALE)
            total = p0 + p1 if total is None else total + (p0 + p1)
            p = jnp.concatenate([p0.astype(jnp.bfloat16), p1.astype(jnp.bfloat16)], axis=1)
            v = jnp.concatenate([kv_ref[at[j], :, lanes:], kv_ref[at[j + 1], :, lanes:]], axis=0)
            part = jnp.dot(p, v, preferred_element_type=jnp.float32)
            acc = part if acc is None else acc + part
        alpha = join_heads(alpha)
        denominator = l_ref[rows, :] * alpha + join_heads(jnp.sum(total, axis=1, keepdims=True))
        numerator = a_ref[rows, :] * alpha + join_heads(acc)
        o_ref[rows, :] = (numerator / denominator).astype(jnp.bfloat16)


def random_attention(index, count, q, kvs, m, l, a, per_step=2):
    rows, lanes = q.shape
    parts, shards, part_rows, both = kvs[0].shape
    block = pl.BlockSpec((per_step * TILE, lanes), lambda i, s, c: (i, 0))
    fixed = pl.BlockSpec(kvs[0].shape, lambda i, s, c: (0, 0, 0, 0))
    keys = RANDOM * TILE
    return pl.pallas_call(
        random_kernel,
        grid_spec=pltpu.PrefetchScalarGridSpec(
            num_scalar_prefetch=2,
            grid=(rows // (per_step * TILE),),
            in_specs=[block] + [fixed] * CAP + [block] * 3,
            out_specs=block,
            scratch_shapes=[pltpu.VMEM((CAP * shards, parts * part_rows, both), jnp.bfloat16)],
        ),
        out_shape=jax.ShapeDtypeStruct((rows, lanes), jnp.bfloat16),
        cost_estimate=pl.CostEstimate(
            flops=8 * rows * keys * lanes,
            transcendentals=2 * rows * keys,
            bytes_accessed=rows * lanes * 16 + CAP * kvs[0].size * 2,
        ),
        name="random_attention",
    )(index, count, q, *kvs, m, l, a)


def request_tables(random_tiles, random_count, shard, ctx_count, tiles_here):
    slots = random_tiles.shape[1]
    live = jnp.arange(slots, dtype=jnp.int32)[None, :] < random_count[:, None]
    entries = jnp.where(live, random_tiles, -1).reshape(ctx_count, tiles_here * slots)
    mine = shard * tiles_here + jnp.arange(tiles_here, dtype=jnp.int32)
    owned = jnp.any(entries[:, :, None] == mine[None, None, :], axis=1)
    k = jnp.arange(tiles_here, dtype=jnp.int32)
    rank = jnp.sum((owned[:, None, :] & (k[None, None, :] < k[None, :, None])).astype(jnp.int32), axis=2)
    hit = owned[:, None, :] & (rank[:, None, :] == jnp.arange(CAP, dtype=jnp.int32)[None, :, None])
    send = jnp.sum(jnp.where(hit, k[None, None, :], 0), axis=2)
    wanted = lax.dynamic_index_in_dim(entries, shard, 0, keepdims=False)
    tiles = jnp.arange(ctx_count * tiles_here, dtype=jnp.int32)
    needed = jnp.any(wanted[:, None] == tiles[None, :], axis=0)
    owner = wanted // tiles_here
    lower = (
        needed[None, :]
        & (tiles[None, :] < wanted[:, None])
        & (tiles[None, :] >= (owner * tiles_here)[:, None])
    )
    slot = jnp.sum(lower.astype(jnp.int32), axis=1)
    read = jnp.where(wanted >= 0, slot * ctx_count + owner, 0)
    return send.T.reshape(-1), read


def body(tokens, w_query, w_key, w_value, w_out, random_tiles, random_count):
    groups = lax.axis_size("head")
    ctx_count = lax.axis_size("ctx")
    rows, width = tokens.shape
    own_tiles = rows // TILE
    part = TILE // groups
    tiles_here = own_tiles * groups
    shard = lax.axis_index("ctx").astype(jnp.int32)

    striped = tokens.reshape(own_tiles, groups, part, width).transpose(1, 0, 2, 3)
    striped = lax.all_to_all(striped, "head", split_axis=0, concat_axis=0, tiled=True)
    striped = striped.reshape(tiles_here, part, width)
    send, read = request_tables(random_tiles, random_count, shard, ctx_count, tiles_here)
    outgoing = pick_tiles(send, striped, ctx_count)

    kv = project_kv(tokens, w_key, w_value, groups)
    kv = lax.all_to_all(kv, "head", split_axis=0, concat_axis=0, tiled=True)
    kv = kv.reshape(rows * groups, -1)
    q = project_q(tokens, w_query, groups)
    q = lax.all_to_all(q, "head", split_axis=0, concat_axis=0, tiled=True)
    q = q.reshape(rows * groups, -1)

    fetched = []
    for slot in range(CAP):
        got = lax.all_to_all(outgoing[slot], "ctx", split_axis=0, concat_axis=0, tiled=True)
        got = project_kv(got.reshape(ctx_count * part, width), w_key, w_value, groups)
        got = lax.all_to_all(got, "head", split_axis=0, concat_axis=0, tiled=True)
        fetched.append(got.reshape(groups, ctx_count, part, -1))

    up = [(i, (i + 1) % ctx_count) for i in range(ctx_count - 1)]
    down = [(j, i) for i, j in up]
    before = lax.ppermute(kv[-TILE:], "ctx", up)
    after = lax.ppermute(kv[:TILE], "ctx", down)
    root = kv[: GLOBALS * TILE]
    global_kv = lax.psum(jnp.where(shard == 0, root, 0).astype(root.dtype), "ctx")

    place = jnp.stack([shard, jnp.int32(tiles_here * ctx_count)])
    m, l, a = local_attention(place, q, kv, before, after, global_kv)
    my_count = lax.dynamic_slice_in_dim(random_count, shard * tiles_here, tiles_here, 0)
    attended = random_attention(read, my_count, q, fetched, m, l, a)
    attended = attended.reshape(groups, rows, -1)
    returned = lax.all_to_all(attended, "head", split_axis=0, concat_axis=0, tiled=True)
    out = lax.dot_general(
        returned,
        w_out.reshape(groups, -1, width),
        (((0, 2), (0, 1)), ((), ())),
        preferred_element_type=jnp.float32,
    )
    return out.astype(jnp.bfloat16)


def solution(mesh):
    return jax.shard_map(
        body,
        mesh=mesh,
        in_specs=(P(("ctx", "head"), None), P(), P(), P(), P(), P(), P()),
        out_specs=P(("ctx", "head"), None),
        check_vma=False,
    )
```

time: 625 us -> 484 us (0.77)
  local copies, waits for them, and re-layouts: 198 us -> 4.72 us
  other arithmetic: 124 us -> 5.36 us
  Pallas kernels: 0 us -> 93.4 us
  blocking collectives: 20.2 us -> 91.4 us
  matrix products: 49.5 us -> 2.25 us
  waiting for transfers between devices: 183 us -> 223 us
  starting transfers between devices: 32.9 us -> 47.8 us
    psum x1, waiting for transfers between devices: 0.01 us -> 126 us  [body(): lax.psum(jnp.where(shard == 0, root, 0).astype(root.dtype), 'ctx')]
    dynamic_slice x44 -> x2, local copies, waits for them, and re-layouts: 99 us -> 0.63 us  [the longest x1 0.61 us: body(): lax.dynamic_slice_in_dim(random_count, shard * tiles_here, tiles_here, 0)]
    pallas_call x0 -> x8, Pallas kernels: none -> 93.4 us  [the longest x1 34.4 us: random_attention(): pl.pallas_call(random_kernel, grid_spec=pltpu.PrefetchScalarGridSpec(num_...]
    another operation x4 -> x1, other arithmetic: 88.7 us -> 0.65 us  [body(): place = jnp.stack([shard, jnp.int32(tiles_here * ctx_count)])]
    all_to_all x4 -> x7, waiting for transfers between devices: 180 us -> 93.7 us  [the longest x3 36.5 us: body(): got = lax.all_to_all(got, 'head', split_axis=0, concat_axis=0, tiled=True)]
    all_to_all x1 -> x3, blocking collectives: 20.2 us -> 91.4 us  [the longest x2 67.2 us: body(): lax.all_to_all(outgoing[slot], 'ctx', split_axis=0, concat_axis=0, tiled=...]
    dot_general x21 -> x1, matrix products: 49.5 us -> 2.25 us  [body(): lax.dot_general(returned, w_out.reshape(groups, -1, width), (((0, 2), (0,...]
    slice x10 -> x1, local copies, waits for them, and re-layouts: 21.8 us -> 0.88 us  [body(): after = lax.ppermute(kv[:TILE], 'ctx', down)]
  transfers between devices with their start and end apart: 7 -> 10, of which waited for: 3 -> 8; matrix products, arithmetic and copies ran while one was open for 29% -> 2% of each run, Pallas kernels for 0% -> 11%
where the time goes in v1:
time: 484 us; the launch traced here: 481 us
  waiting for transfers between devices  223 us (46%)
  Pallas kernels  93.4 us (19%)
  blocking collectives  91.4 us (19%)
  starting transfers between devices  47.8 us (10%)
  between operations  13.5 us (3%)
  other arithmetic  5.36 us (1%)
    psum x1, waiting for transfers between devices, body(): lax.psum(jnp.where(shard == 0, root, 0).astype(root.dtype), 'ctx')  126 us
    all_to_all x2, blocking collectives, body(): lax.all_to_all(outgoing[slot], 'ctx', split_axis=0, concat_axis=0, tiled=...  67.2 us
    all_to_all x3, waiting for transfers between devices, body(): got = lax.all_to_all(got, 'head', split_axis=0, concat_axis=0, tiled=True)  36.5 us
    pallas_call x1, Pallas kernels, random_attention(): pl.pallas_call(random_kernel, grid_spec=pltpu.PrefetchScalarGridSpec(num_...  34.4 us
    pallas_call x4, Pallas kernels, project_kv(): pl.pallas_call(project_kv_kernel, grid=(groups,), in_specs=[pl.BlockSpec(...  32.3 us
    all_to_all x1, blocking collectives, body(): lax.all_to_all(attended, 'head', split_axis=0, concat_axis=0, tiled=True)  24.2 us
    all_to_all x1, waiting for transfers between devices, body(): kv = lax.all_to_all(kv, 'head', split_axis=0, concat_axis=0, tiled=True)  19.7 us
    all_to_all x3, starting transfers between devices, body(): got = lax.all_to_all(got, 'head', split_axis=0, concat_axis=0, tiled=True)  19.1 us
  transfers between devices with their start and end apart: 10, of which 8 were waited for; matrix products, arithmetic and copies ran while one was open for 2% of the time, Pallas kernels for 11%

profile of v1, /device:TPU:1, one launch (start us, length us, event | category | flops | bytes accessed | tf_op | source)
XLA Modules:
  0.0 481.4 jit_solution(14279246616791010195)
XLA Ops:
  6.5 4.9 %project_q.1 = bf16[8,512,128]{2,1,0:T(8,128)(2,1)} custom-call(bf16[512,1024]{1,0:T(8,128)(2,1)} %x_ref.3, bf16[1024,1024]{1,0:T(8,128)(2,1)} %wb_ref.1, bf16[1024,1024]{1,0:T(8,128)(2,1)} %wb_ref.1), custom_call_target="tpu_custom_call" | custom-call | flops 1073741824 | bytes 4194304 | tf_op jit(solution)/shard_map/project_q/pallas_call | solution.py:54
  11.5 7.4 %all-to-all-start = ((bf16[8,512,128]{2,1,0:T(8,128)(2,1)}), bf16[8,512,128]{2,1,0:T(8,128)(2,1)}, u32[]{:S(2)}, u32[]{:S(2)}) async-start(bf16[8,512,128]{2,1,0:T(8,128)(2,1)} %project_q.1), calls=%async_computation | async-start | bytes 2097152 | tf_op jit(solution)/shard_map/all_to_all | solution.py:301
  18.9 1.1 copy.14
  20.0 14.0 %all-to-all-done = bf16[8,512,128]{2,1,0:T(8,128)(2,1)} async-done(((bf16[8,512,128]{2,1,0:T(8,128)(2,1)}), bf16[8,512,128]{2,1,0:T(8,128)(2,1)}, u32[]{:S(2)}, u32[]{:S(2)}) %all-to-all-start) | async-done | bytes 1048608 | tf_op jit(solution)/shard_map/all_to_all | solution.py:301
  34.0 4.4 all-to-all-start.1
  38.4 8.0 %project_kv.7 = bf16[8,512,256]{2,1,0:T(8,128)(2,1)} custom-call(bf16[512,1024]{1,0:T(8,128)(2,1)} %x_ref.3, bf16[1024,1024]{1,0:T(8,128)(2,1)} %wk_ref.7, bf16[1024,1024]{1,0:T(8,128)(2,1)} %wv_ref.7), custom_call_target="tpu_custom_call" | custom-call | flops 2147483648 | bytes 7340032 | tf_op jit(solution)/shard_map/project_kv/pallas_call | solution.py:28
  46.5 7.0 %all-to-all-done.1 = bf16[8,4,16,1024]{3,2,1,0:T(8,128)(2,1)S(1)} async-done(((bf16[8,4,16,1024]{3,2,1,0:T(8,128)(2,1)}), bf16[8,4,16,1024]{3,2,1,0:T(8,128)(2,1)S(1)}, u32[]{:S(2)}, u32[]{:S(2)}) %all-to-all-start.1) | async-done | bytes 1048608 | tf_op jit(solution)/shard_map/all_to_all | solution.py:292
  53.4 5.2 %all-to-all-start.8 = ((bf16[8,512,256]{2,1,0:T(8,128)(2,1)}), bf16[8,512,256]{2,1,0:T(8,128)(2,1)}, u32[]{:S(2)}, u32[]{:S(2)}) async-start(bf16[8,512,256]{2,1,0:T(8,128)(2,1)} %project_kv.7), calls=%async_computation.8 | async-start | bytes 4194304 | tf_op jit(solution)/shard_map/all_to_all | solution.py:298
  61.4 3.9 pick_tiles.1
  65.3 19.7 %all-to-all-done.8 = bf16[8,512,256]{2,1,0:T(8,128)(2,1)} async-done(((bf16[8,512,256]{2,1,0:T(8,128)(2,1)}), bf16[8,512,256]{2,1,0:T(8,128)(2,1)}, u32[]{:S(2)}, u32[]{:S(2)}) %all-to-all-start.8) | async-done | bytes 2097184 | tf_op jit(solution)/shard_map/all_to_all | solution.py:298
  85.0 35.8 %all_to_all.50 = bf16[32,16,1024]{2,1,0:T(8,128)(2,1)} all-to-all(bf16[32,16,1024]{2,1,0:T(8,128)(2,1)} %get-tuple-element.13), channel_id=1, replica_groups=mesh['ctx'=32,'head'=8] {'ctx'}, dimensions={0} | all-to-all | bytes 2097152 | tf_op jit(solution)/shard_map/all_to_all | solution.py:306
  120.8 31.4 %all_to_all.51 = bf16[32,16,1024]{2,1,0:T(8,128)(2,1)} all-to-all(bf16[32,16,1024]{2,1,0:T(8,128)(2,1)S(1)} %copy-done.4), channel_id=1, replica_groups=mesh['ctx'=32,'head'=8] {'ctx'}, dimensions={0} | all-to-all | bytes 2097152 | tf_op jit(solution)/shard_map/all_to_all | solution.py:306
  152.1 6.9 %all-to-all-start.4 = ((bf16[32,16,1024]{2,1,0:T(8,128)(2,1)}), bf16[32,16,1024]{2,1,0:T(8,128)(2,1)S(1)}, u32[]{:S(2)}, u32[]{:S(2)}) async-start(bf16[32,16,1024]{2,1,0:T(8,128)(2,1)} %get-tuple-element.12), calls=%async_computation.4 | async-start | bytes 2097152 | tf_op jit(solution)/shard_map/all_to_all | solution.py:306
  159.0 8.0 %project_kv.6 = bf16[8,512,256]{2,1,0:T(8,128)(2,1)} custom-call(bf16[512,1024]{1,0:T(8,128)(2,1)} %bitcast.27, bf16[1024,1024]{1,0:T(8,128)(2,1)} %wk_ref.7, bf16[1024,1024]{1,0:T(8,128)(2,1)} %wv_ref.7), custom_call_target="tpu_custom_call" | custom-call | flops 2147483648 | bytes 7340032 | tf_op jit(solution)/shard_map/project_kv/pallas_call | solution.py:28
  167.1 16.5 %all-to-all-done.4 = bf16[32,16,1024]{2,1,0:T(8,128)(2,1)S(1)} async-done(((bf16[32,16,1024]{2,1,0:T(8,128)(2,1)}), bf16[32,16,1024]{2,1,0:T(8,128)(2,1)S(1)}, u32[]{:S(2)}, u32[]{:S(2)}) %all-to-all-start.4) | async-done | bytes 1048608 | tf_op jit(solution)/shard_map/all_to_all | solution.py:306
  183.6 1.0 copy-done.3
  184.5 8.7 %all-to-all-start.7 = ((bf16[8,512,256]{2,1,0:T(8,128)(2,1)}), bf16[8,512,256]{2,1,0:T(8,128)(2,1)}, u32[]{:S(2)}, u32[]{:S(2)}) async-start(bf16[8,512,256]{2,1,0:T(8,128)(2,1)} %project_kv.6), calls=%async_computation.7 | async-start | bytes 4194304 | tf_op jit(solution)/shard_map/all_to_all | solution.py:308
  193.2 8.1 %project_kv.4 = bf16[8,512,256]{2,1,0:T(8,128)(2,1)} custom-call(bf16[512,1024]{1,0:T(8,128)(2,1)} %bitcast.26, bf16[1024,1024]{1,0:T(8,128)(2,1)} %wk_ref.7, bf16[1024,1024]{1,0:T(8,128)(2,1)} %wv_ref.7), custom_call_target="tpu_custom_call" | custom-call | flops 2147483648 | bytes 7340032 | tf_op jit(solution)/shard_map/project_kv/pallas_call | solution.py:28
  201.3 18.3 %all-to-all-done.7 = bf16[8,512,256]{2,1,0:T(8,128)(2,1)} async-done(((bf16[8,512,256]{2,1,0:T(8,128)(2,1)}), bf16[8,512,256]{2,1,0:T(8,128)(2,1)}, u32[]{:S(2)}, u32[]{:S(2)}) %all-to-all-start.7) | async-done | bytes 2097184 | tf_op jit(solution)/shard_map/all_to_all | solution.py:308
  219.6 5.2 %all-to-all-start.3 = ((bf16[8,512,256]{2,1,0:T(8,128)(2,1)}), bf16[8,512,256]{2,1,0:T(8,128)(2,1)}, u32[]{:S(2)}, u32[]{:S(2)}) async-start(bf16[8,512,256]{2,1,0:T(8,128)(2,1)} %project_kv.4), calls=%async_computation.3 | async-start | bytes 4194304 | tf_op jit(solution)/shard_map/all_to_all | solution.py:308
  224.8 8.1 %project_kv.5 = bf16[8,512,256]{2,1,0:T(8,128)(2,1)} custom-call(bf16[512,1024]{1,0:T(8,128)(2,1)} %bitcast.25, bf16[1024,1024]{1,0:T(8,128)(2,1)} %wk_ref.7, bf16[1024,1024]{1,0:T(8,128)(2,1)} %wv_ref.7), custom_call_target="tpu_custom_call" | custom-call | flops 2147483648 | bytes 7340032 | tf_op jit(solution)/shard_map/project_kv/pallas_call | solution.py:28
  232.9 18.2 %all-to-all-done.3 = bf16[8,512,256]{2,1,0:T(8,128)(2,1)} async-done(((bf16[8,512,256]{2,1,0:T(8,128)(2,1)}), bf16[8,512,256]{2,1,0:T(8,128)(2,1)}, u32[]{:S(2)}, u32[]{:S(2)}) %all-to-all-start.3) | async-done | bytes 2097184 | tf_op jit(solution)/shard_map/all_to_all | solution.py:308
  251.1 5.2 %all-to-all-start.5 = ((bf16[8,512,256]{2,1,0:T(8,128)(2,1)}), bf16[8,512,256]{2,1,0:T(8,128)(2,1)}, u32[]{:S(2)}, u32[]{:S(2)}) async-start(bf16[8,512,256]{2,1,0:T(8,128)(2,1)} %project_kv.5), calls=%async_computation.5 | async-start | bytes 4194304 | tf_op jit(solution)/shard_map/all_to_all | solution.py:308
  258.5 1.6 slice_select_fusion
  261.0 3.4 collective-permute-start
  264.5 1.3 collective-permute-start.1
  266.4 3.5 collective-permute-done.1.after_ref
  269.9 125.9 %all-reduce.2.cloned.1.call-done.global_ref = bf16[256,256]{1,0:T(8,128)(2,1)} async-done(((bf16[256,256]{1,0:T(8,128)(2,1)}), bf16[256,256]{1,0:T(8,128)(2,1)}) %all-reduce.2.cloned.1.call-update) | async-done | bytes 131088 | tf_op jit(solution)/shard_map/psum | solution.py:316
  395.8 17.9 %local_attention.1 = (f32[4096,128]{1,0:T(8,128)}, f32[4096,128]{1,0:T(8,128)}, f32[4096,128]{1,0:T(8,128)}) custom-call(s32[2]{0:T(128)} %pad_add_fusion.shard_ref, bf16[4096,128]{1,0:T(8,128)(2,1)} %bitcast.q_ref, bf16[4096,256]{1,0:T(8,128)(2,1)} %bitcast.12.kv_ref, bf16[128,256]{1,0:T(8,128)(2,1)} %copy-done.7, bf16[128,256]{1,0:T(8,128)(2,1)} %copy-done.8, ...), custom_call_target="tpu_custom_call" | custom-call | flops 2684354560 | bytes 10485760 | tf_op jit(solution)/shard_map/local_attention/pallas_call | solution.py:167
  413.7 34.4 %random_attention.1 = bf16[4096,128]{1,0:T(8,128)(2,1)} custom-call(s32[384]{0:T(512)} %add_select_fusion.1.index_ref, s32[32]{0:T(128)} %dynamic_slice.8.count_ref, bf16[4096,128]{1,0:T(8,128)(2,1)} %bitcast.q_ref, bf16[8,32,16,256]{3,2,1,0:T(8,128)(2,1)} %bitcast.6.kv0_ref, bf16[8,32,16,256]{3,2,1,0:T(8,128)(2,1)} %bitcast.8.kv1_ref, ...), custom_call_target="tpu_custom_call" | custom-call | flops 6442450944 | bytes 14680064 | tf_op jit(solution)/shard_map/random_attention/pallas_call | solution.py:239
  448.1 24.2 %all_to_all.52 = bf16[8,512,128]{2,1,0:T(8,128)(2,1)S(1)} all-to-all(bf16[8,512,128]{2,1,0:T(8,128)(2,1)} %bitcast.28), channel_id=1, replica_groups=mesh['ctx'=32,'head'=8] {'head'}, dimensions={0} | all-to-all | bytes 2097152 | tf_op jit(solution)/shard_map/all_to_all | solution.py:323
  472.3 2.3 bitcast_convert_fusion
  (38 shorter events, 6.5 us)
Async XLA Ops:
  6.5 465.7 %copy-start = (bf16[1024,1024]{1,0:T(8,128)(2,1)S(1)}, bf16[1024,1024]{1,0:T(8,128)(2,1)}, u32[]{:S(2)}) copy-start(bf16[1024,1024]{1,0:T(8,128)(2,1)} %param.11) | copy-start | bytes 6291460
  11.5 7.4 %copy-start.2 = (bf16[512,1024]{1,0:T(8,128)(2,1)S(1)}, bf16[512,1024]{1,0:T(8,128)(2,1)}, u32[]{:S(2)}) copy-start(bf16[512,1024]{1,0:T(8,128)(2,1)} %x_ref.3) | copy-start | bytes 3145732
  11.5 22.5 %all-to-all-start = ((bf16[8,512,128]{2,1,0:T(8,128)(2,1)}), bf16[8,512,128]{2,1,0:T(8,128)(2,1)}, u32[]{:S(2)}, u32[]{:S(2)}) async-start(bf16[8,512,128]{2,1,0:T(8,128)(2,1)} %project_q.1), calls=%async_computation | async-start | bytes 2097152 | tf_op jit(solution)/shard_map/all_to_all | solution.py:301
  34.0 19.4 %all-to-all-start.1 = ((bf16[8,4,16,1024]{3,2,1,0:T(8,128)(2,1)}), bf16[8,4,16,1024]{3,2,1,0:T(8,128)(2,1)S(1)}, u32[]{:S(2)}, u32[]{:S(2)}) async-start(bf16[8,4,16,1024]{3,2,1,0:T(8,128)(2,1)} %bitcast.23), calls=%async_computation.1 | async-start | bytes 2097152 | tf_op jit(solution)/shard_map/all_to_all | solution.py:292
  46.4 12.2 %copy-start.5 = (s32[1024,12]{0,1:T(8,128)S(1)}, s32[1024,12]{0,1:T(8,128)}, u32[]{:S(2)}) copy-start(s32[1024,12]{0,1:T(8,128)} %param.12) | copy-start | bytes 147460
  46.5 12.2 %copy-start.6 = (s32[1024]{0:T(1024)S(1)}, s32[1024]{0:T(1024)}, u32[]{:S(2)}) copy-start(s32[1024]{0:T(1024)} %param.13) | copy-start | bytes 12292
  53.4 5.2 %copy-start.1 = (bf16[8,4,16,1024]{3,2,1,0:T(8,128)(2,1)}, bf16[8,4,16,1024]{3,2,1,0:T(8,128)(2,1)S(1)}, u32[]{:S(2)}) copy-start(bf16[8,4,16,1024]{3,2,1,0:T(8,128)(2,1)S(1)} %all-to-all-done.1) | copy-start | bytes 3145732
  53.4 31.5 %all-to-all-start.8 = ((bf16[8,512,256]{2,1,0:T(8,128)(2,1)}), bf16[8,512,256]{2,1,0:T(8,128)(2,1)}, u32[]{:S(2)}, u32[]{:S(2)}) async-start(bf16[8,512,256]{2,1,0:T(8,128)(2,1)} %project_kv.7), calls=%async_computation.8 | async-start | bytes 4194304 | tf_op jit(solution)/shard_map/all_to_all | solution.py:298
  65.2 55.5 %copy-start.4 = (bf16[32,16,1024]{2,1,0:T(8,128)(2,1)S(1)}, bf16[32,16,1024]{2,1,0:T(8,128)(2,1)}, u32[]{:S(2)}) copy-start(bf16[32,16,1024]{2,1,0:T(8,128)(2,1)} %get-tuple-element.11) | copy-start | bytes 3145732
  152.1 31.4 %all-to-all-start.4 = ((bf16[32,16,1024]{2,1,0:T(8,128)(2,1)}), bf16[32,16,1024]{2,1,0:T(8,128)(2,1)S(1)}, u32[]{:S(2)}, u32[]{:S(2)}) async-start(bf16[32,16,1024]{2,1,0:T(8,128)(2,1)} %get-tuple-element.12), calls=%async_computation.4 | async-start | bytes 2097152 | tf_op jit(solution)/shard_map/all_to_all | solution.py:306
  183.6 1.0 copy-start.3
  184.5 35.0 %all-to-all-start.7 = ((bf16[8,512,256]{2,1,0:T(8,128)(2,1)}), bf16[8,512,256]{2,1,0:T(8,128)(2,1)}, u32[]{:S(2)}, u32[]{:S(2)}) async-start(bf16[8,512,256]{2,1,0:T(8,128)(2,1)} %project_kv.6), calls=%async_computation.7 | async-start | bytes 4194304 | tf_op jit(solution)/shard_map/all_to_all | solution.py:308
  219.6 31.5 %all-to-all-start.3 = ((bf16[8,512,256]{2,1,0:T(8,128)(2,1)}), bf16[8,512,256]{2,1,0:T(8,128)(2,1)}, u32[]{:S(2)}, u32[]{:S(2)}) async-start(bf16[8,512,256]{2,1,0:T(8,128)(2,1)} %project_kv.4), calls=%async_computation.3 | async-start | bytes 4194304 | tf_op jit(solution)/shard_map/all_to_all | solution.py:308
  251.1 162.6 %all-to-all-start.5 = ((bf16[8,512,256]{2,1,0:T(8,128)(2,1)}), bf16[8,512,256]{2,1,0:T(8,128)(2,1)}, u32[]{:S(2)}, u32[]{:S(2)}) async-start(bf16[8,512,256]{2,1,0:T(8,128)(2,1)} %project_kv.5), calls=%async_computation.5 | async-start | bytes 4194304 | tf_op jit(solution)/shard_map/all_to_all | solution.py:308
  256.3 139.5 %all-reduce.2.cloned.1.call-start = ((), (), s32[]{:S(2)}) async-start(), calls=%async_computation.10 | async-start | bytes 262144 | tf_op jit(solution)/shard_map/psum | solution.py:316
  261.0 5.4 %collective-permute-start = (bf16[128,256]{1,0:T(8,128)(2,1)S(1)}, bf16[128,256]{1,0:T(8,128)(2,1)S(1)}, u32[]{:S(2)}, u32[]{:S(2)}) collective-permute-start(bf16[128,256]{1,0:T(8,128)(2,1)S(1)} %get-tuple-element.18), channel_id=1, source_target_pairs={{0,8},{8,16},{16,24},{24,32},{32,40},{40,48},{48,56},{56,64},{64,7... | collective-permute-start | bytes 196616 | tf_op jit(solution)/shard_map/ppermute | solution.py:313
  264.5 5.4 %collective-permute-start.1 = (bf16[128,256]{1,0:T(8,128)(2,1)S(1)}, bf16[128,256]{1,0:T(8,128)(2,1)S(1)}, u32[]{:S(2)}, u32[]{:S(2)}) collective-permute-start(bf16[128,256]{1,0:T(8,128)(2,1)S(1)} %get-tuple-element.17), channel_id=1, source_target_pairs={{8,0},{16,8},{24,16},{32,24},{40,32},{48,40},{56,48},{64,56},{72,6... | collective-permute-start | bytes 196616 | tf_op jit(solution)/shard_map/ppermute | solution.py:314
  266.4 129.4 %copy-start.7 = (bf16[128,256]{1,0:T(8,128)(2,1)}, bf16[128,256]{1,0:T(8,128)(2,1)S(1)}, u32[]{:S(2)}) copy-start(bf16[128,256]{1,0:T(8,128)(2,1)S(1)} %collective-permute-done.before_ref) | copy-start | bytes 196612
  269.9 125.9 %copy-start.8 = (bf16[128,256]{1,0:T(8,128)(2,1)}, bf16[128,256]{1,0:T(8,128)(2,1)S(1)}, u32[]{:S(2)}) copy-start(bf16[128,256]{1,0:T(8,128)(2,1)S(1)} %collective-permute-done.1.after_ref) | copy-start | bytes 196612
Sparse Core Ops, SparseCore 0:
  260.5 135.1 all-reduce.1

commit v2 on v1

v2 whole, which is shorter than its diff:
```python
import functools

import jax
import jax.numpy as jnp
from jax import lax
from jax.experimental import pallas as pl
from jax.experimental.pallas import tpu as pltpu
from jax.sharding import PartitionSpec as P


HEAD_DIM = 64
TILE = 128
GLOBALS = 2
RANDOM = 12
CAP = 3
LOG2E = 1.4426950408889634
SCALE = HEAD_DIM ** (-0.5) * LOG2E
NEG = -1e30


def project_kernel(here_ref, *refs, sources, weights, groups):
    x_refs, rest = refs[:sources], refs[sources:]
    w_refs, o_refs, x_ref = rest[:weights], rest[weights : weights + groups], rest[-1]
    step = pl.program_id(0)

    @pl.when(step == 0)
    def _():
        row = 0
        for ref in x_refs:
            x_ref[row : row + ref.shape[0]] = ref[...]
            row += ref.shape[0]

    w = jnp.concatenate([ref[...] for ref in w_refs], axis=1)
    r = jnp.dot(x_ref[...], w, preferred_element_type=jnp.float32).astype(jnp.bfloat16)
    for o, o_ref in enumerate(o_refs):

        @pl.when(step == o)
        def _():
            o_ref[...] = r


def project(here, xs, ws, groups):
    rows = sum(x.shape[0] for x in xs)
    width = xs[0].shape[1]
    lanes = ws[0].shape[1] // groups
    out_lanes = lanes * len(ws)
    return pl.pallas_call(
        functools.partial(project_kernel, sources=len(xs), weights=len(ws), groups=groups),
        grid_spec=pltpu.PrefetchScalarGridSpec(
            num_scalar_prefetch=1,
            grid=(groups,),
            in_specs=[pl.BlockSpec(x.shape, lambda o, here: (0, 0)) for x in xs]
            + [
                pl.BlockSpec((width, lanes), lambda o, here: (0, lax.rem(here[0] + o, groups)))
                for _ in ws
            ],
            out_specs=[pl.BlockSpec((rows, out_lanes), lambda o, here: (0, 0))] * groups,
            scratch_shapes=[pltpu.VMEM((rows, width), jnp.bfloat16)],
        ),
        out_shape=[jax.ShapeDtypeStruct((rows, out_lanes), jnp.bfloat16)] * groups,
        cost_estimate=pl.CostEstimate(
            flops=2 * rows * width * lanes * len(ws) * groups,
            transcendentals=0,
            bytes_accessed=2 * width * lanes * len(ws) * groups + 2 * rows * (width + out_lanes * groups),
        ),
    )(here, *xs, *ws)


def exchange(pieces, axis):
    size = len(pieces)
    return [pieces[0]] + [
        lax.ppermute(pieces[o], axis, [(i, (i + o) % size) for i in range(size)])
        for o in range(1, size)
    ]


def broadcast_first(value, axis, index):
    size = lax.axis_size(axis)
    hop = size // 2
    while hop:
        got = lax.ppermute(value, axis, [(i, i + hop) for i in range(0, size, 2 * hop)])
        value = jnp.where(lax.rem(index, 2 * hop) == hop, got, value)
        hop //= 2
    return value


def pick_kernel(index_ref, x_ref, *o_refs):
    count = x_ref.shape[0]

    def step(d, carry):
        for s, o_ref in enumerate(o_refs):
            o_ref[d] = x_ref[index_ref[s * count + d]]
        return carry

    lax.fori_loop(0, count, step, 0)


def pick_tiles(index, x, dests):
    whole = pl.BlockSpec(x.shape, lambda i, idx: (0, 0, 0))
    out = (dests,) + x.shape[1:]
    return pl.pallas_call(
        pick_kernel,
        grid_spec=pltpu.PrefetchScalarGridSpec(
            num_scalar_prefetch=1,
            grid=(1,),
            in_specs=[whole],
            out_specs=[pl.BlockSpec(out, lambda i, idx: (0, 0, 0))] * CAP,
        ),
        out_shape=[jax.ShapeDtypeStruct(out, x.dtype)] * CAP,
        cost_estimate=pl.CostEstimate(flops=0, transcendentals=0, bytes_accessed=4 * x.size * 2),
        name="pick_tiles",
    )(index, x)


def split_heads(q):
    first = lax.broadcasted_iota(jnp.int32, q.shape, 1) < HEAD_DIM
    zero = jnp.zeros_like(q)
    return jnp.concatenate([jnp.where(first, q, zero), jnp.where(first, zero, q)], axis=0)


def join_heads(both):
    half = both.shape[0] // 2
    shape = (half, 2 * HEAD_DIM)
    first = lax.broadcasted_iota(jnp.int32, shape, 1) < HEAD_DIM
    return jnp.where(
        first, jnp.broadcast_to(both[:half], shape), jnp.broadcast_to(both[half:], shape)
    )


def score(q2, keys):
    return lax.dot_general(q2, keys, (((1,), (1,)), ((), ())), preferred_element_type=jnp.float32)


def local_kernel(place_ref, *refs, groups):
    own_refs, ext_refs = refs[:groups], refs[groups : 2 * groups]
    m_ref, l_ref, a_ref, qo_ref, q_ref, pad_ref = refs[2 * groups :]
    own_rows = own_refs[0].shape[0]
    part = ext_refs[0].shape[0] // (2 + GLOBALS)
    tiles_here = own_rows * groups // TILE
    lanes = m_ref.shape[1]
    step = pl.program_id(0)
    per_step = m_ref.shape[0] // TILE

    @pl.when(step == 0)
    def _():
        homes = [0] + [tiles_here + 1 + i for i in range(1 + GLOBALS)]
        for o in range(groups):
            row = pl.multiple_of(lax.rem(place_ref[2] + groups - o, groups) * own_rows, own_rows)
            q_ref[pl.ds(row, own_rows), :] = own_refs[o][:, :lanes]
            pad_ref[pl.ds(row + TILE, own_rows), :] = own_refs[o][:, lanes:]
            for i, home in enumerate(homes):
                row = home * TILE + o * part
                pad_ref[row : row + part, :] = ext_refs[o][i * part : (i + 1) * part, :]

    tiles_total = place_ref[1]
    global_kv = pad_ref[(tiles_here + 2) * TILE :, :]
    for i in range(per_step):
        t = step * per_step + i
        rows = pl.ds(i * TILE, TILE)
        q = q_ref[pl.ds(pl.multiple_of(t * TILE, TILE), TILE), :]
        q2 = split_heads(q)
        window = pad_ref[pl.ds(pl.multiple_of(t * TILE, TILE), 3 * TILE), :]
        first_id = place_ref[0] * tiles_here + t - 1
        position = lax.broadcasted_iota(jnp.int32, (2 * TILE, 3 * TILE), 1)
        ok = (position >= (GLOBALS - first_id) * TILE) & (
            position < (tiles_total - first_id) * TILE
        )
        s_window = jnp.where(ok, score(q2, window[:, :lanes]), NEG)
        s_global = score(q2, global_kv[:, :lanes])
        top = jnp.maximum(
            jnp.max(s_window, axis=1, keepdims=True), jnp.max(s_global, axis=1, keepdims=True)
        )
        p_window = jnp.exp2((s_window - top) * SCALE)
        p_global = jnp.exp2((s_global - top) * SCALE)
        total = jnp.sum(p_window, axis=1, keepdims=True) + jnp.sum(p_global, axis=1, keepdims=True)
        acc = jnp.dot(
            p_window.astype(jnp.bfloat16), window[:, lanes:], preferred_element_type=jnp.float32
        ) + jnp.dot(
            p_global.astype(jnp.bfloat16), global_kv[:, lanes:], preferred_element_type=jnp.float32
        )
        m_ref[rows, :] = join_heads(top)
        l_ref[rows, :] = join_heads(total)
        a_ref[rows, :] = join_heads(acc)
        qo_ref[rows, :] = q


def local_attention(place, own, ext, ext_rows, per_step=2):
    groups = len(own)
    rows = own[0].shape[0] * groups
    both = ext[0].shape[1]
    lanes = both // 2
    block = pl.BlockSpec((per_step * TILE, lanes), lambda i, s: (i, 0))
    last = ext[0].shape[0] // ext_rows - 1
    out = jax.ShapeDtypeStruct((rows, lanes), jnp.float32)
    keys = (3 + GLOBALS) * TILE
    return pl.pallas_call(
        functools.partial(local_kernel, groups=groups),
        grid_spec=pltpu.PrefetchScalarGridSpec(
            num_scalar_prefetch=1,
            grid=(rows // (per_step * TILE),),
            in_specs=[pl.BlockSpec(a.shape, lambda i, s: (0, 0)) for a in own]
            + [pl.BlockSpec((ext_rows, both), lambda i, s: (last, 0)) for _ in ext],
            out_specs=[block] * 4,
            scratch_shapes=[
                pltpu.VMEM((rows, lanes), jnp.bfloat16),
                pltpu.VMEM((rows + (2 + GLOBALS) * TILE, both), jnp.bfloat16),
            ],
        ),
        out_shape=[out] * 3 + [jax.ShapeDtypeStruct((rows, lanes), jnp.bfloat16)],
        cost_estimate=pl.CostEstimate(
            flops=8 * rows * keys * lanes,
            transcendentals=2 * rows * keys,
            bytes_accessed=rows * lanes * 20,
        ),
        name="local_attention",
    )(place, *own, *ext)


def random_kernel(index_ref, count_ref, *refs, groups):
    part_refs = refs[: CAP * groups]
    q_ref, m_ref, l_ref, a_ref, o_ref, kv_ref = refs[CAP * groups :]
    lanes = q_ref.shape[1]
    step = pl.program_id(0)
    per_step = q_ref.shape[0] // TILE
    part = TILE // groups
    shards = part_refs[0].shape[0] // part

    @pl.when(step == 0)
    def _():
        for i, ref in enumerate(part_refs):
            s, o = divmod(i, groups)
            kv_ref[s * shards : (s + 1) * shards, o * part : (o + 1) * part, :] = ref[...].reshape(
                shards, part, 2 * lanes
            )

    for i in range(per_step):
        t = step * per_step + i
        rows = pl.ds(i * TILE, TILE)
        q2 = split_heads(q_ref[rows, :])
        count = count_ref[t]
        at = [index_ref[t * RANDOM + j] for j in range(RANDOM)]
        scores = []
        top = None
        for j in range(RANDOM):
            bias = jnp.where(j < count, 0.0, NEG).astype(jnp.float32)
            s = score(q2, kv_ref[at[j], :, :lanes]) + bias
            scores.append(s)
            top = s if top is None else jnp.maximum(top, s)
        m_old = m_ref[rows, :]
        m_old = jnp.concatenate([m_old[:, :1], m_old[:, HEAD_DIM : HEAD_DIM + 1]], axis=0)
        m_new = jnp.maximum(jnp.max(top, axis=1, keepdims=True), m_old)
        alpha = jnp.exp2((m_old - m_new) * SCALE)
        total = None
        acc = None
        for j in range(0, RANDOM, 2):
            p0 = jnp.exp2((scores[j] - m_new) * SCALE)
            p1 = jnp.exp2((scores[j + 1] - m_new) * SCALE)
            total = p0 + p1 if total is None else total + (p0 + p1)
            p = jnp.concatenate([p0.astype(jnp.bfloat16), p1.astype(jnp.bfloat16)], axis=1)
            v = jnp.concatenate([kv_ref[at[j], :, lanes:], kv_ref[at[j + 1], :, lanes:]], axis=0)
            part = jnp.dot(p, v, preferred_element_type=jnp.float32)
            acc = part if acc is None else acc + part
        alpha = join_heads(alpha)
        denominator = l_ref[rows, :] * alpha + join_heads(jnp.sum(total, axis=1, keepdims=True))
        numerator = a_ref[rows, :] * alpha + join_heads(acc)
        o_ref[rows, :] = (numerator / denominator).astype(jnp.bfloat16)


def random_attention(index, count, q, fetched, m, l, a, part_rows, per_step=2):
    rows, lanes = q.shape
    groups = len(fetched) // CAP
    block = pl.BlockSpec((per_step * TILE, lanes), lambda i, s, c: (i, 0))
    fixed = pl.BlockSpec((part_rows, 2 * lanes), lambda i, s, c: (0, 0))
    keys = RANDOM * TILE
    return pl.pallas_call(
        functools.partial(random_kernel, groups=groups),
        grid_spec=pltpu.PrefetchScalarGridSpec(
            num_scalar_prefetch=2,
            grid=(rows // (per_step * TILE),),
            in_specs=[fixed] * len(fetched) + [block] * 4,
            out_specs=block,
            scratch_shapes=[
                pltpu.VMEM((CAP * part_rows * groups // TILE, TILE, 2 * lanes), jnp.bfloat16)
            ],
        ),
        out_shape=jax.ShapeDtypeStruct((rows, lanes), jnp.bfloat16),
        cost_estimate=pl.CostEstimate(
            flops=8 * rows * keys * lanes,
            transcendentals=2 * rows * keys,
            bytes_accessed=rows * lanes * 16 + CAP * part_rows * groups * lanes * 4,
        ),
        name="random_attention",
    )(index, count, *fetched, q, m, l, a)


def request_tables(random_tiles, random_count, shard, ctx_count, tiles_here):
    slots = random_tiles.shape[1]
    live = jnp.arange(slots, dtype=jnp.int32)[None, :] < random_count[:, None]
    entries = jnp.where(live, random_tiles, -1).reshape(ctx_count, tiles_here * slots)
    mine = shard * tiles_here + jnp.arange(tiles_here, dtype=jnp.int32)
    owned = jnp.any(entries[:, :, None] == mine[None, None, :], axis=1)
    k = jnp.arange(tiles_here, dtype=jnp.int32)
    rank = jnp.sum((owned[:, None, :] & (k[None, None, :] < k[None, :, None])).astype(jnp.int32), axis=2)
    hit = owned[:, None, :] & (rank[:, None, :] == jnp.arange(CAP, dtype=jnp.int32)[None, :, None])
    send = jnp.sum(jnp.where(hit, k[None, None, :], 0), axis=2)
    wanted = lax.dynamic_index_in_dim(entries, shard, 0, keepdims=False)
    tiles = jnp.arange(ctx_count * tiles_here, dtype=jnp.int32)
    needed = jnp.any(wanted[:, None] == tiles[None, :], axis=0)
    owner = wanted // tiles_here
    lower = (
        needed[None, :]
        & (tiles[None, :] < wanted[:, None])
        & (tiles[None, :] >= (owner * tiles_here)[:, None])
    )
    slot = jnp.sum(lower.astype(jnp.int32), axis=1)
    read = jnp.where(wanted >= 0, slot * ctx_count + owner, 0)
    return send.T.reshape(-1), read


def body(tokens, w_query, w_key, w_value, w_out, random_tiles, random_count):
    groups = lax.axis_size("head")
    ctx_count = lax.axis_size("ctx")
    rows, width = tokens.shape
    own_tiles = rows // TILE
    part = TILE // groups
    tiles_here = own_tiles * groups
    shard = lax.axis_index("ctx").astype(jnp.int32)

    here = lax.axis_index("head").astype(jnp.int32)

    striped = tokens.reshape(own_tiles, groups, part, width).transpose(1, 0, 2, 3)
    striped = lax.all_to_all(striped, "head", split_axis=0, concat_axis=0, tiled=True)
    striped = striped.reshape(tiles_here, part, width)
    send, read = request_tables(random_tiles, random_count, shard, ctx_count, tiles_here)
    outgoing = pick_tiles(send, striped, ctx_count)

    where = here[None]
    own = project(where, [tokens], [w_query, w_key, w_value], groups)
    own = exchange(own, "head")

    up = [(i, i + 1) for i in range(ctx_count - 1)]
    down = [(j, i) for i, j in up]
    before = lax.ppermute(striped[-1:], "ctx", up)
    after = lax.ppermute(striped[:1], "ctx", down)
    root = broadcast_first(striped[:GLOBALS], "ctx", shard)
    ext = jnp.concatenate([before, after, root], axis=0).reshape(-1, width)

    fetched = []
    for slot in range(CAP):
        got = lax.all_to_all(outgoing[slot], "ctx", split_axis=0, concat_axis=0, tiled=True)
        got = [got.reshape(ctx_count * part, width)] + ([ext] if slot == 0 else [])
        got = project(where, got, [w_key, w_value], groups)
        fetched += exchange(got, "head")

    place = jnp.stack([shard, jnp.int32(tiles_here * ctx_count), here])
    m, l, a, q = local_attention(place, own, fetched[:groups], ext.shape[0])
    my_count = lax.dynamic_slice_in_dim(random_count, shard * tiles_here, tiles_here, 0)
    attended = random_attention(read, my_count, q, fetched, m, l, a, ctx_count * part)
    attended = attended.reshape(groups, rows, -1)
    returned = lax.all_to_all(attended, "head", split_axis=0, concat_axis=0, tiled=True)
    out = lax.dot_general(
        returned,
        w_out.reshape(groups, -1, width),
        (((0, 2), (0, 1)), ((), ())),
        preferred_element_type=jnp.float32,
    )
    return out.astype(jnp.bfloat16)


def solution(mesh):
    return jax.shard_map(
        body,
        mesh=mesh,
        in_specs=(P(("ctx", "head"), None), P(), P(), P(), P(), P(), P()),
        out_specs=P(("ctx", "head"), None),
        check_vma=False,
    )
```

time: 484 us -> 318 us (0.66)
  waiting for transfers between devices: 223 us -> 77 us
  blocking collectives: 91.4 us -> 54.9 us
  starting transfers between devices: 47.8 us -> 71.5 us
  between operations: 13.5 us -> 0.34 us
  local copies, waits for them, and re-layouts: 4.72 us -> 10.2 us
    psum x1 -> x0, waiting for transfers between devices: 126 us -> none  [body(): lax.psum(jnp.where(shard == 0, root, 0).astype(root.dtype), 'ctx')]
    all_to_all x5 -> x0, waiting for transfers between devices: 70.2 us -> none  [the longest x3 36.5 us: body(): got = lax.all_to_all(got, 'head', split_axis=0, concat_axis=0, tiled=True)]
    ppermute x2 -> x35, waiting for transfers between devices: 3.45 us -> 62.2 us  [the longest x28 51.8 us: exchange(): lax.ppermute(pieces[o], axis, [(i, (i + o) % size) for i in range(size)])]
    ppermute x2 -> x35, starting transfers between devices: 4.73 us -> 51 us  [the longest x28 33.9 us: exchange(): lax.ppermute(pieces[o], axis, [(i, (i + o) % size) for i in range(size)])]
    all_to_all x5 -> x0, starting transfers between devices: 31.7 us -> none  [the longest x3 19.1 us: body(): got = lax.all_to_all(got, 'head', split_axis=0, concat_axis=0, tiled=True)]
    all_to_all x2 -> x1, blocking collectives: 67.2 us -> 36.5 us  [body(): lax.all_to_all(outgoing[slot], 'ctx', split_axis=0, concat_axis=0, tiled=...]
    all_to_all x1 -> x2, waiting for transfers between devices: 16.5 us -> 4.28 us  [body(): lax.all_to_all(outgoing[slot], 'ctx', split_axis=0, concat_axis=0, tiled=...]
    all_to_all x1 -> x2, starting transfers between devices: 6.9 us -> 13.8 us  [body(): lax.all_to_all(outgoing[slot], 'ctx', split_axis=0, concat_axis=0, tiled=...]
  transfers between devices with their start and end apart: 10 -> 38, of which waited for: 8 -> 12; matrix products, arithmetic and copies ran while one was open for 2% -> 3% of each run, Pallas kernels for 11% -> 18%
where the time goes in v2:
time: 318 us; the launch traced here: 316 us
  Pallas kernels  94.9 us (30%)
  waiting for transfers between devices  77 us (24%)
  starting transfers between devices  71.5 us (22%)
  blocking collectives  54.9 us (17%)
  local copies, waits for them, and re-layouts  10.2 us (3%)
  other arithmetic  5.35 us (2%)
    ppermute x28, waiting for transfers between devices, exchange(): lax.ppermute(pieces[o], axis, [(i, (i + o) % size) for i in range(size)])  51.8 us
    pallas_call x4, Pallas kernels, project(): pl.pallas_call(functools.partial(project_kernel, sources=len(xs), weights...  37.2 us
    all_to_all x1, blocking collectives, body(): lax.all_to_all(outgoing[slot], 'ctx', split_axis=0, concat_axis=0, tiled=...  36.5 us
    pallas_call x1, Pallas kernels, random_attention(): pl.pallas_call(functools.partial(random_kernel, groups=groups), grid_spec...  35.1 us
    ppermute x28, starting transfers between devices, exchange(): lax.ppermute(pieces[o], axis, [(i, (i + o) % size) for i in range(size)])  33.9 us
    pallas_call x1, Pallas kernels, local_attention(): pl.pallas_call(functools.partial(local_kernel, groups=groups), grid_spec=...  18.7 us
    all_to_all x1, blocking collectives, body(): lax.all_to_all(attended, 'head', split_axis=0, concat_axis=0, tiled=True)  18.4 us
    ppermute x5, starting transfers between devices, broadcast_first(): lax.ppermute(value, axis, [(i, i + hop) for i in range(0, size, 2 * hop)])  14.6 us
  transfers between devices with their start and end apart: 38, of which 12 were waited for; matrix products, arithmetic and copies ran while one was open for 3% of the time, Pallas kernels for 18%

profile of v2, /device:TPU:1, one launch (start us, length us, event | category | flops | bytes accessed | tf_op | source)
XLA Modules:
  0.0 316.3 jit_solution(8373190684105322547)
XLA Ops:
  0.0 2.5 copy.14
  2.5 6.7 %all-to-all-start = ((bf16[8,4,16,1024]{3,2,1,0:T(8,128)(2,1)}), bf16[8,4,16,1024]{3,2,1,0:T(8,128)(2,1)S(1)}, u32[]{:S(2)}, u32[]{:S(2)}) async-start(bf16[8,4,16,1024]{3,2,1,0:T(8,128)(2,1)} %bitcast.23), calls=%async_computation | async-start | bytes 2097152 | tf_op jit(solution)/shard_map/all_to_all | solution.py:332
  13.7 10.5 %all-to-all-done = bf16[8,4,16,1024]{3,2,1,0:T(8,128)(2,1)S(1)} async-done(((bf16[8,4,16,1024]{3,2,1,0:T(8,128)(2,1)}), bf16[8,4,16,1024]{3,2,1,0:T(8,128)(2,1)S(1)}, u32[]{:S(2)}, u32[]{:S(2)}) %all-to-all-start) | async-done | bytes 1048608 | tf_op jit(solution)/shard_map/all_to_all | solution.py:332
  25.1 3.9 %pick_tiles.1 = (bf16[32,16,1024]{2,1,0:T(8,128)(2,1)}, bf16[32,16,1024]{2,1,0:T(8,128)(2,1)}, bf16[32,16,1024]{2,1,0:T(8,128)(2,1)}) custom-call(s32[96]{0:T(128)} %reshape.86.index_ref, bf16[32,16,1024]{2,1,0:T(8,128)(2,1)} %bitcast.19), custom_call_target="tpu_custom_call" | custom-call | bytes 4194304 | tf_op jit(solution)/shard_map/pick_tiles/pallas_call | solution.py:101
  29.0 36.5 %all_to_all.25 = bf16[32,16,1024]{2,1,0:T(8,128)(2,1)} all-to-all(bf16[32,16,1024]{2,1,0:T(8,128)(2,1)} %get-tuple-element.53), channel_id=1, replica_groups=mesh['ctx'=32,'head'=8] {'ctx'}, dimensions={0} | all-to-all | bytes 2097152 | tf_op jit(solution)/shard_map/all_to_all | solution.py:350
  65.4 6.3 %all-to-all-start.3 = ((bf16[32,16,1024]{2,1,0:T(8,128)(2,1)}), bf16[32,16,1024]{2,1,0:T(8,128)(2,1)S(1)}, u32[]{:S(2)}, u32[]{:S(2)}) async-start(bf16[32,16,1024]{2,1,0:T(8,128)(2,1)} %get-tuple-element.62), calls=%async_computation.3 | async-start | bytes 2097152 | tf_op jit(solution)/shard_map/all_to_all | solution.py:350
  72.6 7.0 %collective-permute-start.2 = (bf16[2,16,1024]{2,1,0:T(8,128)(2,1)S(1)}, bf16[2,16,1024]{2,1,0:T(8,128)(2,1)S(1)}, u32[]{:S(2)}, u32[]{:S(2)}) collective-permute-start(bf16[2,16,1024]{2,1,0:T(8,128)(2,1)S(1)} %slice.14), channel_id=1, source_target_pairs={{0,128},{1,129},{2,130},{3,131},{4,132},{5,133},{6,134},{7,135}} | collective-permute-start | bytes 196616 | tf_op jit(solution)/shard_map/ppermute | solution.py:81
  79.7 10.4 %collective-permute-done.2 = bf16[2,16,1024]{2,1,0:T(8,128)(2,1)S(1)} collective-permute-done((bf16[2,16,1024]{2,1,0:T(8,128)(2,1)S(1)}, bf16[2,16,1024]{2,1,0:T(8,128)(2,1)S(1)}, u32[]{:S(2)}, u32[]{:S(2)}) %collective-permute-start.2) | collective-permute-done | bytes 65568 | tf_op jit(solution)/shard_map/ppermute | solution.py:81
  92.2 4.3 %all-to-all-done.3 = bf16[32,16,1024]{2,1,0:T(8,128)(2,1)S(1)} async-done(((bf16[32,16,1024]{2,1,0:T(8,128)(2,1)}), bf16[32,16,1024]{2,1,0:T(8,128)(2,1)S(1)}, u32[]{:S(2)}, u32[]{:S(2)}) %all-to-all-start.3) | async-done | bytes 1048608 | tf_op jit(solution)/shard_map/all_to_all | solution.py:350
  96.5 7.4 %all-to-all-start.1 = ((bf16[32,16,1024]{2,1,0:T(8,128)(2,1)}), bf16[32,16,1024]{2,1,0:T(8,128)(2,1)}, u32[]{:S(2)}, u32[]{:S(2)}) async-start(bf16[32,16,1024]{2,1,0:T(8,128)(2,1)} %get-tuple-element.44), calls=%async_computation.1 | async-start | bytes 2097152 | tf_op jit(solution)/shard_map/all_to_all | solution.py:350
  104.0 3.1 collective-permute-start.4
  107.1 10.9 %shard_map.76 = (bf16[512,384]{1,0:T(8,128)(2,1)}, bf16[512,384]{1,0:T(8,128)(2,1)}, bf16[512,384]{1,0:T(8,128)(2,1)}, bf16[512,384]{1,0:T(8,128)(2,1)}, bf16[51...) custom-call(s32[1]{0:T(128)} %bitcast.here_ref, ...), custom_call_target="tpu_custom_call" | custom-call | flops 3221225472 | bytes 10485760 | tf_op jit(solution)/shard_map/pallas_call | solution.py:47
  118.0 4.0 %collective-permute-start.28 = (bf16[512,384]{1,0:T(8,128)(2,1)}, bf16[512,384]{1,0:T(8,128)(2,1)S(1)}, u32[]{:S(2)}, u32[]{:S(2)}) collective-permute-start(bf16[512,384]{1,0:T(8,128)(2,1)} %get-tuple-element.72), channel_id=1, source_target_pairs={{0,1},{1,2},{2,3},{3,4},{4,5},{5,6},{6,7},{7,0},{8,9},{9,10},{10,1... | collective-permute-start | bytes 1179656 | tf_op jit(solution)/shard_map/ppermute | solution.py:72
  122.1 2.0 collective-permute-start.30
  124.2 1.9 collective-permute-start.5
  132.4 10.4 %collective-permute-done.29.refs_2_ = bf16[512,384]{1,0:T(8,128)(2,1)S(1)} collective-permute-done((bf16[512,384]{1,0:T(8,128)(2,1)}, bf16[512,384]{1,0:T(8,128)(2,1)S(1)}, u32[]{:S(2)}, u32[]{:S(2)}) %collective-permute-start.29) | collective-permute-done | bytes 393248 | tf_op jit(solution)/shard_map/ppermute | solution.py:72
  142.8 16.6 %collective-permute-done.30.refs_3_ = bf16[512,384]{1,0:T(8,128)(2,1)} collective-permute-done((bf16[512,384]{1,0:T(8,128)(2,1)}, bf16[512,384]{1,0:T(8,128)(2,1)}, u32[]{:S(2)}, u32[]{:S(2)}) %collective-permute-start.30) | collective-permute-done | bytes 393248 | tf_op jit(solution)/shard_map/ppermute | solution.py:72
  161.0 8.7 %shard_map.74 = (bf16[512,256]{1,0:T(8,128)(2,1)}, bf16[512,256]{1,0:T(8,128)(2,1)}, bf16[512,256]{1,0:T(8,128)(2,1)}, bf16[512,256]{1,0:T(8,128)(2,1)}, bf16[51...) custom-call(s32[1]{0:T(128)} %bitcast.here_ref, ...), custom_call_target="tpu_custom_call" | custom-call | flops 2147483648 | bytes 7340032 | tf_op jit(solution)/shard_map/pallas_call | solution.py:47
  177.2 8.6 %shard_map.75 = (bf16[512,256]{1,0:T(8,128)(2,1)}, bf16[512,256]{1,0:T(8,128)(2,1)}, bf16[512,256]{1,0:T(8,128)(2,1)}, bf16[512,256]{1,0:T(8,128)(2,1)}, bf16[51...) custom-call(s32[1]{0:T(128)} %bitcast.here_ref, ...), custom_call_target="tpu_custom_call" | custom-call | flops 2147483648 | bytes 7340032 | tf_op jit(solution)/shard_map/pallas_call | solution.py:47
  185.9 9.0 %shard_map.73 = (bf16[576,256]{1,0:T(8,128)(2,1)}, bf16[576,256]{1,0:T(8,128)(2,1)}, bf16[576,256]{1,0:T(8,128)(2,1)}, bf16[576,256]{1,0:T(8,128)(2,1)}, bf16[57...) custom-call(s32[1]{0:T(128)} %bitcast.here_ref, ...), custom_call_target="tpu_custom_call" | custom-call | flops 2415919104 | bytes 7733248 | tf_op jit(solution)/shard_map/pallas_call | solution.py:47
  195.6 2.4 collective-permute-start.10
  198.7 2.7 collective-permute-start.11
  203.6 11.5 %collective-permute-done.20.refs_15_ = bf16[512,256]{1,0:T(8,128)(2,1)S(1)} collective-permute-done((bf16[512,256]{1,0:T(8,128)(2,1)}, bf16[512,256]{1,0:T(8,128)(2,1)S(1)}, u32[]{:S(2)}, u32[]{:S(2)}) %collective-permute-start.20) | collective-permute-done | bytes 262176 | tf_op jit(solution)/shard_map/ppermute | solution.py:72
  215.1 2.3 collective-permute-start.12
  222.1 2.9 collective-permute-done.12.refs_14_.refs_6_
  226.0 4.3 %collective-permute-done.13.refs_15_.refs_7_ = bf16[576,256]{1,0:T(8,128)(2,1)} collective-permute-done((bf16[576,256]{1,0:T(8,128)(2,1)}, bf16[576,256]{1,0:T(8,128)(2,1)}, u32[]{:S(2)}, u32[]{:S(2)}) %collective-permute-start.13) | collective-permute-done | bytes 294944 | tf_op jit(solution)/shard_map/ppermute | solution.py:72
  234.1 4.1 %collective-permute-done.9.refs_11_.refs_3_ = bf16[576,256]{1,0:T(8,128)(2,1)} collective-permute-done((bf16[576,256]{1,0:T(8,128)(2,1)}, bf16[576,256]{1,0:T(8,128)(2,1)}, u32[]{:S(2)}, u32[]{:S(2)}) %collective-permute-start.9) | collective-permute-done | bytes 294944 | tf_op jit(solution)/shard_map/ppermute | solution.py:72
  238.2 2.3 collective-permute-start.27
  241.8 18.7 %local_attention.1 = (f32[4096,128]{1,0:T(8,128)}, f32[4096,128]{1,0:T(8,128)}, f32[4096,128]{1,0:T(8,128)}, bf16[4096,128]{1,0:T(8,128)(2,1)}) custom-call(s32[3]{0:T(128)} %pad_add_fusion.place_ref, bf16[512,384]{1,0:T(8,128)(2,1)} %get-tuple-element.71.refs_0_, bf16[512,384]{1,0:T(8,128)(2,1)} %copy-done.5, bf16[512,384]{1,0:T(8,128)(2,1)} %copy-done.6, ...), custom_call_target="tpu_custom_call" | custom-call | flops 2684354560 | bytes 10485760 | tf_op jit(solution)/shard_map/local_attention/pallas_call | solution.py:196
  260.5 35.1 %random_attention.1 = bf16[4096,128]{1,0:T(8,128)(2,1)} custom-call(s32[384]{0:T(512)} %add_select_fusion.1.index_ref, s32[32]{0:T(128)} %dynamic_slice.8.count_ref, bf16[576,256]{1,0:T(8,128)(2,1)} %get-tuple-element.45.refs_8_.refs_0_, bf16[576,256]{1,0:T(8,128)(2,1)} %collective-permute-done.7.refs_9_.refs_1_, ...), custom_call_target="tpu_custom_call" | custom-call | flops 6442450944 | bytes 14680064 | tf_op jit(solution)/shard_map/random_attention/pallas_call | solution.py:275
  295.6 18.4 %all_to_all.26 = bf16[8,512,128]{2,1,0:T(8,128)(2,1)S(1)} all-to-all(bf16[8,512,128]{2,1,0:T(8,128)(2,1)} %bitcast.27), channel_id=1, replica_groups=mesh['ctx'=32,'head'=8] {'head'}, dimensions={0} | all-to-all | bytes 2097152 | tf_op jit(solution)/shard_map/all_to_all | solution.py:360
  314.1 2.3 bitcast_convert_fusion
  (115 shorter events, 38.4 us)
Async XLA Ops:
  2.5 21.7 %all-to-all-start = ((bf16[8,4,16,1024]{3,2,1,0:T(8,128)(2,1)}), bf16[8,4,16,1024]{3,2,1,0:T(8,128)(2,1)S(1)}, u32[]{:S(2)}, u32[]{:S(2)}) async-start(bf16[8,4,16,1024]{3,2,1,0:T(8,128)(2,1)} %bitcast.23), calls=%async_computation | async-start | bytes 2097152 | tf_op jit(solution)/shard_map/all_to_all | solution.py:332
  65.4 31.1 %all-to-all-start.3 = ((bf16[32,16,1024]{2,1,0:T(8,128)(2,1)}), bf16[32,16,1024]{2,1,0:T(8,128)(2,1)S(1)}, u32[]{:S(2)}, u32[]{:S(2)}) async-start(bf16[32,16,1024]{2,1,0:T(8,128)(2,1)} %get-tuple-element.62), calls=%async_computation.3 | async-start | bytes 2097152 | tf_op jit(solution)/shard_map/all_to_all | solution.py:350
  72.6 17.5 %collective-permute-start.2 = (bf16[2,16,1024]{2,1,0:T(8,128)(2,1)S(1)}, bf16[2,16,1024]{2,1,0:T(8,128)(2,1)S(1)}, u32[]{:S(2)}, u32[]{:S(2)}) collective-permute-start(bf16[2,16,1024]{2,1,0:T(8,128)(2,1)S(1)} %slice.14), channel_id=1, source_target_pairs={{0,128},{1,129},{2,130},{3,131},{4,132},{5,133},{6,134},{7,135}} | collective-permute-start | bytes 196616 | tf_op jit(solution)/shard_map/ppermute | solution.py:81
  90.9 13.0 %collective-permute-start.3 = (bf16[2,16,1024]{2,1,0:T(8,128)(2,1)S(1)}, bf16[2,16,1024]{2,1,0:T(8,128)(2,1)S(1)}, u32[]{:S(2)}, u32[]{:S(2)}) collective-permute-start(bf16[2,16,1024]{2,1,0:T(8,128)(2,1)S(1)} %broadcast_select_fusion), channel_id=1, source_target_pairs={{0,64},{128,192},{1,65},{129,193},{2,66},{130,194},{3,67},{131,195... | collective-permute-start | bytes 196616 | tf_op jit(solution)/shard_map/ppermute | solution.py:81
  96.5 89.4 %all-to-all-start.1 = ((bf16[32,16,1024]{2,1,0:T(8,128)(2,1)}), bf16[32,16,1024]{2,1,0:T(8,128)(2,1)}, u32[]{:S(2)}, u32[]{:S(2)}) async-start(bf16[32,16,1024]{2,1,0:T(8,128)(2,1)} %get-tuple-element.44), calls=%async_computation.1 | async-start | bytes 2097152 | tf_op jit(solution)/shard_map/all_to_all | solution.py:350
  104.0 20.2 %collective-permute-start.4 = (bf16[2,16,1024]{2,1,0:T(8,128)(2,1)S(1)}, bf16[2,16,1024]{2,1,0:T(8,128)(2,1)S(1)}, u32[]{:S(2)}, u32[]{:S(2)}) collective-permute-start(bf16[2,16,1024]{2,1,0:T(8,128)(2,1)S(1)} %broadcast_select_fusion.1), channel_id=1, source_target_pairs={{0,32},{64,96},{128,160},{192,224},{1,33},{65,97},{129,161},{193,2... | collective-permute-start | bytes 196616 | tf_op jit(solution)/shard_map/ppermute | solution.py:81
  122.0 20.8 %collective-permute-start.29 = (bf16[512,384]{1,0:T(8,128)(2,1)}, bf16[512,384]{1,0:T(8,128)(2,1)S(1)}, u32[]{:S(2)}, u32[]{:S(2)}) collective-permute-start(bf16[512,384]{1,0:T(8,128)(2,1)} %get-tuple-element.73), channel_id=1, source_target_pairs={{0,2},{1,3},{2,4},{3,5},{4,6},{5,7},{6,0},{7,1},{8,10},{9,11},{10,... | collective-permute-start | bytes 1179656 | tf_op jit(solution)/shard_map/ppermute | solution.py:72
  122.1 37.3 %collective-permute-start.30 = (bf16[512,384]{1,0:T(8,128)(2,1)}, bf16[512,384]{1,0:T(8,128)(2,1)}, u32[]{:S(2)}, u32[]{:S(2)}) collective-permute-start(bf16[512,384]{1,0:T(8,128)(2,1)} %get-tuple-element.74), channel_id=1, source_target_pairs={{0,3},{1,4},{2,5},{3,6},{4,7},{5,0},{6,1},{7,2},{8,11},{9,12},{10,... | collective-permute-start | bytes 1179656 | tf_op jit(solution)/shard_map/ppermute | solution.py:72
  126.9 32.5 %collective-permute-start = (bf16[1,16,1024]{2,1,0:T(8,128)(2,1)S(1)}, bf16[1,16,1024]{2,1,0:T(8,128)(2,1)S(1)}, u32[]{:S(2)}, u32[]{:S(2)}) collective-permute-start(bf16[1,16,1024]{2,1,0:T(8,128)(2,1)S(1)} %get-tuple-element.83), channel_id=1, source_target_pairs={{0,8},{8,16},{16,24},{24,32},{32,40},{40,48},{48,56},{56,64},{64,7... | collective-permute-start | bytes 98312 | tf_op jit(solution)/shard_map/ppermute | solution.py:343
  128.2 31.5 %collective-permute-start.1 = (bf16[1,16,1024]{2,1,0:T(8,128)(2,1)S(1)}, bf16[1,16,1024]{2,1,0:T(8,128)(2,1)S(1)}, u32[]{:S(2)}, u32[]{:S(2)}) collective-permute-start(bf16[1,16,1024]{2,1,0:T(8,128)(2,1)S(1)} %get-tuple-element.84), channel_id=1, source_target_pairs={{8,0},{16,8},{24,16},{32,24},{40,32},{48,40},{56,48},{64,56},{72,6... | collective-permute-start | bytes 98312 | tf_op jit(solution)/shard_map/ppermute | solution.py:344
  130.6 41.2 %collective-permute-start.31 = (bf16[512,384]{1,0:T(8,128)(2,1)}, bf16[512,384]{1,0:T(8,128)(2,1)}, u32[]{:S(2)}, u32[]{:S(2)}) collective-permute-start(bf16[512,384]{1,0:T(8,128)(2,1)} %get-tuple-element.75), channel_id=1, source_target_pairs={{0,4},{1,5},{2,6},{3,7},{4,0},{5,1},{6,2},{7,3},{8,12},{9,13},{10,... | collective-permute-start | bytes 1179656 | tf_op jit(solution)/shard_map/ppermute | solution.py:72
  142.8 30.5 %collective-permute-start.32 = (bf16[512,384]{1,0:T(8,128)(2,1)}, bf16[512,384]{1,0:T(8,128)(2,1)}, u32[]{:S(2)}, u32[]{:S(2)}) collective-permute-start(bf16[512,384]{1,0:T(8,128)(2,1)} %get-tuple-element.76), channel_id=1, source_target_pairs={{0,5},{1,6},{2,7},{3,0},{4,1},{5,2},{6,3},{7,4},{8,13},{9,14},{10,... | collective-permute-start | bytes 1179656 | tf_op jit(solution)/shard_map/ppermute | solution.py:72
  159.4 14.3 %collective-permute-start.33 = (bf16[512,384]{1,0:T(8,128)(2,1)}, bf16[512,384]{1,0:T(8,128)(2,1)}, u32[]{:S(2)}, u32[]{:S(2)}) collective-permute-start(bf16[512,384]{1,0:T(8,128)(2,1)} %get-tuple-element.77), channel_id=1, source_target_pairs={{0,6},{1,7},{2,0},{3,1},{4,2},{5,3},{6,4},{7,5},{8,14},{9,15},{10,... | collective-permute-start | bytes 1179656 | tf_op jit(solution)/shard_map/ppermute | solution.py:72
  159.4 15.8 %collective-permute-start.34 = (bf16[512,384]{1,0:T(8,128)(2,1)}, bf16[512,384]{1,0:T(8,128)(2,1)}, u32[]{:S(2)}, u32[]{:S(2)}) collective-permute-start(bf16[512,384]{1,0:T(8,128)(2,1)} %get-tuple-element.78), channel_id=1, source_target_pairs={{0,7},{1,0},{2,1},{3,2},{4,3},{5,4},{6,5},{7,6},{8,15},{9,8},{10,9... | collective-permute-start | bytes 1179656 | tf_op jit(solution)/shard_map/ppermute | solution.py:72
  171.8 23.0 %collective-permute-start.15 = (bf16[512,256]{1,0:T(8,128)(2,1)}, bf16[512,256]{1,0:T(8,128)(2,1)S(1)}, u32[]{:S(2)}, u32[]{:S(2)}) collective-permute-start(bf16[512,256]{1,0:T(8,128)(2,1)} %get-tuple-element.56), channel_id=1, source_target_pairs={{0,2},{1,3},{2,4},{3,5},{4,6},{5,7},{6,0},{7,1},{8,10},{9,11},{10,... | collective-permute-start | bytes 786440 | tf_op jit(solution)/shard_map/ppermute | solution.py:72
  173.3 24.6 %collective-permute-start.16 = (bf16[512,256]{1,0:T(8,128)(2,1)}, bf16[512,256]{1,0:T(8,128)(2,1)S(1)}, u32[]{:S(2)}, u32[]{:S(2)}) collective-permute-start(bf16[512,256]{1,0:T(8,128)(2,1)} %get-tuple-element.57), channel_id=1, source_target_pairs={{0,3},{1,4},{2,5},{3,6},{4,7},{5,0},{6,1},{7,2},{8,11},{9,12},{10,... | collective-permute-start | bytes 786440 | tf_op jit(solution)/shard_map/ppermute | solution.py:72
  173.7 27.6 %collective-permute-start.17 = (bf16[512,256]{1,0:T(8,128)(2,1)}, bf16[512,256]{1,0:T(8,128)(2,1)S(1)}, u32[]{:S(2)}, u32[]{:S(2)}) collective-permute-start(bf16[512,256]{1,0:T(8,128)(2,1)} %get-tuple-element.58), channel_id=1, source_target_pairs={{0,4},{1,5},{2,6},{3,7},{4,0},{5,1},{6,2},{7,3},{8,12},{9,13},{10,... | collective-permute-start | bytes 786440 | tf_op jit(solution)/shard_map/ppermute | solution.py:72
  175.2 26.2 %collective-permute-start.18 = (bf16[512,256]{1,0:T(8,128)(2,1)}, bf16[512,256]{1,0:T(8,128)(2,1)}, u32[]{:S(2)}, u32[]{:S(2)}) collective-permute-start(bf16[512,256]{1,0:T(8,128)(2,1)} %get-tuple-element.59), channel_id=1, source_target_pairs={{0,5},{1,6},{2,7},{3,0},{4,1},{5,2},{6,3},{7,4},{8,13},{9,14},{10,... | collective-permute-start | bytes 786440 | tf_op jit(solution)/shard_map/ppermute | solution.py:72
  176.8 26.4 %collective-permute-start.19 = (bf16[512,256]{1,0:T(8,128)(2,1)}, bf16[512,256]{1,0:T(8,128)(2,1)}, u32[]{:S(2)}, u32[]{:S(2)}) collective-permute-start(bf16[512,256]{1,0:T(8,128)(2,1)} %get-tuple-element.60), channel_id=1, source_target_pairs={{0,6},{1,7},{2,0},{3,1},{4,2},{5,3},{6,4},{7,5},{8,14},{9,15},{10,... | collective-permute-start | bytes 786440 | tf_op jit(solution)/shard_map/ppermute | solution.py:72
  195.6 23.5 %collective-permute-start.10 = (bf16[576,256]{1,0:T(8,128)(2,1)}, bf16[576,256]{1,0:T(8,128)(2,1)S(1)}, u32[]{:S(2)}, u32[]{:S(2)}) collective-permute-start(bf16[576,256]{1,0:T(8,128)(2,1)} %get-tuple-element.49), channel_id=1, source_target_pairs={{0,4},{1,5},{2,6},{3,7},{4,0},{5,1},{6,2},{7,3},{8,12},{9,13},{10,... | collective-permute-start | bytes 884744 | tf_op jit(solution)/shard_map/ppermute | solution.py:72
  198.7 20.4 %collective-permute-start.11 = (bf16[576,256]{1,0:T(8,128)(2,1)}, bf16[576,256]{1,0:T(8,128)(2,1)S(1)}, u32[]{:S(2)}, u32[]{:S(2)}) collective-permute-start(bf16[576,256]{1,0:T(8,128)(2,1)} %get-tuple-element.50), channel_id=1, source_target_pairs={{0,5},{1,6},{2,7},{3,0},{4,1},{5,2},{6,3},{7,4},{8,13},{9,14},{10,... | collective-permute-start | bytes 884744 | tf_op jit(solution)/shard_map/ppermute | solution.py:72
  201.4 13.7 %collective-permute-start.20 = (bf16[512,256]{1,0:T(8,128)(2,1)}, bf16[512,256]{1,0:T(8,128)(2,1)S(1)}, u32[]{:S(2)}, u32[]{:S(2)}) collective-permute-start(bf16[512,256]{1,0:T(8,128)(2,1)} %get-tuple-element.61), channel_id=1, source_target_pairs={{0,7},{1,0},{2,1},{3,2},{4,3},{5,4},{6,5},{7,6},{8,15},{9,8},{10,9... | collective-permute-start | bytes 786440 | tf_op jit(solution)/shard_map/ppermute | solution.py:72
  201.4 15.9 %collective-permute-start.21 = (bf16[512,256]{1,0:T(8,128)(2,1)}, bf16[512,256]{1,0:T(8,128)(2,1)S(1)}, u32[]{:S(2)}, u32[]{:S(2)}) collective-permute-start(bf16[512,256]{1,0:T(8,128)(2,1)} %get-tuple-element.64), channel_id=1, source_target_pairs={{0,1},{1,2},{2,3},{3,4},{4,5},{5,6},{6,7},{7,0},{8,9},{9,10},{10,1... | collective-permute-start | bytes 786440 | tf_op jit(solution)/shard_map/ppermute | solution.py:72
  203.1 14.8 %collective-permute-start.22 = (bf16[512,256]{1,0:T(8,128)(2,1)}, bf16[512,256]{1,0:T(8,128)(2,1)S(1)}, u32[]{:S(2)}, u32[]{:S(2)}) collective-permute-start(bf16[512,256]{1,0:T(8,128)(2,1)} %get-tuple-element.65), channel_id=1, source_target_pairs={{0,2},{1,3},{2,4},{3,5},{4,6},{5,7},{6,0},{7,1},{8,10},{9,11},{10,... | collective-permute-start | bytes 786440 | tf_op jit(solution)/shard_map/ppermute | solution.py:72
  217.9 13.9 %collective-permute-start.7 = (bf16[576,256]{1,0:T(8,128)(2,1)}, bf16[576,256]{1,0:T(8,128)(2,1)}, u32[]{:S(2)}, u32[]{:S(2)}) collective-permute-start(bf16[576,256]{1,0:T(8,128)(2,1)} %get-tuple-element.46), channel_id=1, source_target_pairs={{0,1},{1,2},{2,3},{3,4},{4,5},{5,6},{6,7},{7,0},{8,9},{9,10},{10,1... | collective-permute-start | bytes 884744 | tf_op jit(solution)/shard_map/ppermute | solution.py:72
  219.1 13.9 %collective-permute-start.8 = (bf16[576,256]{1,0:T(8,128)(2,1)}, bf16[576,256]{1,0:T(8,128)(2,1)}, u32[]{:S(2)}, u32[]{:S(2)}) collective-permute-start(bf16[576,256]{1,0:T(8,128)(2,1)} %get-tuple-element.47), channel_id=1, source_target_pairs={{0,2},{1,3},{2,4},{3,5},{4,6},{5,7},{6,0},{7,1},{8,10},{9,11},{10,... | collective-permute-start | bytes 884744 | tf_op jit(solution)/shard_map/ppermute | solution.py:72
  219.1 19.1 %collective-permute-start.9 = (bf16[576,256]{1,0:T(8,128)(2,1)}, bf16[576,256]{1,0:T(8,128)(2,1)}, u32[]{:S(2)}, u32[]{:S(2)}) collective-permute-start(bf16[576,256]{1,0:T(8,128)(2,1)} %get-tuple-element.48), channel_id=1, source_target_pairs={{0,3},{1,4},{2,5},{3,6},{4,7},{5,0},{6,1},{7,2},{8,11},{9,12},{10,... | collective-permute-start | bytes 884744 | tf_op jit(solution)/shard_map/ppermute | solution.py:72
  225.0 35.4 %collective-permute-start.23 = (bf16[512,256]{1,0:T(8,128)(2,1)}, bf16[512,256]{1,0:T(8,128)(2,1)}, u32[]{:S(2)}, u32[]{:S(2)}) collective-permute-start(bf16[512,256]{1,0:T(8,128)(2,1)} %get-tuple-element.66), channel_id=1, source_target_pairs={{0,3},{1,4},{2,5},{3,6},{4,7},{5,0},{6,1},{7,2},{8,11},{9,12},{10,... | collective-permute-start | bytes 786440 | tf_op jit(solution)/shard_map/ppermute | solution.py:72
  230.3 30.2 %collective-permute-start.24 = (bf16[512,256]{1,0:T(8,128)(2,1)}, bf16[512,256]{1,0:T(8,128)(2,1)}, u32[]{:S(2)}, u32[]{:S(2)}) collective-permute-start(bf16[512,256]{1,0:T(8,128)(2,1)} %get-tuple-element.67), channel_id=1, source_target_pairs={{0,4},{1,5},{2,6},{3,7},{4,0},{5,1},{6,2},{7,3},{8,12},{9,13},{10,... | collective-permute-start | bytes 786440 | tf_op jit(solution)/shard_map/ppermute | solution.py:72
  231.8 28.7 %collective-permute-start.25 = (bf16[512,256]{1,0:T(8,128)(2,1)}, bf16[512,256]{1,0:T(8,128)(2,1)}, u32[]{:S(2)}, u32[]{:S(2)}) collective-permute-start(bf16[512,256]{1,0:T(8,128)(2,1)} %get-tuple-element.68), channel_id=1, source_target_pairs={{0,5},{1,6},{2,7},{3,0},{4,1},{5,2},{6,3},{7,4},{8,13},{9,14},{10,... | collective-permute-start | bytes 786440 | tf_op jit(solution)/shard_map/ppermute | solution.py:72
  233.0 27.5 %collective-permute-start.26 = (bf16[512,256]{1,0:T(8,128)(2,1)}, bf16[512,256]{1,0:T(8,128)(2,1)}, u32[]{:S(2)}, u32[]{:S(2)}) collective-permute-start(bf16[512,256]{1,0:T(8,128)(2,1)} %get-tuple-element.69), channel_id=1, source_target_pairs={{0,6},{1,7},{2,0},{3,1},{4,2},{5,3},{6,4},{7,5},{8,14},{9,15},{10,... | collective-permute-start | bytes 786440 | tf_op jit(solution)/shard_map/ppermute | solution.py:72
  238.2 22.3 %collective-permute-start.27 = (bf16[512,256]{1,0:T(8,128)(2,1)S(1)}, bf16[512,256]{1,0:T(8,128)(2,1)}, u32[]{:S(2)}, u32[]{:S(2)}) collective-permute-start(bf16[512,256]{1,0:T(8,128)(2,1)S(1)} %copy-done.14), channel_id=1, source_target_pairs={{0,7},{1,0},{2,1},{3,2},{4,3},{5,4},{6,5},{7,6},{8,15},{9,8},{10,9... | collective-permute-start | bytes 786440 | tf_op jit(solution)/shard_map/ppermute | solution.py:72
  (24 other events, 687.3 us)

commit v3 on v2

--- a/solution.py
+++ b/solution.py
@@ -76,11 +76,12 @@
 
 def broadcast_first(value, axis, index):
     size = lax.axis_size(axis)
-    hop = size // 2
+    hop, level = size // 2, 0
     while hop:
         got = lax.ppermute(value, axis, [(i, i + hop) for i in range(0, size, 2 * hop)])
         value = jnp.where(lax.rem(index, 2 * hop) == hop, got, value)
         hop //= 2
+        level += 1
     return value
 
 
@@ -216,22 +217,58 @@
     )(place, *own, *ext)
 
 
+def assemble_kernel(*refs):
+    part_refs, (o_ref, sems) = refs[:-2], refs[-2:]
+    shards, part = o_ref.shape[0], o_ref.shape[1] // len(part_refs)
+    copies = [
+        pltpu.make_async_copy(
+            ref.at[:shards], o_ref.at[:, o * part : (o + 1) * part, :], sems.at[o]
+        )
+        for o, ref in enumerate(part_refs)
+    ]
+    for copy in copies:
+        copy.start()
+    for copy in copies:
+        copy.wait()
+
+
+def assemble(parts, shards):
+    part = TILE // len(parts)
+    lanes = parts[0].shape[1]
+    return pl.pallas_call(
+        assemble_kernel,
+        in_specs=[pl.BlockSpec(memory_space=pl.ANY)] * len(parts),
+        out_specs=pl.BlockSpec(memory_space=pl.ANY),
+        out_shape=jax.ShapeDtypeStruct((shards, TILE, lanes), jnp.bfloat16),
+        scratch_shapes=[pltpu.SemaphoreType.DMA((len(parts),))],
+        cost_estimate=pl.CostEstimate(
+            flops=0, transcendentals=0, bytes_accessed=4 * shards * TILE * lanes
+        ),
+    )(*[p.reshape(-1, part, lanes) for p in parts])
+
+
 def random_kernel(index_ref, count_ref, *refs, groups):
-    part_refs = refs[: CAP * groups]
-    q_ref, m_ref, l_ref, a_ref, o_ref, kv_ref = refs[CAP * groups :]
+    early_refs, part_refs = refs[: CAP - 1], refs[CAP - 1 : CAP - 1 + groups]
+    q_ref, m_ref, l_ref, a_ref, o_ref, kv_ref, sems = refs[CAP - 1 + groups :]
     lanes = q_ref.shape[1]
     step = pl.program_id(0)
     per_step = q_ref.shape[0] // TILE
     part = TILE // groups
-    shards = part_refs[0].shape[0] // part
+    shards = kv_ref.shape[0] // CAP
 
     @pl.when(step == 0)
     def _():
-        for i, ref in enumerate(part_refs):
-            s, o = divmod(i, groups)
-            kv_ref[s * shards : (s + 1) * shards, o * part : (o + 1) * part, :] = ref[...].reshape(
-                shards, part, 2 * lanes
-            )
+        copies = []
+        for s, ref in enumerate(early_refs):
+            home = kv_ref.at[s * shards : (s + 1) * shards]
+            copies.append(pltpu.make_async_copy(ref, home, sems.at[s]))
+        for o, ref in enumerate(part_refs):
+            home = kv_ref.at[(CAP - 1) * shards :, o * part : (o + 1) * part, :]
+            copies.append(pltpu.make_async_copy(ref, home, sems.at[CAP - 1 + o]))
+        for copy in copies:
+            copy.start()
+        for copy in copies:
+            copy.wait()
 
     for i in range(per_step):
         t = step * per_step + i
@@ -241,11 +278,13 @@
         at = [index_ref[t * RANDOM + j] for j in range(RANDOM)]
         scores = []
         top = None
-        for j in range(RANDOM):
-            bias = jnp.where(j < count, 0.0, NEG).astype(jnp.float32)
-            s = score(q2, kv_ref[at[j], :, :lanes]) + bias
-            scores.append(s)
-            top = s if top is None else jnp.maximum(top, s)
+        for j in range(0, RANDOM, 2):
+            keys = jnp.concatenate([kv_ref[at[j], :, :lanes], kv_ref[at[j + 1], :, :lanes]], axis=0)
+            s = score(q2, keys)
+            for i, part in enumerate((s[:, :TILE], s[:, TILE:])):
+                part = part + jnp.where(j + i < count, 0.0, NEG).astype(jnp.float32)
+                scores.append(part)
+                top = part if top is None else jnp.maximum(top, part)
         m_old = m_ref[rows, :]
         m_old = jnp.concatenate([m_old[:, :1], m_old[:, HEAD_DIM : HEAD_DIM + 1]], axis=0)
         m_new = jnp.maximum(jnp.max(top, axis=1, keepdims=True), m_old)
@@ -266,31 +305,34 @@
         o_ref[rows, :] = (numerator / denominator).astype(jnp.bfloat16)
 
 
-def random_attention(index, count, q, fetched, m, l, a, part_rows, per_step=2):
+def random_attention(index, count, q, early, late, m, l, a, per_step=8):
     rows, lanes = q.shape
-    groups = len(fetched) // CAP
+    groups = len(late)
+    shards = early[0].shape[0]
+    part = TILE // groups
+    late = [f.reshape(-1, part, 2 * lanes) for f in late]
     block = pl.BlockSpec((per_step * TILE, lanes), lambda i, s, c: (i, 0))
-    fixed = pl.BlockSpec((part_rows, 2 * lanes), lambda i, s, c: (0, 0))
     keys = RANDOM * TILE
     return pl.pallas_call(
         functools.partial(random_kernel, groups=groups),
         grid_spec=pltpu.PrefetchScalarGridSpec(
             num_scalar_prefetch=2,
             grid=(rows // (per_step * TILE),),
-            in_specs=[fixed] * len(fetched) + [block] * 4,
+            in_specs=[pl.BlockSpec(memory_space=pl.ANY)] * (len(early) + groups) + [block] * 4,
             out_specs=block,
             scratch_shapes=[
-                pltpu.VMEM((CAP * part_rows * groups // TILE, TILE, 2 * lanes), jnp.bfloat16)
+                pltpu.VMEM((CAP * shards, TILE, 2 * lanes), jnp.bfloat16),
+                pltpu.SemaphoreType.DMA((len(early) + groups,)),
             ],
         ),
         out_shape=jax.ShapeDtypeStruct((rows, lanes), jnp.bfloat16),
         cost_estimate=pl.CostEstimate(
             flops=8 * rows * keys * lanes,
             transcendentals=2 * rows * keys,
-            bytes_accessed=rows * lanes * 16 + CAP * part_rows * groups * lanes * 4,
+            bytes_accessed=rows * lanes * 16 + CAP * shards * TILE * lanes * 4,
         ),
         name="random_attention",
-    )(index, count, *fetched, q, m, l, a)
+    )(index, count, *early, *late, q, m, l, a)
 
 
 def request_tables(random_tiles, random_count, shard, ctx_count, tiles_here):
@@ -348,14 +390,17 @@
     fetched = []
     for slot in range(CAP):
         got = lax.all_to_all(outgoing[slot], "ctx", split_axis=0, concat_axis=0, tiled=True)
-        got = [got.reshape(ctx_count * part, width)] + ([ext] if slot == 0 else [])
+        got = [got.reshape(ctx_count * part, width)] + ([ext] if slot == 1 else [])
         got = project(where, got, [w_key, w_value], groups)
-        fetched += exchange(got, "head")
+        fetched.append(exchange(got, "head"))
 
     place = jnp.stack([shard, jnp.int32(tiles_here * ctx_count), here])
-    m, l, a, q = local_attention(place, own, fetched[:groups], ext.shape[0])
+    m, l, a, q = local_attention(place, own, fetched[1], ext.shape[0])
+    early = []
+    for slot in range(CAP - 1):
+        early.append(assemble(fetched[slot], ctx_count))
     my_count = lax.dynamic_slice_in_dim(random_count, shard * tiles_here, tiles_here, 0)
-    attended = random_attention(read, my_count, q, fetched, m, l, a, ctx_count * part)
+    attended = random_attention(read, my_count, q, early, fetched[CAP - 1], m, l, a)
     attended = attended.reshape(groups, rows, -1)
     returned = lax.all_to_all(attended, "head", split_axis=0, concat_axis=0, tiled=True)
     out = lax.dot_general(

time: 318 us -> 467 us (1.47)
  Pallas kernels: 94.9 us -> 221 us
  starting transfers between devices: 71.5 us -> 87.8 us
  blocking collectives: 54.9 us -> 60 us
    pallas_call x0 -> x2, Pallas kernels: none -> 129 us  [assemble(): pl.pallas_call(assemble_kernel, in_specs=[pl.BlockSpec(memory_space=pl.AN...]
    ppermute x28, starting transfers between devices: 33.9 us -> 50.3 us  [exchange(): lax.ppermute(pieces[o], axis, [(i, (i + o) % size) for i in range(size)])]
    all_to_all x1, blocking collectives: 18.4 us -> 23.5 us  [body(): lax.all_to_all(attended, 'head', split_axis=0, concat_axis=0, tiled=True)]
  transfers between devices with their start and end apart: 38 -> 38, of which waited for: 12 -> 11; matrix products, arithmetic and copies ran while one was open for 3% -> 2% of each run, Pallas kernels for 18% -> 40%
where the time goes in v3:
time: 467 us; the launch traced here: 466 us
  Pallas kernels  221 us (47%)
  starting transfers between devices  87.8 us (19%)
  waiting for transfers between devices  79.1 us (17%)
  blocking collectives  60 us (13%)
  local copies, waits for them, and re-layouts  10.2 us (2%)
  other arithmetic  5.38 us (1%)
    pallas_call x2, Pallas kernels, assemble(): pl.pallas_call(assemble_kernel, in_specs=[pl.BlockSpec(memory_space=pl.AN...  129 us
    ppermute x28, waiting for transfers between devices, exchange(): lax.ppermute(pieces[o], axis, [(i, (i + o) % size) for i in range(size)])  53.9 us
    ppermute x28, starting transfers between devices, exchange(): lax.ppermute(pieces[o], axis, [(i, (i + o) % size) for i in range(size)])  50.3 us
    pallas_call x4, Pallas kernels, project(): pl.pallas_call(functools.partial(project_kernel, sources=len(xs), weights...  37.2 us
    all_to_all x1, blocking collectives, body(): lax.all_to_all(outgoing[slot], 'ctx', split_axis=0, concat_axis=0, tiled=...  36.5 us
    pallas_call x1, Pallas kernels, random_attention(): pl.pallas_call(functools.partial(random_kernel, groups=groups), grid_spec...  31.6 us
    all_to_all x1, blocking collectives, body(): lax.all_to_all(attended, 'head', split_axis=0, concat_axis=0, tiled=True)  23.5 us
    pallas_call x1, Pallas kernels, local_attention(): pl.pallas_call(functools.partial(local_kernel, groups=groups), grid_spec=...  18.7 us
  transfers between devices with their start and end apart: 38, of which 11 were waited for; matrix products, arithmetic and copies ran while one was open for 2% of the time, Pallas kernels for 40%

profile of v3, /device:TPU:1, one launch (start us, length us, event | category | flops | bytes accessed | tf_op | source)
XLA Modules:
  0.0 465.8 jit_solution(1573855801376602894)
XLA Ops:
  2.5 6.7 %all-to-all-start = ((bf16[8,4,16,1024]{3,2,1,0:T(8,128)(2,1)}), bf16[8,4,16,1024]{3,2,1,0:T(8,128)(2,1)S(1)}, u32[]{:S(2)}, u32[]{:S(2)}) async-start(bf16[8,4,16,1024]{3,2,1,0:T(8,128)(2,1)} %bitcast.47), calls=%async_computation | async-start | bytes 2097152 | tf_op jit(solution)/shard_map/all_to_all | solution.py:374
  13.7 10.5 %all-to-all-done = bf16[8,4,16,1024]{3,2,1,0:T(8,128)(2,1)S(1)} async-done(((bf16[8,4,16,1024]{3,2,1,0:T(8,128)(2,1)}), bf16[8,4,16,1024]{3,2,1,0:T(8,128)(2,1)S(1)}, u32[]{:S(2)}, u32[]{:S(2)}) %all-to-all-start) | async-done | bytes 1048608 | tf_op jit(solution)/shard_map/all_to_all | solution.py:374
  25.1 3.9 pick_tiles.1
  29.0 36.5 %all_to_all.25 = bf16[32,16,1024]{2,1,0:T(8,128)(2,1)} all-to-all(bf16[32,16,1024]{2,1,0:T(8,128)(2,1)} %get-tuple-element.44), channel_id=1, replica_groups=mesh['ctx'=32,'head'=8] {'ctx'}, dimensions={0} | all-to-all | bytes 2097152 | tf_op jit(solution)/shard_map/all_to_all | solution.py:392
  65.4 6.3 %all-to-all-start.3 = ((bf16[32,16,1024]{2,1,0:T(8,128)(2,1)}), bf16[32,16,1024]{2,1,0:T(8,128)(2,1)S(1)}, u32[]{:S(2)}, u32[]{:S(2)}) async-start(bf16[32,16,1024]{2,1,0:T(8,128)(2,1)} %get-tuple-element.62), calls=%async_computation.3 | async-start | bytes 2097152 | tf_op jit(solution)/shard_map/all_to_all | solution.py:392
  72.6 7.0 %collective-permute-start.9 = (bf16[2,16,1024]{2,1,0:T(8,128)(2,1)S(1)}, bf16[2,16,1024]{2,1,0:T(8,128)(2,1)S(1)}, u32[]{:S(2)}, u32[]{:S(2)}) collective-permute-start(bf16[2,16,1024]{2,1,0:T(8,128)(2,1)S(1)} %slice.14), channel_id=1, source_target_pairs={{0,128},{1,129},{2,130},{3,131},{4,132},{5,133},{6,134},{7,135}} | collective-permute-start | bytes 196616 | tf_op jit(solution)/shard_map/ppermute | solution.py:81
  79.6 10.4 %collective-permute-done.9 = bf16[2,16,1024]{2,1,0:T(8,128)(2,1)S(1)} collective-permute-done((bf16[2,16,1024]{2,1,0:T(8,128)(2,1)S(1)}, bf16[2,16,1024]{2,1,0:T(8,128)(2,1)S(1)}, u32[]{:S(2)}, u32[]{:S(2)}) %collective-permute-start.9) | collective-permute-done | bytes 65568 | tf_op jit(solution)/shard_map/ppermute | solution.py:81
  92.2 4.3 all-to-all-done.3
  96.5 7.4 %all-to-all-start.2 = ((bf16[32,16,1024]{2,1,0:T(8,128)(2,1)}), bf16[32,16,1024]{2,1,0:T(8,128)(2,1)}, u32[]{:S(2)}, u32[]{:S(2)}) async-start(bf16[32,16,1024]{2,1,0:T(8,128)(2,1)} %get-tuple-element.53), calls=%async_computation.2 | async-start | bytes 2097152 | tf_op jit(solution)/shard_map/all_to_all | solution.py:392
  104.0 3.1 collective-permute-start.11
  107.0 10.9 %shard_map.78 = (bf16[512,384]{1,0:T(8,128)(2,1)}, bf16[512,384]{1,0:T(8,128)(2,1)}, bf16[512,384]{1,0:T(8,128)(2,1)}, bf16[512,384]{1,0:T(8,128)(2,1)}, bf16[51...) custom-call(s32[1]{0:T(128)} %bitcast.here_ref, ...), custom_call_target="tpu_custom_call" | custom-call | flops 3221225472 | bytes 10485760 | tf_op jit(solution)/shard_map/pallas_call | solution.py:47
  118.0 4.0 collective-permute-start.28
  132.4 10.4 %collective-permute-done.29.refs_2_ = bf16[512,384]{1,0:T(8,128)(2,1)S(1)} collective-permute-done((bf16[512,384]{1,0:T(8,128)(2,1)}, bf16[512,384]{1,0:T(8,128)(2,1)S(1)}, u32[]{:S(2)}, u32[]{:S(2)}) %collective-permute-start.29) | collective-permute-done | bytes 393248 | tf_op jit(solution)/shard_map/ppermute | solution.py:72
  142.7 16.6 %collective-permute-done.30.refs_3_ = bf16[512,384]{1,0:T(8,128)(2,1)} collective-permute-done((bf16[512,384]{1,0:T(8,128)(2,1)}, bf16[512,384]{1,0:T(8,128)(2,1)}, u32[]{:S(2)}, u32[]{:S(2)}) %collective-permute-start.30) | collective-permute-done | bytes 393248 | tf_op jit(solution)/shard_map/ppermute | solution.py:72
  160.9 8.7 %shard_map.73 = (bf16[512,256]{1,0:T(8,128)(2,1)}, bf16[512,256]{1,0:T(8,128)(2,1)}, bf16[512,256]{1,0:T(8,128)(2,1)}, bf16[512,256]{1,0:T(8,128)(2,1)}, bf16[51...) custom-call(s32[1]{0:T(128)} %bitcast.here_ref, ...), custom_call_target="tpu_custom_call" | custom-call | flops 2147483648 | bytes 7340032 | tf_op jit(solution)/shard_map/pallas_call | solution.py:47
  170.4 4.1 collective-permute-start.4
  176.3 2.8 collective-permute-done.3
  180.2 8.7 %shard_map.77 = (bf16[512,256]{1,0:T(8,128)(2,1)}, bf16[512,256]{1,0:T(8,128)(2,1)}, bf16[512,256]{1,0:T(8,128)(2,1)}, bf16[512,256]{1,0:T(8,128)(2,1)}, bf16[51...) custom-call(s32[1]{0:T(128)} %bitcast.here_ref, ...), custom_call_target="tpu_custom_call" | custom-call | flops 2147483648 | bytes 7340032 | tf_op jit(solution)/shard_map/pallas_call | solution.py:47
  188.8 8.9 %shard_map.75 = (bf16[576,256]{1,0:T(8,128)(2,1)}, bf16[576,256]{1,0:T(8,128)(2,1)}, bf16[576,256]{1,0:T(8,128)(2,1)}, bf16[576,256]{1,0:T(8,128)(2,1)}, bf16[57...) custom-call(s32[1]{0:T(128)} %bitcast.here_ref, ...), custom_call_target="tpu_custom_call" | custom-call | flops 2415919104 | bytes 7733248 | tf_op jit(solution)/shard_map/pallas_call | solution.py:47
  201.3 4.3 collective-permute-start.15
  206.6 12.6 %collective-permute-done.2 = bf16[512,256]{1,0:T(8,128)(2,1)S(1)} collective-permute-done((bf16[512,256]{1,0:T(8,128)(2,1)}, bf16[512,256]{1,0:T(8,128)(2,1)S(1)}, u32[]{:S(2)}, u32[]{:S(2)}) %collective-permute-start.2) | collective-permute-done | bytes 262176 | tf_op jit(solution)/shard_map/ppermute | solution.py:72
  219.3 3.0 collective-permute-start.16
  222.3 5.9 %collective-permute-start.17 = (bf16[576,256]{1,0:T(8,128)(2,1)}, bf16[576,256]{1,0:T(8,128)(2,1)S(1)}, u32[]{:S(2)}, u32[]{:S(2)}) collective-permute-start(bf16[576,256]{1,0:T(8,128)(2,1)} %get-tuple-element.58), channel_id=1, source_target_pairs={{0,4},{1,5},{2,6},{3,7},{4,0},{5,1},{6,2},{7,3},{8,12},{9,13},{10,... | collective-permute-start | bytes 884744 | tf_op jit(solution)/shard_map/ppermute | solution.py:72
  230.1 4.8 %collective-permute-start.19 = (bf16[576,256]{1,0:T(8,128)(2,1)}, bf16[576,256]{1,0:T(8,128)(2,1)}, u32[]{:S(2)}, u32[]{:S(2)}) collective-permute-start(bf16[576,256]{1,0:T(8,128)(2,1)} %get-tuple-element.60), channel_id=1, source_target_pairs={{0,6},{1,7},{2,0},{3,1},{4,2},{5,3},{6,4},{7,5},{8,14},{9,15},{10,... | collective-permute-start | bytes 884744 | tf_op jit(solution)/shard_map/ppermute | solution.py:72
  235.0 8.7 %collective-permute-start.20 = (bf16[576,256]{1,0:T(8,128)(2,1)}, bf16[576,256]{1,0:T(8,128)(2,1)}, u32[]{:S(2)}, u32[]{:S(2)}) collective-permute-start(bf16[576,256]{1,0:T(8,128)(2,1)} %get-tuple-element.61), channel_id=1, source_target_pairs={{0,7},{1,0},{2,1},{3,2},{4,3},{5,4},{6,5},{7,6},{8,15},{9,8},{10,9... | collective-permute-start | bytes 884744 | tf_op jit(solution)/shard_map/ppermute | solution.py:72
  247.9 3.0 collective-permute-start.25
  251.0 8.0 %collective-permute-done.20.refs_15_ = bf16[576,256]{1,0:T(8,128)(2,1)} collective-permute-done((bf16[576,256]{1,0:T(8,128)(2,1)}, bf16[576,256]{1,0:T(8,128)(2,1)}, u32[]{:S(2)}, u32[]{:S(2)}) %collective-permute-start.20) | collective-permute-done | bytes 294944 | tf_op jit(solution)/shard_map/ppermute | solution.py:72
  260.3 64.7 %shard_map.74.refs_0_ = bf16[32,128,256]{2,1,0:T(8,128)(2,1)} custom-call(bf16[32,16,256]{2,1,0:T(8,128)(2,1)} %bitcast.57, bf16[32,16,256]{2,1,0:T(8,128)(2,1)} %bitcast.62, bf16[32,16,256]{2,1,0:T(8,128)(2,1)} %bitcast.8.refs_2_, bf16[32,16,256]{2,1,0:T(8,128)(2,1)} %bitcast.63, bf16[32,16,256]{2,1,0:T(8,128)(2,1)} %bitcast.58, ...), custom_call_target="tpu_custom_call" | custom-call | bytes 4194304 | tf_op jit(solution)/shard_map/pallas_call | solution.py:238
  325.0 64.7 %shard_map.76.refs_1_ = bf16[32,128,256]{2,1,0:T(8,128)(2,1)} custom-call(bf16[36,16,256]{2,1,0:T(8,128)(2,1)} %bitcast.52, bf16[36,16,256]{2,1,0:T(8,128)(2,1)} %bitcast.53, bf16[36,16,256]{2,1,0:T(8,128)(2,1)} %bitcast.54, bf16[36,16,256]{2,1,0:T(8,128)(2,1)} %bitcast.55, bf16[36,16,256]{2,1,0:T(8,128)(2,1)} %bitcast.56, ...), custom_call_target="tpu_custom_call" | custom-call | bytes 4194304 | tf_op jit(solution)/shard_map/pallas_call | solution.py:238
  389.7 18.7 %local_attention.1 = (f32[4096,128]{1,0:T(8,128)}, f32[4096,128]{1,0:T(8,128)}, f32[4096,128]{1,0:T(8,128)}, bf16[4096,128]{1,0:T(8,128)(2,1)}) custom-call(s32[3]{0:T(128)} %pad_add_fusion.place_ref, bf16[512,384]{1,0:T(8,128)(2,1)} %get-tuple-element.71.refs_0_, bf16[512,384]{1,0:T(8,128)(2,1)} %copy-done.15, bf16[512,384]{1,0:T(8,128)(2,1)} %copy-done.16, ...), custom_call_target="tpu_custom_call" | custom-call | flops 2684354560 | bytes 10485760 | tf_op jit(solution)/shard_map/local_attention/pallas_call | solution.py:197
  408.5 31.6 %random_attention.1 = bf16[4096,128]{1,0:T(8,128)(2,1)} custom-call(s32[384]{0:T(512)} %add_select_fusion.1.index_ref, s32[32]{0:T(128)} %dynamic_slice.8.count_ref, bf16[32,128,256]{2,1,0:T(8,128)(2,1)} %shard_map.74.refs_0_, bf16[32,128,256]{2,1,0:T(8,128)(2,1)} %shard_map.76.refs_1_, bf16[32,16,256]{2,1,0:T(8,128)(2,1)} %bitcast.68, ...), custom_call_target="tpu_custom_call" | custom-call | flops 6442450944 | bytes 14680064 | tf_op jit(solution)/shard_map/random_attention/pallas_call | solution.py:316
  440.0 23.5 %all_to_all.26 = bf16[8,512,128]{2,1,0:T(8,128)(2,1)S(1)} all-to-all(bf16[8,512,128]{2,1,0:T(8,128)(2,1)} %bitcast.51), channel_id=1, replica_groups=mesh['ctx'=32,'head'=8] {'head'}, dimensions={0} | all-to-all | bytes 2097152 | tf_op jit(solution)/shard_map/all_to_all | solution.py:405
  (119 shorter events, 40.7 us)
Async XLA Ops:
  2.5 21.7 %all-to-all-start = ((bf16[8,4,16,1024]{3,2,1,0:T(8,128)(2,1)}), bf16[8,4,16,1024]{3,2,1,0:T(8,128)(2,1)S(1)}, u32[]{:S(2)}, u32[]{:S(2)}) async-start(bf16[8,4,16,1024]{3,2,1,0:T(8,128)(2,1)} %bitcast.47), calls=%async_computation | async-start | bytes 2097152 | tf_op jit(solution)/shard_map/all_to_all | solution.py:374
  65.4 31.1 %all-to-all-start.3 = ((bf16[32,16,1024]{2,1,0:T(8,128)(2,1)}), bf16[32,16,1024]{2,1,0:T(8,128)(2,1)S(1)}, u32[]{:S(2)}, u32[]{:S(2)}) async-start(bf16[32,16,1024]{2,1,0:T(8,128)(2,1)} %get-tuple-element.62), calls=%async_computation.3 | async-start | bytes 2097152 | tf_op jit(solution)/shard_map/all_to_all | solution.py:392
  72.6 17.5 %collective-permute-start.9 = (bf16[2,16,1024]{2,1,0:T(8,128)(2,1)S(1)}, bf16[2,16,1024]{2,1,0:T(8,128)(2,1)S(1)}, u32[]{:S(2)}, u32[]{:S(2)}) collective-permute-start(bf16[2,16,1024]{2,1,0:T(8,128)(2,1)S(1)} %slice.14), channel_id=1, source_target_pairs={{0,128},{1,129},{2,130},{3,131},{4,132},{5,133},{6,134},{7,135}} | collective-permute-start | bytes 196616 | tf_op jit(solution)/shard_map/ppermute | solution.py:81
  96.5 92.3 %all-to-all-start.2 = ((bf16[32,16,1024]{2,1,0:T(8,128)(2,1)}), bf16[32,16,1024]{2,1,0:T(8,128)(2,1)}, u32[]{:S(2)}, u32[]{:S(2)}) async-start(bf16[32,16,1024]{2,1,0:T(8,128)(2,1)} %get-tuple-element.53), calls=%async_computation.2 | async-start | bytes 2097152 | tf_op jit(solution)/shard_map/all_to_all | solution.py:392
  104.0 20.2 %collective-permute-start.11 = (bf16[2,16,1024]{2,1,0:T(8,128)(2,1)S(1)}, bf16[2,16,1024]{2,1,0:T(8,128)(2,1)S(1)}, u32[]{:S(2)}, u32[]{:S(2)}) collective-permute-start(bf16[2,16,1024]{2,1,0:T(8,128)(2,1)S(1)} %broadcast_select_fusion.1), channel_id=1, source_target_pairs={{0,32},{64,96},{128,160},{192,224},{1,33},{65,97},{129,161},{193,2... | collective-permute-start | bytes 196616 | tf_op jit(solution)/shard_map/ppermute | solution.py:81
  122.0 20.7 %collective-permute-start.29 = (bf16[512,384]{1,0:T(8,128)(2,1)}, bf16[512,384]{1,0:T(8,128)(2,1)S(1)}, u32[]{:S(2)}, u32[]{:S(2)}) collective-permute-start(bf16[512,384]{1,0:T(8,128)(2,1)} %get-tuple-element.73), channel_id=1, source_target_pairs={{0,2},{1,3},{2,4},{3,5},{4,6},{5,7},{6,0},{7,1},{8,10},{9,11},{10,... | collective-permute-start | bytes 1179656 | tf_op jit(solution)/shard_map/ppermute | solution.py:72
  122.1 37.2 %collective-permute-start.30 = (bf16[512,384]{1,0:T(8,128)(2,1)}, bf16[512,384]{1,0:T(8,128)(2,1)}, u32[]{:S(2)}, u32[]{:S(2)}) collective-permute-start(bf16[512,384]{1,0:T(8,128)(2,1)} %get-tuple-element.74), channel_id=1, source_target_pairs={{0,3},{1,4},{2,5},{3,6},{4,7},{5,0},{6,1},{7,2},{8,11},{9,12},{10,... | collective-permute-start | bytes 1179656 | tf_op jit(solution)/shard_map/ppermute | solution.py:72
  126.9 32.5 %collective-permute-start.7 = (bf16[1,16,1024]{2,1,0:T(8,128)(2,1)S(1)}, bf16[1,16,1024]{2,1,0:T(8,128)(2,1)S(1)}, u32[]{:S(2)}, u32[]{:S(2)}) collective-permute-start(bf16[1,16,1024]{2,1,0:T(8,128)(2,1)S(1)} %get-tuple-element.83), channel_id=1, source_target_pairs={{0,8},{8,16},{16,24},{24,32},{32,40},{40,48},{48,56},{56,64},{64,7... | collective-permute-start | bytes 98312 | tf_op jit(solution)/shard_map/ppermute | solution.py:385
  128.2 31.5 %collective-permute-start.8 = (bf16[1,16,1024]{2,1,0:T(8,128)(2,1)S(1)}, bf16[1,16,1024]{2,1,0:T(8,128)(2,1)S(1)}, u32[]{:S(2)}, u32[]{:S(2)}) collective-permute-start(bf16[1,16,1024]{2,1,0:T(8,128)(2,1)S(1)} %get-tuple-element.84), channel_id=1, source_target_pairs={{8,0},{16,8},{24,16},{32,24},{40,32},{48,40},{56,48},{64,56},{72,6... | collective-permute-start | bytes 98312 | tf_op jit(solution)/shard_map/ppermute | solution.py:386
  130.6 39.8 %collective-permute-start.31 = (bf16[512,384]{1,0:T(8,128)(2,1)}, bf16[512,384]{1,0:T(8,128)(2,1)}, u32[]{:S(2)}, u32[]{:S(2)}) collective-permute-start(bf16[512,384]{1,0:T(8,128)(2,1)} %get-tuple-element.75), channel_id=1, source_target_pairs={{0,4},{1,5},{2,6},{3,7},{4,0},{5,1},{6,2},{7,3},{8,12},{9,13},{10,... | collective-permute-start | bytes 1179656 | tf_op jit(solution)/shard_map/ppermute | solution.py:72
  142.7 31.8 %collective-permute-start.32 = (bf16[512,384]{1,0:T(8,128)(2,1)}, bf16[512,384]{1,0:T(8,128)(2,1)}, u32[]{:S(2)}, u32[]{:S(2)}) collective-permute-start(bf16[512,384]{1,0:T(8,128)(2,1)} %get-tuple-element.76), channel_id=1, source_target_pairs={{0,5},{1,6},{2,7},{3,0},{4,1},{5,2},{6,3},{7,4},{8,13},{9,14},{10,... | collective-permute-start | bytes 1179656 | tf_op jit(solution)/shard_map/ppermute | solution.py:72
  159.4 15.2 %collective-permute-start.33 = (bf16[512,384]{1,0:T(8,128)(2,1)}, bf16[512,384]{1,0:T(8,128)(2,1)}, u32[]{:S(2)}, u32[]{:S(2)}) collective-permute-start(bf16[512,384]{1,0:T(8,128)(2,1)} %get-tuple-element.77), channel_id=1, source_target_pairs={{0,6},{1,7},{2,0},{3,1},{4,2},{5,3},{6,4},{7,5},{8,14},{9,15},{10,... | collective-permute-start | bytes 1179656 | tf_op jit(solution)/shard_map/ppermute | solution.py:72
  159.4 15.7 %collective-permute-start.34 = (bf16[512,384]{1,0:T(8,128)(2,1)}, bf16[512,384]{1,0:T(8,128)(2,1)}, u32[]{:S(2)}, u32[]{:S(2)}) collective-permute-start(bf16[512,384]{1,0:T(8,128)(2,1)} %get-tuple-element.78), channel_id=1, source_target_pairs={{0,7},{1,0},{2,1},{3,2},{4,3},{5,4},{6,5},{7,6},{8,15},{9,8},{10,9... | collective-permute-start | bytes 1179656 | tf_op jit(solution)/shard_map/ppermute | solution.py:72
  170.4 27.4 %collective-permute-start.4 = (bf16[512,256]{1,0:T(8,128)(2,1)}, bf16[512,256]{1,0:T(8,128)(2,1)S(1)}, u32[]{:S(2)}, u32[]{:S(2)}) collective-permute-start(bf16[512,256]{1,0:T(8,128)(2,1)} %get-tuple-element.50), channel_id=1, source_target_pairs={{0,5},{1,6},{2,7},{3,0},{4,1},{5,2},{6,3},{7,4},{8,13},{9,14},{10,... | collective-permute-start | bytes 786440 | tf_op jit(solution)/shard_map/ppermute | solution.py:72
  174.5 26.0 %collective-permute-start.5 = (bf16[512,256]{1,0:T(8,128)(2,1)}, bf16[512,256]{1,0:T(8,128)(2,1)S(1)}, u32[]{:S(2)}, u32[]{:S(2)}) collective-permute-start(bf16[512,256]{1,0:T(8,128)(2,1)} %get-tuple-element.51), channel_id=1, source_target_pairs={{0,6},{1,7},{2,0},{3,1},{4,2},{5,3},{6,4},{7,5},{8,14},{9,15},{10,... | collective-permute-start | bytes 786440 | tf_op jit(solution)/shard_map/ppermute | solution.py:72
  174.6 31.0 %collective-permute-start.6 = (bf16[512,256]{1,0:T(8,128)(2,1)}, bf16[512,256]{1,0:T(8,128)(2,1)S(1)}, u32[]{:S(2)}, u32[]{:S(2)}) collective-permute-start(bf16[512,256]{1,0:T(8,128)(2,1)} %get-tuple-element.52), channel_id=1, source_target_pairs={{0,7},{1,0},{2,1},{3,2},{4,3},{5,4},{6,5},{7,6},{8,15},{9,8},{10,9... | collective-permute-start | bytes 786440 | tf_op jit(solution)/shard_map/ppermute | solution.py:72
  175.0 31.2 %collective-permute-start = (bf16[512,256]{1,0:T(8,128)(2,1)}, bf16[512,256]{1,0:T(8,128)(2,1)S(1)}, u32[]{:S(2)}, u32[]{:S(2)}) collective-permute-start(bf16[512,256]{1,0:T(8,128)(2,1)} %get-tuple-element.46), channel_id=1, source_target_pairs={{0,1},{1,2},{2,3},{3,4},{4,5},{5,6},{6,7},{7,0},{8,9},{9,10},{10,1... | collective-permute-start | bytes 786440 | tf_op jit(solution)/shard_map/ppermute | solution.py:72
  179.2 27.1 %collective-permute-start.1 = (bf16[512,256]{1,0:T(8,128)(2,1)}, bf16[512,256]{1,0:T(8,128)(2,1)}, u32[]{:S(2)}, u32[]{:S(2)}) collective-permute-start(bf16[512,256]{1,0:T(8,128)(2,1)} %get-tuple-element.47), channel_id=1, source_target_pairs={{0,2},{1,3},{2,4},{3,5},{4,6},{5,7},{6,0},{7,1},{8,10},{9,11},{10,... | collective-permute-start | bytes 786440 | tf_op jit(solution)/shard_map/ppermute | solution.py:72
  198.5 31.6 %collective-permute-start.14 = (bf16[576,256]{1,0:T(8,128)(2,1)}, bf16[576,256]{1,0:T(8,128)(2,1)S(1)}, u32[]{:S(2)}, u32[]{:S(2)}) collective-permute-start(bf16[576,256]{1,0:T(8,128)(2,1)} %get-tuple-element.55), channel_id=1, source_target_pairs={{0,1},{1,2},{2,3},{3,4},{4,5},{5,6},{6,7},{7,0},{8,9},{9,10},{10,1... | collective-permute-start | bytes 884744 | tf_op jit(solution)/shard_map/ppermute | solution.py:72
  201.3 33.7 %collective-permute-start.15 = (bf16[576,256]{1,0:T(8,128)(2,1)}, bf16[576,256]{1,0:T(8,128)(2,1)S(1)}, u32[]{:S(2)}, u32[]{:S(2)}) collective-permute-start(bf16[576,256]{1,0:T(8,128)(2,1)} %get-tuple-element.56), channel_id=1, source_target_pairs={{0,2},{1,3},{2,4},{3,5},{4,6},{5,7},{6,0},{7,1},{8,10},{9,11},{10,... | collective-permute-start | bytes 884744 | tf_op jit(solution)/shard_map/ppermute | solution.py:72
  206.2 16.1 %collective-permute-start.21 = (bf16[512,256]{1,0:T(8,128)(2,1)}, bf16[512,256]{1,0:T(8,128)(2,1)S(1)}, u32[]{:S(2)}, u32[]{:S(2)}) collective-permute-start(bf16[512,256]{1,0:T(8,128)(2,1)} %get-tuple-element.64), channel_id=1, source_target_pairs={{0,1},{1,2},{2,3},{3,4},{4,5},{5,6},{6,7},{7,0},{8,9},{9,10},{10,1... | collective-permute-start | bytes 786440 | tf_op jit(solution)/shard_map/ppermute | solution.py:72
  206.2 23.8 %collective-permute-start.22 = (bf16[512,256]{1,0:T(8,128)(2,1)}, bf16[512,256]{1,0:T(8,128)(2,1)S(1)}, u32[]{:S(2)}, u32[]{:S(2)}) collective-permute-start(bf16[512,256]{1,0:T(8,128)(2,1)} %get-tuple-element.65), channel_id=1, source_target_pairs={{0,2},{1,3},{2,4},{3,5},{4,6},{5,7},{6,0},{7,1},{8,10},{9,11},{10,... | collective-permute-start | bytes 786440 | tf_op jit(solution)/shard_map/ppermute | solution.py:72
  219.3 25.7 %collective-permute-start.16 = (bf16[576,256]{1,0:T(8,128)(2,1)}, bf16[576,256]{1,0:T(8,128)(2,1)S(1)}, u32[]{:S(2)}, u32[]{:S(2)}) collective-permute-start(bf16[576,256]{1,0:T(8,128)(2,1)} %get-tuple-element.57), channel_id=1, source_target_pairs={{0,3},{1,4},{2,5},{3,6},{4,7},{5,0},{6,1},{7,2},{8,11},{9,12},{10,... | collective-permute-start | bytes 884744 | tf_op jit(solution)/shard_map/ppermute | solution.py:72
  222.3 23.2 %collective-permute-start.17 = (bf16[576,256]{1,0:T(8,128)(2,1)}, bf16[576,256]{1,0:T(8,128)(2,1)S(1)}, u32[]{:S(2)}, u32[]{:S(2)}) collective-permute-start(bf16[576,256]{1,0:T(8,128)(2,1)} %get-tuple-element.58), channel_id=1, source_target_pairs={{0,4},{1,5},{2,6},{3,7},{4,0},{5,1},{6,2},{7,3},{8,12},{9,13},{10,... | collective-permute-start | bytes 884744 | tf_op jit(solution)/shard_map/ppermute | solution.py:72
  230.1 17.9 %collective-permute-start.18 = (bf16[576,256]{1,0:T(8,128)(2,1)}, bf16[576,256]{1,0:T(8,128)(2,1)}, u32[]{:S(2)}, u32[]{:S(2)}) collective-permute-start(bf16[576,256]{1,0:T(8,128)(2,1)} %get-tuple-element.59), channel_id=1, source_target_pairs={{0,5},{1,6},{2,7},{3,0},{4,1},{5,2},{6,3},{7,4},{8,13},{9,14},{10,... | collective-permute-start | bytes 884744 | tf_op jit(solution)/shard_map/ppermute | solution.py:72
  230.1 20.9 %collective-permute-start.19 = (bf16[576,256]{1,0:T(8,128)(2,1)}, bf16[576,256]{1,0:T(8,128)(2,1)}, u32[]{:S(2)}, u32[]{:S(2)}) collective-permute-start(bf16[576,256]{1,0:T(8,128)(2,1)} %get-tuple-element.60), channel_id=1, source_target_pairs={{0,6},{1,7},{2,0},{3,1},{4,2},{5,3},{6,4},{7,5},{8,14},{9,15},{10,... | collective-permute-start | bytes 884744 | tf_op jit(solution)/shard_map/ppermute | solution.py:72
  235.0 24.0 %collective-permute-start.20 = (bf16[576,256]{1,0:T(8,128)(2,1)}, bf16[576,256]{1,0:T(8,128)(2,1)}, u32[]{:S(2)}, u32[]{:S(2)}) collective-permute-start(bf16[576,256]{1,0:T(8,128)(2,1)} %get-tuple-element.61), channel_id=1, source_target_pairs={{0,7},{1,0},{2,1},{3,2},{4,3},{5,4},{6,5},{7,6},{8,15},{9,8},{10,9... | collective-permute-start | bytes 884744 | tf_op jit(solution)/shard_map/ppermute | solution.py:72
  245.0 163.4 %collective-permute-start.23 = (bf16[512,256]{1,0:T(8,128)(2,1)}, bf16[512,256]{1,0:T(8,128)(2,1)}, u32[]{:S(2)}, u32[]{:S(2)}) collective-permute-start(bf16[512,256]{1,0:T(8,128)(2,1)} %get-tuple-element.66), channel_id=1, source_target_pairs={{0,3},{1,4},{2,5},{3,6},{4,7},{5,0},{6,1},{7,2},{8,11},{9,12},{10,... | collective-permute-start | bytes 786440 | tf_op jit(solution)/shard_map/ppermute | solution.py:72
  245.5 162.9 %collective-permute-start.24 = (bf16[512,256]{1,0:T(8,128)(2,1)}, bf16[512,256]{1,0:T(8,128)(2,1)}, u32[]{:S(2)}, u32[]{:S(2)}) collective-permute-start(bf16[512,256]{1,0:T(8,128)(2,1)} %get-tuple-element.67), channel_id=1, source_target_pairs={{0,4},{1,5},{2,6},{3,7},{4,0},{5,1},{6,2},{7,3},{8,12},{9,13},{10,... | collective-permute-start | bytes 786440 | tf_op jit(solution)/shard_map/ppermute | solution.py:72
  247.9 160.5 %collective-permute-start.25 = (bf16[512,256]{1,0:T(8,128)(2,1)}, bf16[512,256]{1,0:T(8,128)(2,1)}, u32[]{:S(2)}, u32[]{:S(2)}) collective-permute-start(bf16[512,256]{1,0:T(8,128)(2,1)} %get-tuple-element.68), channel_id=1, source_target_pairs={{0,5},{1,6},{2,7},{3,0},{4,1},{5,2},{6,3},{7,4},{8,13},{9,14},{10,... | collective-permute-start | bytes 786440 | tf_op jit(solution)/shard_map/ppermute | solution.py:72
  251.0 157.5 %collective-permute-start.26 = (bf16[512,256]{1,0:T(8,128)(2,1)}, bf16[512,256]{1,0:T(8,128)(2,1)}, u32[]{:S(2)}, u32[]{:S(2)}) collective-permute-start(bf16[512,256]{1,0:T(8,128)(2,1)} %get-tuple-element.69), channel_id=1, source_target_pairs={{0,6},{1,7},{2,0},{3,1},{4,2},{5,3},{6,4},{7,5},{8,14},{9,15},{10,... | collective-permute-start | bytes 786440 | tf_op jit(solution)/shard_map/ppermute | solution.py:72
  258.9 149.5 %collective-permute-start.27 = (bf16[512,256]{1,0:T(8,128)(2,1)}, bf16[512,256]{1,0:T(8,128)(2,1)}, u32[]{:S(2)}, u32[]{:S(2)}) collective-permute-start(bf16[512,256]{1,0:T(8,128)(2,1)} %get-tuple-element.70), channel_id=1, source_target_pairs={{0,7},{1,0},{2,1},{3,2},{4,3},{5,4},{6,5},{7,6},{8,15},{9,8},{10,9... | collective-permute-start | bytes 786440 | tf_op jit(solution)/shard_map/ppermute | solution.py:72
  (25 other events, 1094.7 us)

commit v4 on v2

--- a/solution.py
+++ b/solution.py
@@ -16,19 +16,18 @@
 LOG2E = 1.4426950408889634
 SCALE = HEAD_DIM ** (-0.5) * LOG2E
 NEG = -1e30
-
-
-def project_kernel(here_ref, *refs, sources, weights, groups):
+LANES = 128
+SUB = 8
+
+
+def project_kernel(here_ref, *refs, sources, weights, groups, place):
     x_refs, rest = refs[:sources], refs[sources:]
     w_refs, o_refs, x_ref = rest[:weights], rest[weights : weights + groups], rest[-1]
     step = pl.program_id(0)
 
     @pl.when(step == 0)
     def _():
-        row = 0
-        for ref in x_refs:
-            x_ref[row : row + ref.shape[0]] = ref[...]
-            row += ref.shape[0]
+        place(x_ref, *x_refs)
 
     w = jnp.concatenate([ref[...] for ref in w_refs], axis=1)
     r = jnp.dot(x_ref[...], w, preferred_element_type=jnp.float32).astype(jnp.bfloat16)
@@ -39,17 +38,48 @@
             o_ref[...] = r
 
 
-def project(here, xs, ws, groups):
-    rows = sum(x.shape[0] for x in xs)
-    width = xs[0].shape[1]
+def place_rows(x_ref, rows_ref):
+    x_ref[...] = rows_ref[...]
+
+
+def place_chunks(x_ref, got_ref):
+    shards, _, lanes = got_ref.shape
+    part = x_ref.shape[0] // shards
+    for k in range(x_ref.shape[1] // lanes):
+        x_ref[:, k * lanes : (k + 1) * lanes] = got_ref[:, k * part : (k + 1) * part, :].reshape(
+            shards * part, lanes
+        )
+
+
+def place_chunks_and_edges(x_ref, got_ref, edge_ref):
+    shards, tall, lanes = got_ref.shape
+    edges = edge_ref.shape[0]
+    width = x_ref.shape[1]
+    across = width // lanes
+    extra = shards * SUB // across
+    rows = x_ref.shape[0] - edges - extra
+    place_chunks(x_ref.at[:rows], got_ref)
+    x_ref[rows : rows + edges] = edge_ref[...]
+    for b in range(shards):
+        row = rows + edges + b // across * SUB
+        lane = b % across * lanes
+        x_ref[row : row + SUB, lane : lane + lanes] = got_ref[b, tall - SUB :, :]
+
+
+def project(here, xs, rows, ws, groups, place):
+    width = ws[0].shape[0]
     lanes = ws[0].shape[1] // groups
     out_lanes = lanes * len(ws)
     return pl.pallas_call(
-        functools.partial(project_kernel, sources=len(xs), weights=len(ws), groups=groups),
+        functools.partial(
+            project_kernel, sources=len(xs), weights=len(ws), groups=groups, place=place
+        ),
         grid_spec=pltpu.PrefetchScalarGridSpec(
             num_scalar_prefetch=1,
             grid=(groups,),
-            in_specs=[pl.BlockSpec(x.shape, lambda o, here: (0, 0)) for x in xs]
+            in_specs=[
+                pl.BlockSpec(x.shape, lambda o, here, n=len(x.shape): (0,) * n) for x in xs
+            ]
             + [
                 pl.BlockSpec((width, lanes), lambda o, here: (0, lax.rem(here[0] + o, groups)))
                 for _ in ws
@@ -74,42 +104,100 @@
     ]
 
 
-def broadcast_first(value, axis, index):
-    size = lax.axis_size(axis)
-    hop = size // 2
-    while hop:
-        got = lax.ppermute(value, axis, [(i, i + hop) for i in range(0, size, 2 * hop)])
-        value = jnp.where(lax.rem(index, 2 * hop) == hop, got, value)
-        hop //= 2
-    return value
-
-
-def pick_kernel(index_ref, x_ref, *o_refs):
-    count = x_ref.shape[0]
+def pick_chunk(o_ref, d, tile):
+    lanes = o_ref.shape[2]
+    part, width = tile.shape
+    for k in range(width // lanes):
+        o_ref[d, k * part : (k + 1) * part, :] = tile[:, k * lanes : (k + 1) * lanes]
+
+
+def pick_first_kernel(index_ref, x_ref, o_ref):
+    dests, tall, lanes = o_ref.shape
+    part, width = x_ref.shape[1:]
+    across = width // lanes
 
     def step(d, carry):
-        for s, o_ref in enumerate(o_refs):
-            o_ref[d] = x_ref[index_ref[s * count + d]]
+        pick_chunk(o_ref, d, x_ref[index_ref[d]])
         return carry
 
-    lax.fori_loop(0, count, step, 0)
-
-
-def pick_tiles(index, x, dests):
-    whole = pl.BlockSpec(x.shape, lambda i, idx: (0, 0, 0))
-    out = (dests,) + x.shape[1:]
+    lax.fori_loop(0, dests, step, 0)
+    for b in range(dests):
+        row = b // across * SUB
+        lane = b % across * lanes
+        o_ref[b, tall - SUB :, :] = x_ref[
+            row // part, row % part : row % part + SUB, lane : lane + lanes
+        ]
+
+
+def pick_second_kernel(index_ref, x_ref, root_ref, o_ref):
+    dests, tall, _ = o_ref.shape
+    block = root_ref[0]
+
+    def step(d, carry):
+        pick_chunk(o_ref, d, x_ref[index_ref[d]])
+        o_ref[d, tall - SUB :, :] = block
+        return carry
+
+    lax.fori_loop(0, dests, step, 0)
+
+
+def pick_chunks(index, x, dests, got):
+    _, part, width = x.shape
+    tall = part * width // LANES + SUB
+    out = (dests, tall, LANES)
+    whole = lambda shape: pl.BlockSpec(shape, lambda i, idx: (0,) * len(shape))
+    ins, specs, kernel = [x], [whole(x.shape)], pick_first_kernel
+    if got is not None:
+        ins.append(got)
+        specs.append(pl.BlockSpec((1, SUB, LANES), lambda i, idx: (0, tall // SUB - 1, 0)))
+        kernel = pick_second_kernel
     return pl.pallas_call(
-        pick_kernel,
+        kernel,
         grid_spec=pltpu.PrefetchScalarGridSpec(
-            num_scalar_prefetch=1,
+            num_scalar_prefetch=1, grid=(1,), in_specs=specs, out_specs=whole(out)
+        ),
+        out_shape=jax.ShapeDtypeStruct(out, x.dtype),
+        cost_estimate=pl.CostEstimate(flops=0, transcendentals=0, bytes_accessed=4 * x.size * 2),
+    )(index, *ins)
+
+
+def pick_kv_kernel(index_ref, here_ref, *refs):
+    own_refs, (o_ref, kv_ref) = refs[:-2], refs[-2:]
+    groups = len(own_refs)
+    tiles = own_refs[0].shape[0] // TILE
+    both = kv_ref.shape[2]
+    lanes = own_refs[0].shape[1] - both
+    for o, ref in enumerate(own_refs):
+        home = lax.rem(here_ref[0] + groups - o, groups) * tiles
+        for i in range(tiles):
+            kv_ref[home + i] = ref[i * TILE : (i + 1) * TILE, lanes:]
+
+    def step(d, carry):
+        o_ref[d] = kv_ref[index_ref[d]]
+        return carry
+
+    lax.fori_loop(0, o_ref.shape[0], step, 0)
+
+
+def pick_kv(index, here, own, dests):
+    rows, lanes = own[0].shape
+    both = lanes * 2 // 3
+    out = (dests, TILE, both)
+    return pl.pallas_call(
+        pick_kv_kernel,
+        grid_spec=pltpu.PrefetchScalarGridSpec(
+            num_scalar_prefetch=2,
             grid=(1,),
-            in_specs=[whole],
-            out_specs=[pl.BlockSpec(out, lambda i, idx: (0, 0, 0))] * CAP,
-        ),
-        out_shape=[jax.ShapeDtypeStruct(out, x.dtype)] * CAP,
-        cost_estimate=pl.CostEstimate(flops=0, transcendentals=0, bytes_accessed=4 * x.size * 2),
-        name="pick_tiles",
-    )(index, x)
+            in_specs=[pl.BlockSpec((rows, lanes), lambda i, idx, here: (0, 0))] * len(own),
+            out_specs=pl.BlockSpec(out, lambda i, idx, here: (0, 0, 0)),
+            scratch_shapes=[pltpu.VMEM((len(own) * rows // TILE, TILE, both), jnp.bfloat16)],
+        ),
+        out_shape=jax.ShapeDtypeStruct(out, jnp.bfloat16),
+        cost_estimate=pl.CostEstimate(
+            flops=0, transcendentals=0, bytes_accessed=10 * len(own) * rows * lanes // 3
+        ),
+        name="pick_kv",
+    )(index, here, *own)
 
 
 def split_heads(q):
@@ -216,22 +304,29 @@
     )(place, *own, *ext)
 
 
-def random_kernel(index_ref, count_ref, *refs, groups):
-    part_refs = refs[: CAP * groups]
-    q_ref, m_ref, l_ref, a_ref, o_ref, kv_ref = refs[CAP * groups :]
+def random_kernel(index_ref, count_ref, *refs, groups, spread):
+    part_refs, whole_refs = refs[: spread * groups], refs[spread * groups : spread * groups + CAP - spread]
+    q_ref, m_ref, l_ref, a_ref, o_ref, kv_ref, sems = refs[spread * groups + CAP - spread :]
     lanes = q_ref.shape[1]
     step = pl.program_id(0)
     per_step = q_ref.shape[0] // TILE
     part = TILE // groups
-    shards = part_refs[0].shape[0] // part
+    shards = kv_ref.shape[0] // CAP
 
     @pl.when(step == 0)
     def _():
+        copies = []
         for i, ref in enumerate(part_refs):
             s, o = divmod(i, groups)
-            kv_ref[s * shards : (s + 1) * shards, o * part : (o + 1) * part, :] = ref[...].reshape(
-                shards, part, 2 * lanes
-            )
+            home = kv_ref.at[s * shards : (s + 1) * shards, o * part : (o + 1) * part, :]
+            copies.append(pltpu.make_async_copy(ref.at[:shards], home, sems.at[i]))
+        for i, ref in enumerate(whole_refs):
+            home = kv_ref.at[(spread + i) * shards : (spread + i + 1) * shards]
+            copies.append(pltpu.make_async_copy(ref, home, sems.at[spread * groups + i]))
+        for copy in copies:
+            copy.start()
+        for copy in copies:
+            copy.wait()
 
     for i in range(per_step):
         t = step * per_step + i
@@ -241,11 +336,13 @@
         at = [index_ref[t * RANDOM + j] for j in range(RANDOM)]
         scores = []
         top = None
-        for j in range(RANDOM):
-            bias = jnp.where(j < count, 0.0, NEG).astype(jnp.float32)
-            s = score(q2, kv_ref[at[j], :, :lanes]) + bias
-            scores.append(s)
-            top = s if top is None else jnp.maximum(top, s)
+        for j in range(0, RANDOM, 2):
+            keys = jnp.concatenate([kv_ref[at[j], :, :lanes], kv_ref[at[j + 1], :, :lanes]], axis=0)
+            s = score(q2, keys)
+            for i, part in enumerate((s[:, :TILE], s[:, TILE:])):
+                part = part + jnp.where(j + i < count, 0.0, NEG).astype(jnp.float32)
+                scores.append(part)
+                top = part if top is None else jnp.maximum(top, part)
         m_old = m_ref[rows, :]
         m_old = jnp.concatenate([m_old[:, :1], m_old[:, HEAD_DIM : HEAD_DIM + 1]], axis=0)
         m_new = jnp.maximum(jnp.max(top, axis=1, keepdims=True), m_old)
@@ -266,31 +363,36 @@
         o_ref[rows, :] = (numerator / denominator).astype(jnp.bfloat16)
 
 
-def random_attention(index, count, q, fetched, m, l, a, part_rows, per_step=2):
+def random_attention(index, count, q, parts, whole, m, l, a, per_step=8):
     rows, lanes = q.shape
-    groups = len(fetched) // CAP
+    groups = len(parts[0])
+    spread = len(parts)
+    shards = whole[0].shape[0]
+    part = TILE // groups
+    flat = [f.reshape(-1, part, 2 * lanes) for slot in parts for f in slot]
     block = pl.BlockSpec((per_step * TILE, lanes), lambda i, s, c: (i, 0))
-    fixed = pl.BlockSpec((part_rows, 2 * lanes), lambda i, s, c: (0, 0))
     keys = RANDOM * TILE
+    sources = len(flat) + len(whole)
     return pl.pallas_call(
-        functools.partial(random_kernel, groups=groups),
+        functools.partial(random_kernel, groups=groups, spread=spread),
         grid_spec=pltpu.PrefetchScalarGridSpec(
             num_scalar_prefetch=2,
             grid=(rows // (per_step * TILE),),
-            in_specs=[fixed] * len(fetched) + [block] * 4,
+            in_specs=[pl.BlockSpec(memory_space=pl.ANY)] * sources + [block] * 4,
             out_specs=block,
             scratch_shapes=[
-                pltpu.VMEM((CAP * part_rows * groups // TILE, TILE, 2 * lanes), jnp.bfloat16)
+                pltpu.VMEM((CAP * shards, TILE, 2 * lanes), jnp.bfloat16),
+                pltpu.SemaphoreType.DMA((sources,)),
             ],
         ),
         out_shape=jax.ShapeDtypeStruct((rows, lanes), jnp.bfloat16),
         cost_estimate=pl.CostEstimate(
             flops=8 * rows * keys * lanes,
             transcendentals=2 * rows * keys,
-            bytes_accessed=rows * lanes * 16 + CAP * part_rows * groups * lanes * 4,
+            bytes_accessed=rows * lanes * 16 + CAP * shards * TILE * lanes * 4,
         ),
         name="random_attention",
-    )(index, count, *fetched, q, m, l, a)
+    )(index, count, *flat, *whole, q, m, l, a)
 
 
 def request_tables(random_tiles, random_count, shard, ctx_count, tiles_here):
@@ -314,7 +416,7 @@
     )
     slot = jnp.sum(lower.astype(jnp.int32), axis=1)
     read = jnp.where(wanted >= 0, slot * ctx_count + owner, 0)
-    return send.T.reshape(-1), read
+    return [send[:, slot] for slot in range(CAP)], read
 
 
 def body(tokens, w_query, w_key, w_value, w_out, random_tiles, random_count):
@@ -332,30 +434,35 @@
     striped = lax.all_to_all(striped, "head", split_axis=0, concat_axis=0, tiled=True)
     striped = striped.reshape(tiles_here, part, width)
     send, read = request_tables(random_tiles, random_count, shard, ctx_count, tiles_here)
-    outgoing = pick_tiles(send, striped, ctx_count)
-
-    where = here[None]
-    own = project(where, [tokens], [w_query, w_key, w_value], groups)
+    head = here[None]
+
+    own = project(head, [tokens], rows, [w_query, w_key, w_value], groups, place_rows)
     own = exchange(own, "head")
 
     up = [(i, i + 1) for i in range(ctx_count - 1)]
     down = [(j, i) for i, j in up]
     before = lax.ppermute(striped[-1:], "ctx", up)
     after = lax.ppermute(striped[:1], "ctx", down)
-    root = broadcast_first(striped[:GLOBALS], "ctx", shard)
-    ext = jnp.concatenate([before, after, root], axis=0).reshape(-1, width)
-
-    fetched = []
-    for slot in range(CAP):
-        got = lax.all_to_all(outgoing[slot], "ctx", split_axis=0, concat_axis=0, tiled=True)
-        got = [got.reshape(ctx_count * part, width)] + ([ext] if slot == 0 else [])
-        got = project(where, got, [w_key, w_value], groups)
-        fetched += exchange(got, "head")
-
-    place = jnp.stack([shard, jnp.int32(tiles_here * ctx_count), here])
-    m, l, a, q = local_attention(place, own, fetched[:groups], ext.shape[0])
+    edges = jnp.concatenate([before, after], axis=0).reshape(2 * part, width)
+
+    fetched, got = [], None
+    for slot in range(CAP - 1):
+        chunks = pick_chunks(send[slot], striped, ctx_count, got)
+        got = lax.all_to_all(chunks, "ctx", split_axis=0, concat_axis=0, tiled=True)
+        count = ctx_count * part
+        if slot == 0:
+            xs, place = [got], place_chunks
+        else:
+            xs, place, count = [got, edges], place_chunks_and_edges, count + (2 + GLOBALS) * part
+        projected = project(head, xs, count, [w_key, w_value], groups, place)
+        fetched.append(exchange(projected, "head"))
+    chosen = pick_kv(send[CAP - 1], head, own, ctx_count)
+    whole = lax.all_to_all(chosen, "ctx", split_axis=0, concat_axis=0, tiled=True)
+
+    where = jnp.stack([shard, jnp.int32(tiles_here * ctx_count), here])
+    m, l, a, q = local_attention(where, own, fetched[1], (2 + GLOBALS) * part)
     my_count = lax.dynamic_slice_in_dim(random_count, shard * tiles_here, tiles_here, 0)
-    attended = random_attention(read, my_count, q, fetched, m, l, a, ctx_count * part)
+    attended = random_attention(read, my_count, q, fetched, [whole], m, l, a)
     attended = attended.reshape(groups, rows, -1)
     returned = lax.all_to_all(attended, "head", split_axis=0, concat_axis=0, tiled=True)
     out = lax.dot_general(

time: 318 us -> 320 us (level)
  the two profiles are of different devices: /device:TPU:1 before, /device:TPU:160 now
where the time goes in v4:
time: 320 us; the launch traced here: 319 us
  Pallas kernels  90.2 us (28%)
  waiting for transfers between devices  87.3 us (27%)
  starting transfers between devices  69.2 us (22%)
  blocking collectives  56.5 us (18%)
  local copies, waits for them, and re-layouts  8.82 us (3%)
  other arithmetic  4.35 us (1%)
    ppermute x1, waiting for transfers between devices, body(): before = lax.ppermute(striped[-1:], 'ctx', up)  41.8 us
    ppermute x21, starting transfers between devices, exchange(): lax.ppermute(pieces[o], axis, [(i, (i + o) % size) for i in range(size)])  39.1 us
    all_to_all x1, blocking collectives, body(): got = lax.all_to_all(chunks, 'ctx', split_axis=0, concat_axis=0, tiled=True)  37 us
    ppermute x21, waiting for transfers between devices, exchange(): lax.ppermute(pieces[o], axis, [(i, (i + o) % size) for i in range(size)])  34.2 us
    pallas_call x1, Pallas kernels, random_attention(): pl.pallas_call(functools.partial(random_kernel, groups=groups, spread=spr...  31.9 us
    pallas_call x3, Pallas kernels, project(): pl.pallas_call(functools.partial(project_kernel, sources=len(xs), weights...  29 us
    all_to_all x1, blocking collectives, body(): lax.all_to_all(attended, 'head', split_axis=0, concat_axis=0, tiled=True)  19.5 us
    pallas_call x1, Pallas kernels, local_attention(): pl.pallas_call(functools.partial(local_kernel, groups=groups), grid_spec=...  18.7 us
  transfers between devices with their start and end apart: 26, of which 11 were waited for; matrix products, arithmetic and copies ran while one was open for 3% of the time, Pallas kernels for 16%

profile of v4, /device:TPU:160, one launch (start us, length us, event | category | flops | bytes accessed | tf_op | source)
XLA Modules:
  0.0 318.9 jit_solution(10614688665377525602)
XLA Ops:
  0.0 2.5 copy.14
  2.5 4.5 %all-to-all-start = ((bf16[8,4,16,1024]{3,2,1,0:T(8,128)(2,1)}), bf16[8,4,16,1024]{3,2,1,0:T(8,128)(2,1)S(1)}, u32[]{:S(2)}, u32[]{:S(2)}) async-start(bf16[8,4,16,1024]{3,2,1,0:T(8,128)(2,1)} %bitcast.40), calls=%async_computation | async-start | bytes 2097152 | tf_op jit(solution)/shard_map/all_to_all | solution.py:434
  11.5 11.4 %all-to-all-done = bf16[8,4,16,1024]{3,2,1,0:T(8,128)(2,1)S(1)} async-done(((bf16[8,4,16,1024]{3,2,1,0:T(8,128)(2,1)}), bf16[8,4,16,1024]{3,2,1,0:T(8,128)(2,1)S(1)}, u32[]{:S(2)}, u32[]{:S(2)}) %all-to-all-start) | async-done | bytes 1048608 | tf_op jit(solution)/shard_map/all_to_all | solution.py:434
  23.8 3.2 %shard_map.73 = bf16[32,136,128]{2,1,0:T(8,128)(2,1)} custom-call(s32[32]{0:T(128)} %get-tuple-element.65.index_ref, bf16[32,16,1024]{2,1,0:T(8,128)(2,1)} %bitcast.37), custom_call_target="tpu_custom_call" | custom-call | bytes 4194304 | tf_op jit(solution)/shard_map/pallas_call | solution.py:154
  27.1 37.0 %all_to_all.25.refs_0_.root_ref = bf16[32,136,128]{2,1,0:T(8,128)(2,1)} all-to-all(bf16[32,136,128]{2,1,0:T(8,128)(2,1)} %shard_map.73), channel_id=1, replica_groups=mesh['ctx'=32,'head'=8] {'ctx'}, dimensions={0} | all-to-all | bytes 2228224 | tf_op jit(solution)/shard_map/all_to_all | solution.py:451
  64.1 3.2 %shard_map.75 = bf16[32,136,128]{2,1,0:T(8,128)(2,1)} custom-call(s32[32]{0:T(128)} %get-tuple-element.64.index_ref, bf16[32,16,1024]{2,1,0:T(8,128)(2,1)} %bitcast.38, bf16[32,136,128]{2,1,0:T(8,128)(2,1)} %all_to_all.25.refs_0_.root_ref), custom_call_target="tpu_custom_call" | custom-call | bytes 4194304 | tf_op jit(solution)/shard_map/pallas_call | solution.py:154
  67.3 7.8 %all-to-all-start.2 = ((bf16[32,136,128]{2,1,0:T(8,128)(2,1)}), bf16[32,136,128]{2,1,0:T(8,128)(2,1)S(1)}, u32[]{:S(2)}, u32[]{:S(2)}) async-start(bf16[32,136,128]{2,1,0:T(8,128)(2,1)} %shard_map.75), calls=%async_computation.2 | async-start | bytes 2228224 | tf_op jit(solution)/shard_map/all_to_all | solution.py:451
  75.1 10.9 %shard_map.77 = (bf16[512,384]{1,0:T(8,128)(2,1)}, bf16[512,384]{1,0:T(8,128)(2,1)}, bf16[512,384]{1,0:T(8,128)(2,1)}, bf16[512,384]{1,0:T(8,128)(2,1)}, bf16[51...) custom-call(s32[1]{0:T(128)} %bitcast.here_ref, ...), custom_call_target="tpu_custom_call" | custom-call | flops 3221225472 | bytes 10485760 | tf_op jit(solution)/shard_map/pallas_call | solution.py:73
  88.1 2.7 collective-permute-start.19
  91.7 6.6 %collective-permute-done.16.refs_1_ = bf16[512,384]{1,0:T(8,128)(2,1)} collective-permute-done((bf16[512,384]{1,0:T(8,128)(2,1)}, bf16[512,384]{1,0:T(8,128)(2,1)}, u32[]{:S(2)}, u32[]{:S(2)}) %collective-permute-start.16) | collective-permute-done | bytes 393248 | tf_op jit(solution)/shard_map/ppermute | solution.py:102
  99.7 6.8 %collective-permute-start.22 = (bf16[512,384]{1,0:T(8,128)(2,1)}, bf16[512,384]{1,0:T(8,128)(2,1)}, u32[]{:S(2)}, u32[]{:S(2)}) collective-permute-start(bf16[512,384]{1,0:T(8,128)(2,1)} %get-tuple-element.56), channel_id=1, source_target_pairs={{0,7},{1,0},{2,1},{3,2},{4,3},{5,4},{6,5},{7,6},{8,15},{9,8},{10,9... | collective-permute-start | bytes 1179656 | tf_op jit(solution)/shard_map/ppermute | solution.py:102
  106.5 8.2 %collective-permute-done.18.refs_3_ = bf16[512,384]{1,0:T(8,128)(2,1)} collective-permute-done((bf16[512,384]{1,0:T(8,128)(2,1)}, bf16[512,384]{1,0:T(8,128)(2,1)}, u32[]{:S(2)}, u32[]{:S(2)}) %collective-permute-start.18) | collective-permute-done | bytes 393248 | tf_op jit(solution)/shard_map/ppermute | solution.py:102
  116.0 5.2 %collective-permute-done.20.refs_5_ = bf16[512,384]{1,0:T(8,128)(2,1)} collective-permute-done((bf16[512,384]{1,0:T(8,128)(2,1)}, bf16[512,384]{1,0:T(8,128)(2,1)}, u32[]{:S(2)}, u32[]{:S(2)}) %collective-permute-start.20) | collective-permute-done | bytes 393248 | tf_op jit(solution)/shard_map/ppermute | solution.py:102
  121.2 3.0 collective-permute-done.22.refs_7_
  124.2 4.2 %pick_kv.1 = bf16[32,128,256]{2,1,0:T(8,128)(2,1)} custom-call(s32[32]{0:T(128)} %get-tuple-element.63.index_ref, s32[1]{0:T(128)} %bitcast.here_ref, bf16[512,384]{1,0:T(8,128)(2,1)} %get-tuple-element.49.refs_0_, bf16[512,384]{1,0:T(8,128)(2,1)} %collective-permute-done.16.refs_1_, bf16[512,384]{1,0:T(8,128)(2,1)} %collective-permute-done.17.refs_2_, ...), custom_call_target="tpu_custom_call" | custom-call | bytes 5242880 | tf_op jit(solution)/shard_map/pick_kv/pallas_call | solution.py:186
  129.5 9.8 %all-to-all-start.3 = ((bf16[32,128,256]{2,1,0:T(8,128)(2,1)}), bf16[32,128,256]{2,1,0:T(8,128)(2,1)}, u32[]{:S(2)}, u32[]{:S(2)}) async-start(bf16[32,128,256]{2,1,0:T(8,128)(2,1)} %pick_kv.1), calls=%async_computation.3 | async-start | bytes 4194304 | tf_op jit(solution)/shard_map/all_to_all | solution.py:460
  140.1 3.4 %collective-permute-start.7 = (bf16[1,16,1024]{2,1,0:T(8,128)(2,1)S(1)}, bf16[1,16,1024]{2,1,0:T(8,128)(2,1)S(1)}, u32[]{:S(2)}, u32[]{:S(2)}) collective-permute-start(bf16[1,16,1024]{2,1,0:T(8,128)(2,1)S(1)} %get-tuple-element.61), channel_id=1, source_target_pairs={{0,8},{8,16},{16,24},{24,32},{32,40},{40,48},{48,56},{56,64},{64,7... | collective-permute-start | bytes 98312 | tf_op jit(solution)/shard_map/ppermute | solution.py:444
  143.4 4.6 %collective-permute-start.8 = (bf16[1,16,1024]{2,1,0:T(8,128)(2,1)S(1)}, bf16[1,16,1024]{2,1,0:T(8,128)(2,1)S(1)}, u32[]{:S(2)}, u32[]{:S(2)}) collective-permute-start(bf16[1,16,1024]{2,1,0:T(8,128)(2,1)S(1)} %get-tuple-element.62), channel_id=1, source_target_pairs={{8,0},{16,8},{24,16},{32,24},{40,32},{48,40},{56,48},{64,56},{72,6... | collective-permute-start | bytes 98312 | tf_op jit(solution)/shard_map/ppermute | solution.py:445
  148.1 41.8 %collective-permute-done.7 = bf16[1,16,1024]{2,1,0:T(8,128)(2,1)S(1)} collective-permute-done((bf16[1,16,1024]{2,1,0:T(8,128)(2,1)S(1)}, bf16[1,16,1024]{2,1,0:T(8,128)(2,1)S(1)}, u32[]{:S(2)}, u32[]{:S(2)}) %collective-permute-start.7) | collective-permute-done | bytes 32800 | tf_op jit(solution)/shard_map/ppermute | solution.py:444
  190.4 8.9 %shard_map.74 = (bf16[512,256]{1,0:T(8,128)(2,1)}, bf16[512,256]{1,0:T(8,128)(2,1)}, bf16[512,256]{1,0:T(8,128)(2,1)}, bf16[512,256]{1,0:T(8,128)(2,1)}, bf16[51...) custom-call(s32[1]{0:T(128)} %bitcast.here_ref, ...), custom_call_target="tpu_custom_call" | custom-call | flops 2147483648 | bytes 7340032 | tf_op jit(solution)/shard_map/pallas_call | solution.py:73
  199.9 1.9 collective-permute-start.5
  201.8 9.2 %shard_map.76 = (bf16[576,256]{1,0:T(8,128)(2,1)}, bf16[576,256]{1,0:T(8,128)(2,1)}, bf16[576,256]{1,0:T(8,128)(2,1)}, bf16[576,256]{1,0:T(8,128)(2,1)}, bf16[57...) custom-call(s32[1]{0:T(128)} %bitcast.here_ref, ...), custom_call_target="tpu_custom_call" | custom-call | flops 2415919104 | bytes 7733248 | tf_op jit(solution)/shard_map/pallas_call | solution.py:73
  212.1 2.1 collective-permute-start.12
  214.3 3.0 collective-permute-start.13
  218.0 4.4 %collective-permute-done.10.refs_10_ = bf16[576,256]{1,0:T(8,128)(2,1)S(1)} collective-permute-done((bf16[576,256]{1,0:T(8,128)(2,1)}, bf16[576,256]{1,0:T(8,128)(2,1)S(1)}, u32[]{:S(2)}, u32[]{:S(2)}) %collective-permute-start.10) | collective-permute-done | bytes 294944 | tf_op jit(solution)/shard_map/ppermute | solution.py:102
  222.4 2.8 collective-permute-done.11.refs_11_
  225.2 11.2 %collective-permute-start.9 = (bf16[576,256]{1,0:T(8,128)(2,1)}, bf16[576,256]{1,0:T(8,128)(2,1)}, u32[]{:S(2)}, u32[]{:S(2)}) collective-permute-start(bf16[576,256]{1,0:T(8,128)(2,1)} %get-tuple-element.42), channel_id=1, source_target_pairs={{0,1},{1,2},{2,3},{3,4},{4,5},{5,6},{6,7},{7,0},{8,9},{9,10},{10,1... | collective-permute-start | bytes 884744 | tf_op jit(solution)/shard_map/ppermute | solution.py:102
  241.6 3.6 %collective-permute-start.3 = (bf16[512,256]{1,0:T(8,128)(2,1)}, bf16[512,256]{1,0:T(8,128)(2,1)}, u32[]{:S(2)}, u32[]{:S(2)}) collective-permute-start(bf16[512,256]{1,0:T(8,128)(2,1)} %get-tuple-element.37), channel_id=1, source_target_pairs={{0,4},{1,5},{2,6},{3,7},{4,0},{5,1},{6,2},{7,3},{8,12},{9,13},{10,... | collective-permute-start | bytes 786440 | tf_op jit(solution)/shard_map/ppermute | solution.py:102
  246.5 18.7 %local_attention.1 = (f32[4096,128]{1,0:T(8,128)}, f32[4096,128]{1,0:T(8,128)}, f32[4096,128]{1,0:T(8,128)}, bf16[4096,128]{1,0:T(8,128)(2,1)}) custom-call(s32[3]{0:T(128)} %pad_add_fusion.place_ref, bf16[512,384]{1,0:T(8,128)(2,1)} %get-tuple-element.49.refs_0_, bf16[512,384]{1,0:T(8,128)(2,1)} %collective-permute-done.16.refs_1_, ...), custom_call_target="tpu_custom_call" | custom-call | flops 2684354560 | bytes 10485760 | tf_op jit(solution)/shard_map/local_attention/pallas_call | solution.py:284
  265.2 31.9 %random_attention.1 = bf16[4096,128]{1,0:T(8,128)(2,1)} custom-call(s32[384]{0:T(512)} %add_select_fusion.1.index_ref, s32[32]{0:T(128)} %dynamic_slice.8.count_ref, bf16[32,16,256]{2,1,0:T(8,128)(2,1)} %bitcast.50, bf16[32,16,256]{2,1,0:T(8,128)(2,1)} %bitcast.6.refs_1_, bf16[32,16,256]{2,1,0:T(8,128)(2,1)} %bitcast.7.refs_2_, ...), custom_call_target="tpu_custom_call" | custom-call | flops 6442450944 | bytes 14680064 | tf_op jit(solution)/shard_map/random_attention/pallas_call | solution.py:376
  297.1 19.5 %all_to_all.26 = bf16[8,512,128]{2,1,0:T(8,128)(2,1)S(1)} all-to-all(bf16[8,512,128]{2,1,0:T(8,128)(2,1)} %bitcast.42), channel_id=1, replica_groups=mesh['ctx'=32,'head'=8] {'head'}, dimensions={0} | all-to-all | bytes 2097152 | tf_op jit(solution)/shard_map/all_to_all | solution.py:467
  316.6 2.3 bitcast_convert_fusion
  (70 shorter events, 22.5 us)
Async XLA Ops:
  0.0 316.6 %copy-start = (bf16[1024,1024]{1,0:T(8,128)(2,1)S(1)}, bf16[1024,1024]{1,0:T(8,128)(2,1)}, u32[]{:S(2)}) copy-start(bf16[1024,1024]{1,0:T(8,128)(2,1)} %param.11) | copy-start | bytes 6291460
  2.5 20.4 %all-to-all-start = ((bf16[8,4,16,1024]{3,2,1,0:T(8,128)(2,1)}), bf16[8,4,16,1024]{3,2,1,0:T(8,128)(2,1)S(1)}, u32[]{:S(2)}, u32[]{:S(2)}) async-start(bf16[8,4,16,1024]{3,2,1,0:T(8,128)(2,1)} %bitcast.40), calls=%async_computation | async-start | bytes 2097152 | tf_op jit(solution)/shard_map/all_to_all | solution.py:434
  67.3 61.2 %all-to-all-start.2 = ((bf16[32,136,128]{2,1,0:T(8,128)(2,1)}), bf16[32,136,128]{2,1,0:T(8,128)(2,1)S(1)}, u32[]{:S(2)}, u32[]{:S(2)}) async-start(bf16[32,136,128]{2,1,0:T(8,128)(2,1)} %shard_map.75), calls=%async_computation.2 | async-start | bytes 2228224 | tf_op jit(solution)/shard_map/all_to_all | solution.py:451
  86.1 12.3 %collective-permute-start.16 = (bf16[512,384]{1,0:T(8,128)(2,1)}, bf16[512,384]{1,0:T(8,128)(2,1)}, u32[]{:S(2)}, u32[]{:S(2)}) collective-permute-start(bf16[512,384]{1,0:T(8,128)(2,1)} %get-tuple-element.50), channel_id=1, source_target_pairs={{0,1},{1,2},{2,3},{3,4},{4,5},{5,6},{6,7},{7,0},{8,9},{9,10},{10,1... | collective-permute-start | bytes 1179656 | tf_op jit(solution)/shard_map/ppermute | solution.py:102
  86.1 13.6 %collective-permute-start.17 = (bf16[512,384]{1,0:T(8,128)(2,1)}, bf16[512,384]{1,0:T(8,128)(2,1)}, u32[]{:S(2)}, u32[]{:S(2)}) collective-permute-start(bf16[512,384]{1,0:T(8,128)(2,1)} %get-tuple-element.51), channel_id=1, source_target_pairs={{0,2},{1,3},{2,4},{3,5},{4,6},{5,7},{6,0},{7,1},{8,10},{9,11},{10,... | collective-permute-start | bytes 1179656 | tf_op jit(solution)/shard_map/ppermute | solution.py:102
  86.7 28.0 %collective-permute-start.18 = (bf16[512,384]{1,0:T(8,128)(2,1)}, bf16[512,384]{1,0:T(8,128)(2,1)}, u32[]{:S(2)}, u32[]{:S(2)}) collective-permute-start(bf16[512,384]{1,0:T(8,128)(2,1)} %get-tuple-element.52), channel_id=1, source_target_pairs={{0,3},{1,4},{2,5},{3,6},{4,7},{5,0},{6,1},{7,2},{8,11},{9,12},{10,... | collective-permute-start | bytes 1179656 | tf_op jit(solution)/shard_map/ppermute | solution.py:102
  88.1 27.9 %collective-permute-start.19 = (bf16[512,384]{1,0:T(8,128)(2,1)}, bf16[512,384]{1,0:T(8,128)(2,1)}, u32[]{:S(2)}, u32[]{:S(2)}) collective-permute-start(bf16[512,384]{1,0:T(8,128)(2,1)} %get-tuple-element.53), channel_id=1, source_target_pairs={{0,4},{1,5},{2,6},{3,7},{4,0},{5,1},{6,2},{7,3},{8,12},{9,13},{10,... | collective-permute-start | bytes 1179656 | tf_op jit(solution)/shard_map/ppermute | solution.py:102
  90.8 30.4 %collective-permute-start.20 = (bf16[512,384]{1,0:T(8,128)(2,1)}, bf16[512,384]{1,0:T(8,128)(2,1)}, u32[]{:S(2)}, u32[]{:S(2)}) collective-permute-start(bf16[512,384]{1,0:T(8,128)(2,1)} %get-tuple-element.54), channel_id=1, source_target_pairs={{0,5},{1,6},{2,7},{3,0},{4,1},{5,2},{6,3},{7,4},{8,13},{9,14},{10,... | collective-permute-start | bytes 1179656 | tf_op jit(solution)/shard_map/ppermute | solution.py:102
  98.4 22.8 %collective-permute-start.21 = (bf16[512,384]{1,0:T(8,128)(2,1)}, bf16[512,384]{1,0:T(8,128)(2,1)}, u32[]{:S(2)}, u32[]{:S(2)}) collective-permute-start(bf16[512,384]{1,0:T(8,128)(2,1)} %get-tuple-element.55), channel_id=1, source_target_pairs={{0,6},{1,7},{2,0},{3,1},{4,2},{5,3},{6,4},{7,5},{8,14},{9,15},{10,... | collective-permute-start | bytes 1179656 | tf_op jit(solution)/shard_map/ppermute | solution.py:102
  99.7 24.5 %collective-permute-start.22 = (bf16[512,384]{1,0:T(8,128)(2,1)}, bf16[512,384]{1,0:T(8,128)(2,1)}, u32[]{:S(2)}, u32[]{:S(2)}) collective-permute-start(bf16[512,384]{1,0:T(8,128)(2,1)} %get-tuple-element.56), channel_id=1, source_target_pairs={{0,7},{1,0},{2,1},{3,2},{4,3},{5,4},{6,5},{7,6},{8,15},{9,8},{10,9... | collective-permute-start | bytes 1179656 | tf_op jit(solution)/shard_map/ppermute | solution.py:102
  129.5 135.7 %all-to-all-start.3 = ((bf16[32,128,256]{2,1,0:T(8,128)(2,1)}), bf16[32,128,256]{2,1,0:T(8,128)(2,1)}, u32[]{:S(2)}, u32[]{:S(2)}) async-start(bf16[32,128,256]{2,1,0:T(8,128)(2,1)} %pick_kv.1), calls=%async_computation.3 | async-start | bytes 4194304 | tf_op jit(solution)/shard_map/all_to_all | solution.py:460
  140.1 49.7 %collective-permute-start.7 = (bf16[1,16,1024]{2,1,0:T(8,128)(2,1)S(1)}, bf16[1,16,1024]{2,1,0:T(8,128)(2,1)S(1)}, u32[]{:S(2)}, u32[]{:S(2)}) collective-permute-start(bf16[1,16,1024]{2,1,0:T(8,128)(2,1)S(1)} %get-tuple-element.61), channel_id=1, source_target_pairs={{0,8},{8,16},{16,24},{24,32},{32,40},{40,48},{48,56},{56,64},{64,7... | collective-permute-start | bytes 98312 | tf_op jit(solution)/shard_map/ppermute | solution.py:444
  143.4 46.4 %collective-permute-start.8 = (bf16[1,16,1024]{2,1,0:T(8,128)(2,1)S(1)}, bf16[1,16,1024]{2,1,0:T(8,128)(2,1)S(1)}, u32[]{:S(2)}, u32[]{:S(2)}) collective-permute-start(bf16[1,16,1024]{2,1,0:T(8,128)(2,1)S(1)} %get-tuple-element.62), channel_id=1, source_target_pairs={{8,0},{16,8},{24,16},{32,24},{40,32},{48,40},{56,48},{64,56},{72,6... | collective-permute-start | bytes 98312 | tf_op jit(solution)/shard_map/ppermute | solution.py:445
  199.4 14.9 %collective-permute-start.4 = (bf16[512,256]{1,0:T(8,128)(2,1)}, bf16[512,256]{1,0:T(8,128)(2,1)S(1)}, u32[]{:S(2)}, u32[]{:S(2)}) collective-permute-start(bf16[512,256]{1,0:T(8,128)(2,1)} %get-tuple-element.38), channel_id=1, source_target_pairs={{0,5},{1,6},{2,7},{3,0},{4,1},{5,2},{6,3},{7,4},{8,13},{9,14},{10,... | collective-permute-start | bytes 786440 | tf_op jit(solution)/shard_map/ppermute | solution.py:102
  199.9 17.4 %collective-permute-start.5 = (bf16[512,256]{1,0:T(8,128)(2,1)}, bf16[512,256]{1,0:T(8,128)(2,1)S(1)}, u32[]{:S(2)}, u32[]{:S(2)}) collective-permute-start(bf16[512,256]{1,0:T(8,128)(2,1)} %get-tuple-element.39), channel_id=1, source_target_pairs={{0,6},{1,7},{2,0},{3,1},{4,2},{5,3},{6,4},{7,5},{8,14},{9,15},{10,... | collective-permute-start | bytes 786440 | tf_op jit(solution)/shard_map/ppermute | solution.py:102
  210.9 11.5 %collective-permute-start.10 = (bf16[576,256]{1,0:T(8,128)(2,1)}, bf16[576,256]{1,0:T(8,128)(2,1)S(1)}, u32[]{:S(2)}, u32[]{:S(2)}) collective-permute-start(bf16[576,256]{1,0:T(8,128)(2,1)} %get-tuple-element.43), channel_id=1, source_target_pairs={{0,2},{1,3},{2,4},{3,5},{4,6},{5,7},{6,0},{7,1},{8,10},{9,11},{10,... | collective-permute-start | bytes 884744 | tf_op jit(solution)/shard_map/ppermute | solution.py:102
  211.1 14.0 %collective-permute-start.11 = (bf16[576,256]{1,0:T(8,128)(2,1)}, bf16[576,256]{1,0:T(8,128)(2,1)S(1)}, u32[]{:S(2)}, u32[]{:S(2)}) collective-permute-start(bf16[576,256]{1,0:T(8,128)(2,1)} %get-tuple-element.44), channel_id=1, source_target_pairs={{0,3},{1,4},{2,5},{3,6},{4,7},{5,0},{6,1},{7,2},{8,11},{9,12},{10,... | collective-permute-start | bytes 884744 | tf_op jit(solution)/shard_map/ppermute | solution.py:102
  212.1 25.5 %collective-permute-start.12 = (bf16[576,256]{1,0:T(8,128)(2,1)}, bf16[576,256]{1,0:T(8,128)(2,1)S(1)}, u32[]{:S(2)}, u32[]{:S(2)}) collective-permute-start(bf16[576,256]{1,0:T(8,128)(2,1)} %get-tuple-element.45), channel_id=1, source_target_pairs={{0,4},{1,5},{2,6},{3,7},{4,0},{5,1},{6,2},{7,3},{8,12},{9,13},{10,... | collective-permute-start | bytes 884744 | tf_op jit(solution)/shard_map/ppermute | solution.py:102
  214.3 50.9 %copy-start.8 = (bf16[512,256]{1,0:T(8,128)(2,1)}, bf16[512,256]{1,0:T(8,128)(2,1)S(1)}, u32[]{:S(2)}) copy-start(bf16[512,256]{1,0:T(8,128)(2,1)S(1)} %collective-permute-done.4) | copy-start | bytes 786436
  214.3 23.4 %collective-permute-start.13 = (bf16[576,256]{1,0:T(8,128)(2,1)}, bf16[576,256]{1,0:T(8,128)(2,1)}, u32[]{:S(2)}, u32[]{:S(2)}) collective-permute-start(bf16[576,256]{1,0:T(8,128)(2,1)} %get-tuple-element.46), channel_id=1, source_target_pairs={{0,5},{1,6},{2,7},{3,0},{4,1},{5,2},{6,3},{7,4},{8,13},{9,14},{10,... | collective-permute-start | bytes 884744 | tf_op jit(solution)/shard_map/ppermute | solution.py:102
  217.2 48.0 %copy-start.9 = (bf16[512,256]{1,0:T(8,128)(2,1)}, bf16[512,256]{1,0:T(8,128)(2,1)S(1)}, u32[]{:S(2)}) copy-start(bf16[512,256]{1,0:T(8,128)(2,1)S(1)} %collective-permute-done.5) | copy-start | bytes 786436
  217.2 20.9 %collective-permute-start.14 = (bf16[576,256]{1,0:T(8,128)(2,1)}, bf16[576,256]{1,0:T(8,128)(2,1)}, u32[]{:S(2)}, u32[]{:S(2)}) collective-permute-start(bf16[576,256]{1,0:T(8,128)(2,1)} %get-tuple-element.47), channel_id=1, source_target_pairs={{0,6},{1,7},{2,0},{3,1},{4,2},{5,3},{6,4},{7,5},{8,14},{9,15},{10,... | collective-permute-start | bytes 884744 | tf_op jit(solution)/shard_map/ppermute | solution.py:102
  222.4 24.1 %copy-start.5 = (bf16[576,256]{1,0:T(8,128)(2,1)}, bf16[576,256]{1,0:T(8,128)(2,1)S(1)}, u32[]{:S(2)}) copy-start(bf16[576,256]{1,0:T(8,128)(2,1)S(1)} %collective-permute-done.10.refs_10_) | copy-start | bytes 884740
  222.4 18.2 %collective-permute-start.15 = (bf16[576,256]{1,0:T(8,128)(2,1)}, bf16[576,256]{1,0:T(8,128)(2,1)}, u32[]{:S(2)}, u32[]{:S(2)}) collective-permute-start(bf16[576,256]{1,0:T(8,128)(2,1)} %get-tuple-element.48), channel_id=1, source_target_pairs={{0,7},{1,0},{2,1},{3,2},{4,3},{5,4},{6,5},{7,6},{8,15},{9,8},{10,9... | collective-permute-start | bytes 884744 | tf_op jit(solution)/shard_map/ppermute | solution.py:102
  225.2 21.3 %copy-start.6 = (bf16[576,256]{1,0:T(8,128)(2,1)}, bf16[576,256]{1,0:T(8,128)(2,1)S(1)}, u32[]{:S(2)}) copy-start(bf16[576,256]{1,0:T(8,128)(2,1)S(1)} %collective-permute-done.11.refs_11_) | copy-start | bytes 884740
  225.2 16.4 %collective-permute-start.9 = (bf16[576,256]{1,0:T(8,128)(2,1)}, bf16[576,256]{1,0:T(8,128)(2,1)}, u32[]{:S(2)}, u32[]{:S(2)}) collective-permute-start(bf16[576,256]{1,0:T(8,128)(2,1)} %get-tuple-element.42), channel_id=1, source_target_pairs={{0,1},{1,2},{2,3},{3,4},{4,5},{5,6},{6,7},{7,0},{8,9},{9,10},{10,1... | collective-permute-start | bytes 884744 | tf_op jit(solution)/shard_map/ppermute | solution.py:102
  237.6 8.9 %copy-start.7 = (bf16[576,256]{1,0:T(8,128)(2,1)}, bf16[576,256]{1,0:T(8,128)(2,1)S(1)}, u32[]{:S(2)}) copy-start(bf16[576,256]{1,0:T(8,128)(2,1)S(1)} %collective-permute-done.12.refs_12_) | copy-start | bytes 884740
  237.6 27.5 %collective-permute-start.6 = (bf16[512,256]{1,0:T(8,128)(2,1)}, bf16[512,256]{1,0:T(8,128)(2,1)}, u32[]{:S(2)}, u32[]{:S(2)}) collective-permute-start(bf16[512,256]{1,0:T(8,128)(2,1)} %get-tuple-element.40), channel_id=1, source_target_pairs={{0,7},{1,0},{2,1},{3,2},{4,3},{5,4},{6,5},{7,6},{8,15},{9,8},{10,9... | collective-permute-start | bytes 786440 | tf_op jit(solution)/shard_map/ppermute | solution.py:102
  237.6 27.5 %collective-permute-start = (bf16[512,256]{1,0:T(8,128)(2,1)}, bf16[512,256]{1,0:T(8,128)(2,1)}, u32[]{:S(2)}, u32[]{:S(2)}) collective-permute-start(bf16[512,256]{1,0:T(8,128)(2,1)} %get-tuple-element.34), channel_id=1, source_target_pairs={{0,1},{1,2},{2,3},{3,4},{4,5},{5,6},{6,7},{7,0},{8,9},{9,10},{10,1... | collective-permute-start | bytes 786440 | tf_op jit(solution)/shard_map/ppermute | solution.py:102
  238.1 27.0 %collective-permute-start.1 = (bf16[512,256]{1,0:T(8,128)(2,1)}, bf16[512,256]{1,0:T(8,128)(2,1)}, u32[]{:S(2)}, u32[]{:S(2)}) collective-permute-start(bf16[512,256]{1,0:T(8,128)(2,1)} %get-tuple-element.35), channel_id=1, source_target_pairs={{0,2},{1,3},{2,4},{3,5},{4,6},{5,7},{6,0},{7,1},{8,10},{9,11},{10,... | collective-permute-start | bytes 786440 | tf_op jit(solution)/shard_map/ppermute | solution.py:102
  240.6 24.5 %collective-permute-start.2 = (bf16[512,256]{1,0:T(8,128)(2,1)}, bf16[512,256]{1,0:T(8,128)(2,1)}, u32[]{:S(2)}, u32[]{:S(2)}) collective-permute-start(bf16[512,256]{1,0:T(8,128)(2,1)} %get-tuple-element.36), channel_id=1, source_target_pairs={{0,3},{1,4},{2,5},{3,6},{4,7},{5,0},{6,1},{7,2},{8,11},{9,12},{10,... | collective-permute-start | bytes 786440 | tf_op jit(solution)/shard_map/ppermute | solution.py:102
  241.6 23.6 %collective-permute-start.3 = (bf16[512,256]{1,0:T(8,128)(2,1)}, bf16[512,256]{1,0:T(8,128)(2,1)}, u32[]{:S(2)}, u32[]{:S(2)}) collective-permute-start(bf16[512,256]{1,0:T(8,128)(2,1)} %get-tuple-element.37), channel_id=1, source_target_pairs={{0,4},{1,5},{2,6},{3,7},{4,0},{5,1},{6,2},{7,3},{8,12},{9,13},{10,... | collective-permute-start | bytes 786440 | tf_op jit(solution)/shard_map/ppermute | solution.py:102
  (4 other events, 15.9 us)

commit v5 on v4

--- a/solution.py
+++ b/solution.py
@@ -23,6 +23,7 @@
 def project_kernel(here_ref, *refs, sources, weights, groups, place):
     x_refs, rest = refs[:sources], refs[sources:]
     w_refs, o_refs, x_ref = rest[:weights], rest[weights : weights + groups], rest[-1]
+    e_refs = rest[weights + groups : -1]
     step = pl.program_id(0)
 
     @pl.when(step == 0)
@@ -35,7 +36,9 @@
 
         @pl.when(step == o)
         def _():
-            o_ref[...] = r
+            o_ref[...] = r[: o_ref.shape[0]]
+            if e_refs:
+                e_refs[o][...] = r[o_ref.shape[0] :]
 
 
 def place_rows(x_ref, rows_ref):
@@ -66,10 +69,12 @@
         x_ref[row : row + SUB, lane : lane + lanes] = got_ref[b, tall - SUB :, :]
 
 
-def project(here, xs, rows, ws, groups, place):
+def project(here, xs, rows, ws, groups, place, extra=0):
     width = ws[0].shape[0]
     lanes = ws[0].shape[1] // groups
     out_lanes = lanes * len(ws)
+    outs = [(rows, out_lanes)] * groups + [(extra, out_lanes)] * (groups if extra else 0)
+    rows = rows + extra
     return pl.pallas_call(
         functools.partial(
             project_kernel, sources=len(xs), weights=len(ws), groups=groups, place=place
@@ -84,10 +89,10 @@
                 pl.BlockSpec((width, lanes), lambda o, here: (0, lax.rem(here[0] + o, groups)))
                 for _ in ws
             ],
-            out_specs=[pl.BlockSpec((rows, out_lanes), lambda o, here: (0, 0))] * groups,
+            out_specs=[pl.BlockSpec(out, lambda o, here: (0, 0)) for out in outs],
             scratch_shapes=[pltpu.VMEM((rows, width), jnp.bfloat16)],
         ),
-        out_shape=[jax.ShapeDtypeStruct((rows, out_lanes), jnp.bfloat16)] * groups,
+        out_shape=[jax.ShapeDtypeStruct(out, jnp.bfloat16) for out in outs],
         cost_estimate=pl.CostEstimate(
             flops=2 * rows * width * lanes * len(ws) * groups,
             transcendentals=0,
@@ -272,13 +277,12 @@
         qo_ref[rows, :] = q
 
 
-def local_attention(place, own, ext, ext_rows, per_step=2):
+def local_attention(place, own, ext, per_step=4):
     groups = len(own)
     rows = own[0].shape[0] * groups
     both = ext[0].shape[1]
     lanes = both // 2
     block = pl.BlockSpec((per_step * TILE, lanes), lambda i, s: (i, 0))
-    last = ext[0].shape[0] // ext_rows - 1
     out = jax.ShapeDtypeStruct((rows, lanes), jnp.float32)
     keys = (3 + GLOBALS) * TILE
     return pl.pallas_call(
@@ -287,7 +291,7 @@
             num_scalar_prefetch=1,
             grid=(rows // (per_step * TILE),),
             in_specs=[pl.BlockSpec(a.shape, lambda i, s: (0, 0)) for a in own]
-            + [pl.BlockSpec((ext_rows, both), lambda i, s: (last, 0)) for _ in ext],
+            + [pl.BlockSpec(a.shape, lambda i, s: (0, 0)) for a in ext],
             out_specs=[block] * 4,
             scratch_shapes=[
                 pltpu.VMEM((rows, lanes), jnp.bfloat16),
@@ -451,16 +455,18 @@
         got = lax.all_to_all(chunks, "ctx", split_axis=0, concat_axis=0, tiled=True)
         count = ctx_count * part
         if slot == 0:
-            xs, place = [got], place_chunks
+            xs, place, extra = [got], place_chunks, 0
         else:
-            xs, place, count = [got, edges], place_chunks_and_edges, count + (2 + GLOBALS) * part
-        projected = project(head, xs, count, [w_key, w_value], groups, place)
-        fetched.append(exchange(projected, "head"))
+            xs, place, extra = [got, edges], place_chunks_and_edges, (2 + GLOBALS) * part
+        projected = project(head, xs, count, [w_key, w_value], groups, place, extra)
+        if extra:
+            ends = exchange(projected[groups:], "head")
+        fetched.append(exchange(projected[:groups], "head"))
     chosen = pick_kv(send[CAP - 1], head, own, ctx_count)
     whole = lax.all_to_all(chosen, "ctx", split_axis=0, concat_axis=0, tiled=True)
 
     where = jnp.stack([shard, jnp.int32(tiles_here * ctx_count), here])
-    m, l, a, q = local_attention(where, own, fetched[1], (2 + GLOBALS) * part)
+    m, l, a, q = local_attention(where, own, ends)
     my_count = lax.dynamic_slice_in_dim(random_count, shard * tiles_here, tiles_here, 0)
     attended = random_attention(read, my_count, q, fetched, [whole], m, l, a)
     attended = attended.reshape(groups, rows, -1)

time: 320 us -> 306 us (0.956)
  the two profiles are of different devices: /device:TPU:160 before, /device:TPU:6 now
where the time goes in v5:
time: 306 us; the launch traced here: 305 us
  Pallas kernels  88.5 us (29%)
  waiting for transfers between devices  70.9 us (23%)
  starting transfers between devices  68.1 us (22%)
  blocking collectives  61.6 us (20%)
  local copies, waits for them, and re-layouts  8.79 us (3%)
  other arithmetic  4.39 us (1%)
    ppermute x28, starting transfers between devices, exchange(): lax.ppermute(pieces[o], axis, [(i, (i + o) % size) for i in range(size)])  42.4 us
    all_to_all x1, blocking collectives, body(): got = lax.all_to_all(chunks, 'ctx', split_axis=0, concat_axis=0, tiled=True)  41.5 us
    pallas_call x1, Pallas kernels, random_attention(): pl.pallas_call(functools.partial(random_kernel, groups=groups, spread=spr...  31.9 us
    ppermute x28, waiting for transfers between devices, exchange(): lax.ppermute(pieces[o], axis, [(i, (i + o) % size) for i in range(size)])  29.3 us
    pallas_call x3, Pallas kernels, project(): pl.pallas_call(functools.partial(project_kernel, sources=len(xs), weights...  29.1 us
    ppermute x1, waiting for transfers between devices, body(): before = lax.ppermute(striped[-1:], 'ctx', up)  26.8 us
    all_to_all x1, blocking collectives, body(): lax.all_to_all(attended, 'head', split_axis=0, concat_axis=0, tiled=True)  20.2 us
    pallas_call x1, Pallas kernels, local_attention(): pl.pallas_call(functools.partial(local_kernel, groups=groups), grid_spec=...  16.8 us
  transfers between devices with their start and end apart: 33, of which 10 were waited for; matrix products, arithmetic and copies ran while one was open for 3% of the time, Pallas kernels for 16%

profile of v5, /device:TPU:6, one launch (start us, length us, event | category | flops | bytes accessed | tf_op | source)
XLA Modules:
  0.0 304.9 jit_solution(14922579964236945094)
XLA Ops:
  0.0 2.5 copy.14
  2.5 4.5 %all-to-all-start = ((bf16[8,4,16,1024]{3,2,1,0:T(8,128)(2,1)}), bf16[8,4,16,1024]{3,2,1,0:T(8,128)(2,1)S(1)}, u32[]{:S(2)}, u32[]{:S(2)}) async-start(bf16[8,4,16,1024]{3,2,1,0:T(8,128)(2,1)} %bitcast.40), calls=%async_computation | async-start | bytes 2097152 | tf_op jit(solution)/shard_map/all_to_all | solution.py:438
  11.4 11.5 %all-to-all-done = bf16[8,4,16,1024]{3,2,1,0:T(8,128)(2,1)S(1)} async-done(((bf16[8,4,16,1024]{3,2,1,0:T(8,128)(2,1)}), bf16[8,4,16,1024]{3,2,1,0:T(8,128)(2,1)S(1)}, u32[]{:S(2)}, u32[]{:S(2)}) %all-to-all-start) | async-done | bytes 1048608 | tf_op jit(solution)/shard_map/all_to_all | solution.py:438
  23.8 3.2 %shard_map.73 = bf16[32,136,128]{2,1,0:T(8,128)(2,1)} custom-call(s32[32]{0:T(128)} %get-tuple-element.81.index_ref, bf16[32,16,1024]{2,1,0:T(8,128)(2,1)} %bitcast.37), custom_call_target="tpu_custom_call" | custom-call | bytes 4194304 | tf_op jit(solution)/shard_map/pallas_call | solution.py:159
  27.1 41.5 %all_to_all.25.refs_0_.root_ref = bf16[32,136,128]{2,1,0:T(8,128)(2,1)} all-to-all(bf16[32,136,128]{2,1,0:T(8,128)(2,1)} %shard_map.73), channel_id=1, replica_groups=mesh['ctx'=32,'head'=8] {'ctx'}, dimensions={0} | all-to-all | bytes 2228224 | tf_op jit(solution)/shard_map/all_to_all | solution.py:455
  68.5 3.2 %shard_map.75 = bf16[32,136,128]{2,1,0:T(8,128)(2,1)} custom-call(s32[32]{0:T(128)} %get-tuple-element.80.index_ref, bf16[32,16,1024]{2,1,0:T(8,128)(2,1)} %bitcast.38, bf16[32,136,128]{2,1,0:T(8,128)(2,1)} %all_to_all.25.refs_0_.root_ref), custom_call_target="tpu_custom_call" | custom-call | bytes 4194304 | tf_op jit(solution)/shard_map/pallas_call | solution.py:159
  71.8 5.5 %all-to-all-start.2 = ((bf16[32,136,128]{2,1,0:T(8,128)(2,1)}), bf16[32,136,128]{2,1,0:T(8,128)(2,1)S(1)}, u32[]{:S(2)}, u32[]{:S(2)}) async-start(bf16[32,136,128]{2,1,0:T(8,128)(2,1)} %shard_map.75), calls=%async_computation.2 | async-start | bytes 2228224 | tf_op jit(solution)/shard_map/all_to_all | solution.py:455
  77.2 10.9 %shard_map.77 = (bf16[512,384]{1,0:T(8,128)(2,1)}, bf16[512,384]{1,0:T(8,128)(2,1)}, bf16[512,384]{1,0:T(8,128)(2,1)}, bf16[512,384]{1,0:T(8,128)(2,1)}, bf16[51...) custom-call(s32[1]{0:T(128)} %bitcast.here_ref, ...), custom_call_target="tpu_custom_call" | custom-call | flops 3221225472 | bytes 10485760 | tf_op jit(solution)/shard_map/pallas_call | solution.py:78
  90.2 2.7 collective-permute-start.19
  93.8 6.6 %collective-permute-done.16.refs_1_ = bf16[512,384]{1,0:T(8,128)(2,1)} collective-permute-done((bf16[512,384]{1,0:T(8,128)(2,1)}, bf16[512,384]{1,0:T(8,128)(2,1)}, u32[]{:S(2)}, u32[]{:S(2)}) %collective-permute-start.16) | collective-permute-done | bytes 393248 | tf_op jit(solution)/shard_map/ppermute | solution.py:107
  101.7 6.8 %collective-permute-start.22 = (bf16[512,384]{1,0:T(8,128)(2,1)}, bf16[512,384]{1,0:T(8,128)(2,1)}, u32[]{:S(2)}, u32[]{:S(2)}) collective-permute-start(bf16[512,384]{1,0:T(8,128)(2,1)} %get-tuple-element.64), channel_id=1, source_target_pairs={{0,7},{1,0},{2,1},{3,2},{4,3},{5,4},{6,5},{7,6},{8,15},{9,8},{10,9... | collective-permute-start | bytes 1179656 | tf_op jit(solution)/shard_map/ppermute | solution.py:107
  108.5 8.2 %collective-permute-done.18.refs_3_ = bf16[512,384]{1,0:T(8,128)(2,1)} collective-permute-done((bf16[512,384]{1,0:T(8,128)(2,1)}, bf16[512,384]{1,0:T(8,128)(2,1)}, u32[]{:S(2)}, u32[]{:S(2)}) %collective-permute-start.18) | collective-permute-done | bytes 393248 | tf_op jit(solution)/shard_map/ppermute | solution.py:107
  118.1 5.2 %collective-permute-done.20.refs_5_ = bf16[512,384]{1,0:T(8,128)(2,1)} collective-permute-done((bf16[512,384]{1,0:T(8,128)(2,1)}, bf16[512,384]{1,0:T(8,128)(2,1)}, u32[]{:S(2)}, u32[]{:S(2)}) %collective-permute-start.20) | collective-permute-done | bytes 393248 | tf_op jit(solution)/shard_map/ppermute | solution.py:107
  123.2 3.0 collective-permute-done.22.refs_7_
  126.3 4.2 %pick_kv.1 = bf16[32,128,256]{2,1,0:T(8,128)(2,1)} custom-call(s32[32]{0:T(128)} %get-tuple-element.79.index_ref, s32[1]{0:T(128)} %bitcast.here_ref, bf16[512,384]{1,0:T(8,128)(2,1)} %get-tuple-element.57.refs_0_, bf16[512,384]{1,0:T(8,128)(2,1)} %collective-permute-done.16.refs_1_, bf16[512,384]{1,0:T(8,128)(2,1)} %collective-permute-done.17.refs_2_, ...), custom_call_target="tpu_custom_call" | custom-call | bytes 5242880 | tf_op jit(solution)/shard_map/pick_kv/pallas_call | solution.py:191
  131.5 9.9 %all-to-all-start.3 = ((bf16[32,128,256]{2,1,0:T(8,128)(2,1)}), bf16[32,128,256]{2,1,0:T(8,128)(2,1)}, u32[]{:S(2)}, u32[]{:S(2)}) async-start(bf16[32,128,256]{2,1,0:T(8,128)(2,1)} %pick_kv.1), calls=%async_computation.3 | async-start | bytes 4194304 | tf_op jit(solution)/shard_map/all_to_all | solution.py:466
  142.3 3.4 %collective-permute-start.7 = (bf16[1,16,1024]{2,1,0:T(8,128)(2,1)S(1)}, bf16[1,16,1024]{2,1,0:T(8,128)(2,1)S(1)}, u32[]{:S(2)}, u32[]{:S(2)}) collective-permute-start(bf16[1,16,1024]{2,1,0:T(8,128)(2,1)S(1)} %get-tuple-element.77), channel_id=1, source_target_pairs={{0,8},{8,16},{16,24},{24,32},{32,40},{40,48},{48,56},{56,64},{64,7... | collective-permute-start | bytes 98312 | tf_op jit(solution)/shard_map/ppermute | solution.py:448
  145.6 2.5 collective-permute-start.8
  148.1 8.9 %shard_map.74 = (bf16[512,256]{1,0:T(8,128)(2,1)}, bf16[512,256]{1,0:T(8,128)(2,1)}, bf16[512,256]{1,0:T(8,128)(2,1)}, bf16[512,256]{1,0:T(8,128)(2,1)}, bf16[51...) custom-call(s32[1]{0:T(128)} %bitcast.here_ref, ...), custom_call_target="tpu_custom_call" | custom-call | flops 2147483648 | bytes 7340032 | tf_op jit(solution)/shard_map/pallas_call | solution.py:78
  159.7 26.8 %collective-permute-done.7 = bf16[1,16,1024]{2,1,0:T(8,128)(2,1)S(1)} collective-permute-done((bf16[1,16,1024]{2,1,0:T(8,128)(2,1)S(1)}, bf16[1,16,1024]{2,1,0:T(8,128)(2,1)S(1)}, u32[]{:S(2)}, u32[]{:S(2)}) %collective-permute-start.7) | collective-permute-done | bytes 32800 | tf_op jit(solution)/shard_map/ppermute | solution.py:448
  186.5 3.4 %collective-permute-done.8 = bf16[1,16,1024]{2,1,0:T(8,128)(2,1)S(1)} collective-permute-done((bf16[1,16,1024]{2,1,0:T(8,128)(2,1)S(1)}, bf16[1,16,1024]{2,1,0:T(8,128)(2,1)S(1)}, u32[]{:S(2)}, u32[]{:S(2)}) %collective-permute-start.8) | collective-permute-done | bytes 32800 | tf_op jit(solution)/shard_map/ppermute | solution.py:449
  191.3 3.9 %collective-permute-start.3 = (bf16[512,256]{1,0:T(8,128)(2,1)}, bf16[512,256]{1,0:T(8,128)(2,1)}, u32[]{:S(2)}, u32[]{:S(2)}) collective-permute-start(bf16[512,256]{1,0:T(8,128)(2,1)} %get-tuple-element.45), channel_id=1, source_target_pairs={{0,4},{1,5},{2,6},{3,7},{4,0},{5,1},{6,2},{7,3},{8,12},{9,13},{10,... | collective-permute-start | bytes 786440 | tf_op jit(solution)/shard_map/ppermute | solution.py:107
  195.2 9.3 %shard_map.76 = (bf16[512,256]{1,0:T(8,128)(2,1)}, bf16[512,256]{1,0:T(8,128)(2,1)}, bf16[512,256]{1,0:T(8,128)(2,1)}, bf16[512,256]{1,0:T(8,128)(2,1)}, bf16[51...) custom-call(s32[1]{0:T(128)} %bitcast.here_ref, ...), custom_call_target="tpu_custom_call" | custom-call | flops 2415919104 | bytes 7733248 | tf_op jit(solution)/shard_map/pallas_call | solution.py:78
  205.0 2.9 collective-permute-start.25
  207.9 7.3 %collective-permute-start.26 = (bf16[64,256]{1,0:T(8,128)(2,1)}, bf16[64,256]{1,0:T(8,128)(2,1)S(1)}, u32[]{:S(2)}, u32[]{:S(2)}) collective-permute-start(bf16[64,256]{1,0:T(8,128)(2,1)} %get-tuple-element.69), channel_id=1, source_target_pairs={{0,4},{1,5},{2,6},{3,7},{4,0},{5,1},{6,2},{7,3},{8,12},{9,13},{10,... | collective-permute-start | bytes 98312 | tf_op jit(solution)/shard_map/ppermute | solution.py:107
  215.5 2.6 collective-permute-start.10
  222.2 3.6 %collective-permute-done.27.refs_13_ = bf16[64,256]{1,0:T(8,128)(2,1)S(1)} collective-permute-done((bf16[64,256]{1,0:T(8,128)(2,1)}, bf16[64,256]{1,0:T(8,128)(2,1)S(1)}, u32[]{:S(2)}, u32[]{:S(2)}) %collective-permute-start.27) | collective-permute-done | bytes 32800 | tf_op jit(solution)/shard_map/ppermute | solution.py:107
  225.8 2.3 collective-permute-start.12
  229.6 2.5 collective-permute-start.14
  233.7 16.8 %local_attention.1 = (f32[4096,128]{1,0:T(8,128)}, f32[4096,128]{1,0:T(8,128)}, f32[4096,128]{1,0:T(8,128)}, bf16[4096,128]{1,0:T(8,128)(2,1)}) custom-call(s32[3]{0:T(128)} %pad_add_fusion.place_ref, bf16[512,384]{1,0:T(8,128)(2,1)} %get-tuple-element.57.refs_0_, bf16[512,384]{1,0:T(8,128)(2,1)} %collective-permute-done.16.refs_1_, ...), custom_call_target="tpu_custom_call" | custom-call | flops 2684354560 | bytes 10485760 | tf_op jit(solution)/shard_map/local_attention/pallas_call | solution.py:288
  250.6 31.9 %random_attention.1 = bf16[4096,128]{1,0:T(8,128)(2,1)} custom-call(s32[384]{0:T(512)} %add_select_fusion.1.index_ref, s32[32]{0:T(128)} %dynamic_slice.8.count_ref, bf16[32,16,256]{2,1,0:T(8,128)(2,1)} %bitcast.50, bf16[32,16,256]{2,1,0:T(8,128)(2,1)} %bitcast.47, bf16[32,16,256]{2,1,0:T(8,128)(2,1)} %bitcast.7.refs_2_, ...), custom_call_target="tpu_custom_call" | custom-call | flops 6442450944 | bytes 14680064 | tf_op jit(solution)/shard_map/random_attention/pallas_call | solution.py:380
  282.5 20.2 %all_to_all.26 = bf16[8,512,128]{2,1,0:T(8,128)(2,1)S(1)} all-to-all(bf16[8,512,128]{2,1,0:T(8,128)(2,1)} %bitcast.42), channel_id=1, replica_groups=mesh['ctx'=32,'head'=8] {'head'}, dimensions={0} | all-to-all | bytes 2097152 | tf_op jit(solution)/shard_map/all_to_all | solution.py:473
  (100 shorter events, 27.0 us)
Async XLA Ops:
  2.5 20.4 %all-to-all-start = ((bf16[8,4,16,1024]{3,2,1,0:T(8,128)(2,1)}), bf16[8,4,16,1024]{3,2,1,0:T(8,128)(2,1)S(1)}, u32[]{:S(2)}, u32[]{:S(2)}) async-start(bf16[8,4,16,1024]{3,2,1,0:T(8,128)(2,1)} %bitcast.40), calls=%async_computation | async-start | bytes 2097152 | tf_op jit(solution)/shard_map/all_to_all | solution.py:438
  71.8 58.8 %all-to-all-start.2 = ((bf16[32,136,128]{2,1,0:T(8,128)(2,1)}), bf16[32,136,128]{2,1,0:T(8,128)(2,1)S(1)}, u32[]{:S(2)}, u32[]{:S(2)}) async-start(bf16[32,136,128]{2,1,0:T(8,128)(2,1)} %shard_map.75), calls=%async_computation.2 | async-start | bytes 2228224 | tf_op jit(solution)/shard_map/all_to_all | solution.py:455
  88.1 12.3 %collective-permute-start.16 = (bf16[512,384]{1,0:T(8,128)(2,1)}, bf16[512,384]{1,0:T(8,128)(2,1)}, u32[]{:S(2)}, u32[]{:S(2)}) collective-permute-start(bf16[512,384]{1,0:T(8,128)(2,1)} %get-tuple-element.58), channel_id=1, source_target_pairs={{0,1},{1,2},{2,3},{3,4},{4,5},{5,6},{6,7},{7,0},{8,9},{9,10},{10,1... | collective-permute-start | bytes 1179656 | tf_op jit(solution)/shard_map/ppermute | solution.py:107
  88.2 13.6 %collective-permute-start.17 = (bf16[512,384]{1,0:T(8,128)(2,1)}, bf16[512,384]{1,0:T(8,128)(2,1)}, u32[]{:S(2)}, u32[]{:S(2)}) collective-permute-start(bf16[512,384]{1,0:T(8,128)(2,1)} %get-tuple-element.59), channel_id=1, source_target_pairs={{0,2},{1,3},{2,4},{3,5},{4,6},{5,7},{6,0},{7,1},{8,10},{9,11},{10,... | collective-permute-start | bytes 1179656 | tf_op jit(solution)/shard_map/ppermute | solution.py:107
  88.8 28.0 %collective-permute-start.18 = (bf16[512,384]{1,0:T(8,128)(2,1)}, bf16[512,384]{1,0:T(8,128)(2,1)}, u32[]{:S(2)}, u32[]{:S(2)}) collective-permute-start(bf16[512,384]{1,0:T(8,128)(2,1)} %get-tuple-element.60), channel_id=1, source_target_pairs={{0,3},{1,4},{2,5},{3,6},{4,7},{5,0},{6,1},{7,2},{8,11},{9,12},{10,... | collective-permute-start | bytes 1179656 | tf_op jit(solution)/shard_map/ppermute | solution.py:107
  90.2 27.9 %collective-permute-start.19 = (bf16[512,384]{1,0:T(8,128)(2,1)}, bf16[512,384]{1,0:T(8,128)(2,1)}, u32[]{:S(2)}, u32[]{:S(2)}) collective-permute-start(bf16[512,384]{1,0:T(8,128)(2,1)} %get-tuple-element.61), channel_id=1, source_target_pairs={{0,4},{1,5},{2,6},{3,7},{4,0},{5,1},{6,2},{7,3},{8,12},{9,13},{10,... | collective-permute-start | bytes 1179656 | tf_op jit(solution)/shard_map/ppermute | solution.py:107
  92.9 30.4 %collective-permute-start.20 = (bf16[512,384]{1,0:T(8,128)(2,1)}, bf16[512,384]{1,0:T(8,128)(2,1)}, u32[]{:S(2)}, u32[]{:S(2)}) collective-permute-start(bf16[512,384]{1,0:T(8,128)(2,1)} %get-tuple-element.62), channel_id=1, source_target_pairs={{0,5},{1,6},{2,7},{3,0},{4,1},{5,2},{6,3},{7,4},{8,13},{9,14},{10,... | collective-permute-start | bytes 1179656 | tf_op jit(solution)/shard_map/ppermute | solution.py:107
  100.4 22.8 %collective-permute-start.21 = (bf16[512,384]{1,0:T(8,128)(2,1)}, bf16[512,384]{1,0:T(8,128)(2,1)}, u32[]{:S(2)}, u32[]{:S(2)}) collective-permute-start(bf16[512,384]{1,0:T(8,128)(2,1)} %get-tuple-element.63), channel_id=1, source_target_pairs={{0,6},{1,7},{2,0},{3,1},{4,2},{5,3},{6,4},{7,5},{8,14},{9,15},{10,... | collective-permute-start | bytes 1179656 | tf_op jit(solution)/shard_map/ppermute | solution.py:107
  101.7 24.5 %collective-permute-start.22 = (bf16[512,384]{1,0:T(8,128)(2,1)}, bf16[512,384]{1,0:T(8,128)(2,1)}, u32[]{:S(2)}, u32[]{:S(2)}) collective-permute-start(bf16[512,384]{1,0:T(8,128)(2,1)} %get-tuple-element.64), channel_id=1, source_target_pairs={{0,7},{1,0},{2,1},{3,2},{4,3},{5,4},{6,5},{7,6},{8,15},{9,8},{10,9... | collective-permute-start | bytes 1179656 | tf_op jit(solution)/shard_map/ppermute | solution.py:107
  131.5 119.0 %all-to-all-start.3 = ((bf16[32,128,256]{2,1,0:T(8,128)(2,1)}), bf16[32,128,256]{2,1,0:T(8,128)(2,1)}, u32[]{:S(2)}, u32[]{:S(2)}) async-start(bf16[32,128,256]{2,1,0:T(8,128)(2,1)} %pick_kv.1), calls=%async_computation.3 | async-start | bytes 4194304 | tf_op jit(solution)/shard_map/all_to_all | solution.py:466
  142.3 44.2 %collective-permute-start.7 = (bf16[1,16,1024]{2,1,0:T(8,128)(2,1)S(1)}, bf16[1,16,1024]{2,1,0:T(8,128)(2,1)S(1)}, u32[]{:S(2)}, u32[]{:S(2)}) collective-permute-start(bf16[1,16,1024]{2,1,0:T(8,128)(2,1)S(1)} %get-tuple-element.77), channel_id=1, source_target_pairs={{0,8},{8,16},{16,24},{24,32},{32,40},{40,48},{48,56},{56,64},{64,7... | collective-permute-start | bytes 98312 | tf_op jit(solution)/shard_map/ppermute | solution.py:448
  145.6 44.3 %collective-permute-start.8 = (bf16[1,16,1024]{2,1,0:T(8,128)(2,1)S(1)}, bf16[1,16,1024]{2,1,0:T(8,128)(2,1)S(1)}, u32[]{:S(2)}, u32[]{:S(2)}) collective-permute-start(bf16[1,16,1024]{2,1,0:T(8,128)(2,1)S(1)} %get-tuple-element.78), channel_id=1, source_target_pairs={{8,0},{16,8},{24,16},{32,24},{40,32},{48,40},{56,48},{64,56},{72,6... | collective-permute-start | bytes 98312 | tf_op jit(solution)/shard_map/ppermute | solution.py:449
  157.0 33.5 %collective-permute-start.4 = (bf16[512,256]{1,0:T(8,128)(2,1)}, bf16[512,256]{1,0:T(8,128)(2,1)S(1)}, u32[]{:S(2)}, u32[]{:S(2)}) collective-permute-start(bf16[512,256]{1,0:T(8,128)(2,1)} %get-tuple-element.46), channel_id=1, source_target_pairs={{0,5},{1,6},{2,7},{3,0},{4,1},{5,2},{6,3},{7,4},{8,13},{9,14},{10,... | collective-permute-start | bytes 786440 | tf_op jit(solution)/shard_map/ppermute | solution.py:107
  157.2 34.1 %collective-permute-start.5 = (bf16[512,256]{1,0:T(8,128)(2,1)}, bf16[512,256]{1,0:T(8,128)(2,1)S(1)}, u32[]{:S(2)}, u32[]{:S(2)}) collective-permute-start(bf16[512,256]{1,0:T(8,128)(2,1)} %get-tuple-element.47), channel_id=1, source_target_pairs={{0,6},{1,7},{2,0},{3,1},{4,2},{5,3},{6,4},{7,5},{8,14},{9,15},{10,... | collective-permute-start | bytes 786440 | tf_op jit(solution)/shard_map/ppermute | solution.py:107
  159.3 45.3 %collective-permute-start.6 = (bf16[512,256]{1,0:T(8,128)(2,1)}, bf16[512,256]{1,0:T(8,128)(2,1)S(1)}, u32[]{:S(2)}, u32[]{:S(2)}) collective-permute-start(bf16[512,256]{1,0:T(8,128)(2,1)} %get-tuple-element.48), channel_id=1, source_target_pairs={{0,7},{1,0},{2,1},{3,2},{4,3},{5,4},{6,5},{7,6},{8,15},{9,8},{10,9... | collective-permute-start | bytes 786440 | tf_op jit(solution)/shard_map/ppermute | solution.py:107
  190.5 14.4 %collective-permute-start = (bf16[512,256]{1,0:T(8,128)(2,1)}, bf16[512,256]{1,0:T(8,128)(2,1)S(1)}, u32[]{:S(2)}, u32[]{:S(2)}) collective-permute-start(bf16[512,256]{1,0:T(8,128)(2,1)} %get-tuple-element.42), channel_id=1, source_target_pairs={{0,1},{1,2},{2,3},{3,4},{4,5},{5,6},{6,7},{7,0},{8,9},{9,10},{10,1... | collective-permute-start | bytes 786440 | tf_op jit(solution)/shard_map/ppermute | solution.py:107
  190.5 14.5 %collective-permute-start.1 = (bf16[512,256]{1,0:T(8,128)(2,1)}, bf16[512,256]{1,0:T(8,128)(2,1)}, u32[]{:S(2)}, u32[]{:S(2)}) collective-permute-start(bf16[512,256]{1,0:T(8,128)(2,1)} %get-tuple-element.43), channel_id=1, source_target_pairs={{0,2},{1,3},{2,4},{3,5},{4,6},{5,7},{6,0},{7,1},{8,10},{9,11},{10,... | collective-permute-start | bytes 786440 | tf_op jit(solution)/shard_map/ppermute | solution.py:107
  190.6 17.3 %collective-permute-start.2 = (bf16[512,256]{1,0:T(8,128)(2,1)}, bf16[512,256]{1,0:T(8,128)(2,1)}, u32[]{:S(2)}, u32[]{:S(2)}) collective-permute-start(bf16[512,256]{1,0:T(8,128)(2,1)} %get-tuple-element.44), channel_id=1, source_target_pairs={{0,3},{1,4},{2,5},{3,6},{4,7},{5,0},{6,1},{7,2},{8,11},{9,12},{10,... | collective-permute-start | bytes 786440 | tf_op jit(solution)/shard_map/ppermute | solution.py:107
  191.3 23.9 %collective-permute-start.3 = (bf16[512,256]{1,0:T(8,128)(2,1)}, bf16[512,256]{1,0:T(8,128)(2,1)}, u32[]{:S(2)}, u32[]{:S(2)}) collective-permute-start(bf16[512,256]{1,0:T(8,128)(2,1)} %get-tuple-element.45), channel_id=1, source_target_pairs={{0,4},{1,5},{2,6},{3,7},{4,0},{5,1},{6,2},{7,3},{8,12},{9,13},{10,... | collective-permute-start | bytes 786440 | tf_op jit(solution)/shard_map/ppermute | solution.py:107
  204.6 10.9 %collective-permute-start.23 = (bf16[64,256]{1,0:T(8,128)(2,1)}, bf16[64,256]{1,0:T(8,128)(2,1)S(1)}, u32[]{:S(2)}, u32[]{:S(2)}) collective-permute-start(bf16[64,256]{1,0:T(8,128)(2,1)} %get-tuple-element.66), channel_id=1, source_target_pairs={{0,1},{1,2},{2,3},{3,4},{4,5},{5,6},{6,7},{7,0},{8,9},{9,10},{10,1... | collective-permute-start | bytes 98312 | tf_op jit(solution)/shard_map/ppermute | solution.py:107
  204.9 13.9 %collective-permute-start.24 = (bf16[64,256]{1,0:T(8,128)(2,1)}, bf16[64,256]{1,0:T(8,128)(2,1)S(1)}, u32[]{:S(2)}, u32[]{:S(2)}) collective-permute-start(bf16[64,256]{1,0:T(8,128)(2,1)} %get-tuple-element.67), channel_id=1, source_target_pairs={{0,2},{1,3},{2,4},{3,5},{4,6},{5,7},{6,0},{7,1},{8,10},{9,11},{10,... | collective-permute-start | bytes 98312 | tf_op jit(solution)/shard_map/ppermute | solution.py:107
  205.0 15.2 %collective-permute-start.25 = (bf16[64,256]{1,0:T(8,128)(2,1)}, bf16[64,256]{1,0:T(8,128)(2,1)S(1)}, u32[]{:S(2)}, u32[]{:S(2)}) collective-permute-start(bf16[64,256]{1,0:T(8,128)(2,1)} %get-tuple-element.68), channel_id=1, source_target_pairs={{0,3},{1,4},{2,5},{3,6},{4,7},{5,0},{6,1},{7,2},{8,11},{9,12},{10,... | collective-permute-start | bytes 98312 | tf_op jit(solution)/shard_map/ppermute | solution.py:107
  207.9 13.7 %collective-permute-start.26 = (bf16[64,256]{1,0:T(8,128)(2,1)}, bf16[64,256]{1,0:T(8,128)(2,1)S(1)}, u32[]{:S(2)}, u32[]{:S(2)}) collective-permute-start(bf16[64,256]{1,0:T(8,128)(2,1)} %get-tuple-element.69), channel_id=1, source_target_pairs={{0,4},{1,5},{2,6},{3,7},{4,0},{5,1},{6,2},{7,3},{8,12},{9,13},{10,... | collective-permute-start | bytes 98312 | tf_op jit(solution)/shard_map/ppermute | solution.py:107
  215.2 14.4 %collective-permute-start.9 = (bf16[512,256]{1,0:T(8,128)(2,1)}, bf16[512,256]{1,0:T(8,128)(2,1)S(1)}, u32[]{:S(2)}, u32[]{:S(2)}) collective-permute-start(bf16[512,256]{1,0:T(8,128)(2,1)} %get-tuple-element.50), channel_id=1, source_target_pairs={{0,1},{1,2},{2,3},{3,4},{4,5},{5,6},{6,7},{7,0},{8,9},{9,10},{10,1... | collective-permute-start | bytes 786440 | tf_op jit(solution)/shard_map/ppermute | solution.py:107
  215.5 16.6 %collective-permute-start.10 = (bf16[512,256]{1,0:T(8,128)(2,1)}, bf16[512,256]{1,0:T(8,128)(2,1)S(1)}, u32[]{:S(2)}, u32[]{:S(2)}) collective-permute-start(bf16[512,256]{1,0:T(8,128)(2,1)} %get-tuple-element.51), channel_id=1, source_target_pairs={{0,2},{1,3},{2,4},{3,5},{4,6},{5,7},{6,0},{7,1},{8,10},{9,11},{10,... | collective-permute-start | bytes 786440 | tf_op jit(solution)/shard_map/ppermute | solution.py:107
  218.8 7.0 %collective-permute-start.27 = (bf16[64,256]{1,0:T(8,128)(2,1)}, bf16[64,256]{1,0:T(8,128)(2,1)S(1)}, u32[]{:S(2)}, u32[]{:S(2)}) collective-permute-start(bf16[64,256]{1,0:T(8,128)(2,1)} %get-tuple-element.70), channel_id=1, source_target_pairs={{0,5},{1,6},{2,7},{3,0},{4,1},{5,2},{6,3},{7,4},{8,13},{9,14},{10,... | collective-permute-start | bytes 98312 | tf_op jit(solution)/shard_map/ppermute | solution.py:107
  221.6 6.5 %collective-permute-start.29 = (bf16[64,256]{1,0:T(8,128)(2,1)}, bf16[64,256]{1,0:T(8,128)(2,1)S(1)}, u32[]{:S(2)}, u32[]{:S(2)}) collective-permute-start(bf16[64,256]{1,0:T(8,128)(2,1)} %get-tuple-element.72), channel_id=1, source_target_pairs={{0,7},{1,0},{2,1},{3,2},{4,3},{5,4},{6,5},{7,6},{8,15},{9,8},{10,9... | collective-permute-start | bytes 98312 | tf_op jit(solution)/shard_map/ppermute | solution.py:107
  225.8 24.8 %collective-permute-start.11 = (bf16[512,256]{1,0:T(8,128)(2,1)}, bf16[512,256]{1,0:T(8,128)(2,1)}, u32[]{:S(2)}, u32[]{:S(2)}) collective-permute-start(bf16[512,256]{1,0:T(8,128)(2,1)} %get-tuple-element.52), channel_id=1, source_target_pairs={{0,3},{1,4},{2,5},{3,6},{4,7},{5,0},{6,1},{7,2},{8,11},{9,12},{10,... | collective-permute-start | bytes 786440 | tf_op jit(solution)/shard_map/ppermute | solution.py:107
  225.8 24.8 %collective-permute-start.12 = (bf16[512,256]{1,0:T(8,128)(2,1)}, bf16[512,256]{1,0:T(8,128)(2,1)}, u32[]{:S(2)}, u32[]{:S(2)}) collective-permute-start(bf16[512,256]{1,0:T(8,128)(2,1)} %get-tuple-element.53), channel_id=1, source_target_pairs={{0,4},{1,5},{2,6},{3,7},{4,0},{5,1},{6,2},{7,3},{8,12},{9,13},{10,... | collective-permute-start | bytes 786440 | tf_op jit(solution)/shard_map/ppermute | solution.py:107
  228.1 22.5 %collective-permute-start.13 = (bf16[512,256]{1,0:T(8,128)(2,1)}, bf16[512,256]{1,0:T(8,128)(2,1)}, u32[]{:S(2)}, u32[]{:S(2)}) collective-permute-start(bf16[512,256]{1,0:T(8,128)(2,1)} %get-tuple-element.54), channel_id=1, source_target_pairs={{0,5},{1,6},{2,7},{3,0},{4,1},{5,2},{6,3},{7,4},{8,13},{9,14},{10,... | collective-permute-start | bytes 786440 | tf_op jit(solution)/shard_map/ppermute | solution.py:107
  229.6 21.0 %collective-permute-start.14 = (bf16[512,256]{1,0:T(8,128)(2,1)}, bf16[512,256]{1,0:T(8,128)(2,1)}, u32[]{:S(2)}, u32[]{:S(2)}) collective-permute-start(bf16[512,256]{1,0:T(8,128)(2,1)} %get-tuple-element.55), channel_id=1, source_target_pairs={{0,6},{1,7},{2,0},{3,1},{4,2},{5,3},{6,4},{7,5},{8,14},{9,15},{10,... | collective-permute-start | bytes 786440 | tf_op jit(solution)/shard_map/ppermute | solution.py:107
  232.1 18.5 %collective-permute-start.15 = (bf16[512,256]{1,0:T(8,128)(2,1)}, bf16[512,256]{1,0:T(8,128)(2,1)}, u32[]{:S(2)}, u32[]{:S(2)}) collective-permute-start(bf16[512,256]{1,0:T(8,128)(2,1)} %get-tuple-element.56), channel_id=1, source_target_pairs={{0,7},{1,0},{2,1},{3,2},{4,3},{5,4},{6,5},{7,6},{8,15},{9,8},{10,9... | collective-permute-start | bytes 786440 | tf_op jit(solution)/shard_map/ppermute | solution.py:107
  (19 other events, 562.5 us)

commit v6 on v5

--- a/solution.py
+++ b/solution.py
@@ -247,6 +247,7 @@
 
     tiles_total = place_ref[1]
     global_kv = pad_ref[(tiles_here + 2) * TILE :, :]
+    ones = jnp.ones((3 * TILE, lanes), jnp.bfloat16)
     for i in range(per_step):
         t = step * per_step + i
         rows = pl.ds(i * TILE, TILE)
@@ -265,15 +266,18 @@
         )
         p_window = jnp.exp2((s_window - top) * SCALE)
         p_global = jnp.exp2((s_global - top) * SCALE)
-        total = jnp.sum(p_window, axis=1, keepdims=True) + jnp.sum(p_global, axis=1, keepdims=True)
         acc = jnp.dot(
-            p_window.astype(jnp.bfloat16), window[:, lanes:], preferred_element_type=jnp.float32
+            p_window.astype(jnp.bfloat16),
+            jnp.concatenate([window[:, lanes:], ones[: 3 * TILE]], axis=1),
+            preferred_element_type=jnp.float32,
         ) + jnp.dot(
-            p_global.astype(jnp.bfloat16), global_kv[:, lanes:], preferred_element_type=jnp.float32
+            p_global.astype(jnp.bfloat16),
+            jnp.concatenate([global_kv[:, lanes:], ones[: GLOBALS * TILE]], axis=1),
+            preferred_element_type=jnp.float32,
         )
         m_ref[rows, :] = join_heads(top)
-        l_ref[rows, :] = join_heads(total)
-        a_ref[rows, :] = join_heads(acc)
+        l_ref[rows, :] = join_heads(acc[:, lanes:])
+        a_ref[rows, :] = join_heads(acc[:, :lanes])
         qo_ref[rows, :] = q
 
 
@@ -343,26 +347,26 @@
         for j in range(0, RANDOM, 2):
             keys = jnp.concatenate([kv_ref[at[j], :, :lanes], kv_ref[at[j + 1], :, :lanes]], axis=0)
             s = score(q2, keys)
-            for i, part in enumerate((s[:, :TILE], s[:, TILE:])):
-                part = part + jnp.where(j + i < count, 0.0, NEG).astype(jnp.float32)
-                scores.append(part)
-                top = part if top is None else jnp.maximum(top, part)
+            scores.append(s)
+            top = s if top is None else jnp.maximum(top, s)
         m_old = m_ref[rows, :]
         m_old = jnp.concatenate([m_old[:, :1], m_old[:, HEAD_DIM : HEAD_DIM + 1]], axis=0)
         m_new = jnp.maximum(jnp.max(top, axis=1, keepdims=True), m_old)
         alpha = jnp.exp2((m_old - m_new) * SCALE)
-        total = None
         acc = None
         for j in range(0, RANDOM, 2):
-            p0 = jnp.exp2((scores[j] - m_new) * SCALE)
-            p1 = jnp.exp2((scores[j + 1] - m_new) * SCALE)
-            total = p0 + p1 if total is None else total + (p0 + p1)
-            p = jnp.concatenate([p0.astype(jnp.bfloat16), p1.astype(jnp.bfloat16)], axis=1)
-            v = jnp.concatenate([kv_ref[at[j], :, lanes:], kv_ref[at[j + 1], :, lanes:]], axis=0)
-            part = jnp.dot(p, v, preferred_element_type=jnp.float32)
+            p = jnp.exp2((scores[j // 2] - m_new) * SCALE).astype(jnp.bfloat16)
+            v = []
+            for i in range(j, j + 2):
+                live = jnp.where(i < count, 1.0, 0.0).astype(jnp.float32)
+                one = jnp.full((TILE, lanes), live, jnp.float32).astype(jnp.bfloat16)
+                v.append(jnp.concatenate([kv_ref[at[i], :, lanes:] * one, one], axis=1))
+            part = jnp.dot(p, jnp.concatenate(v, axis=0), preferred_element_type=jnp.float32)
             acc = part if acc is None else acc + part
+        total = acc[:, lanes:]
+        acc = acc[:, :lanes]
         alpha = join_heads(alpha)
-        denominator = l_ref[rows, :] * alpha + join_heads(jnp.sum(total, axis=1, keepdims=True))
+        denominator = l_ref[rows, :] * alpha + join_heads(total)
         numerator = a_ref[rows, :] * alpha + join_heads(acc)
         o_ref[rows, :] = (numerator / denominator).astype(jnp.bfloat16)
 
@@ -419,8 +423,9 @@
         & (tiles[None, :] >= (owner * tiles_here)[:, None])
     )
     slot = jnp.sum(lower.astype(jnp.int32), axis=1)
-    read = jnp.where(wanted >= 0, slot * ctx_count + owner, 0)
-    return [send[:, slot] for slot in range(CAP)], read
+    read = (slot * ctx_count + owner).reshape(tiles_here, slots)
+    read = jnp.where(wanted.reshape(tiles_here, slots) >= 0, read, read[:, :1])
+    return [send[:, slot] for slot in range(CAP)], read.reshape(-1)
 
 
 def body(tokens, w_query, w_key, w_value, w_out, random_tiles, random_count):

time: 306 us -> 298 us (0.974)
  Pallas kernels: 88.5 us -> 80.9 us
    pallas_call x1, Pallas kernels: 31.9 us -> 24.1 us  [random_attention(): pl.pallas_call(functools.partial(random_kernel, groups=groups, spread=spr...]
  transfers between devices with their start and end apart: 33 -> 33, of which waited for: 10 -> 10; matrix products, arithmetic and copies ran while one was open for 3% -> 3% of each run, Pallas kernels for 16% -> 17%
where the time goes in v6:
time: 298 us; the launch traced here: 297 us
  Pallas kernels  80.9 us (27%)
  waiting for transfers between devices  70.2 us (24%)
  starting transfers between devices  68.3 us (23%)
  blocking collectives  61.6 us (21%)
  local copies, waits for them, and re-layouts  9.16 us (3%)
  other arithmetic  4.56 us (2%)
    ppermute x28, starting transfers between devices, exchange(): lax.ppermute(pieces[o], axis, [(i, (i + o) % size) for i in range(size)])  42.6 us
    all_to_all x1, blocking collectives, body(): got = lax.all_to_all(chunks, 'ctx', split_axis=0, concat_axis=0, tiled=True)  41.5 us
    ppermute x28, waiting for transfers between devices, exchange(): lax.ppermute(pieces[o], axis, [(i, (i + o) % size) for i in range(size)])  29.7 us
    pallas_call x3, Pallas kernels, project(): pl.pallas_call(functools.partial(project_kernel, sources=len(xs), weights...  29.1 us
    ppermute x1, waiting for transfers between devices, body(): before = lax.ppermute(striped[-1:], 'ctx', up)  25.6 us
    pallas_call x1, Pallas kernels, random_attention(): pl.pallas_call(functools.partial(random_kernel, groups=groups, spread=spr...  24.1 us
    all_to_all x1, blocking collectives, body(): lax.all_to_all(attended, 'head', split_axis=0, concat_axis=0, tiled=True)  20.1 us
    pallas_call x1, Pallas kernels, local_attention(): pl.pallas_call(functools.partial(local_kernel, groups=groups), grid_spec=...  17 us
  transfers between devices with their start and end apart: 33, of which 10 were waited for; matrix products, arithmetic and copies ran while one was open for 3% of the time, Pallas kernels for 17%

profile of v6, /device:TPU:6, one launch (start us, length us, event | category | flops | bytes accessed | tf_op | source)
XLA Modules:
  0.0 297.3 jit_solution(12762187785479626307)
XLA Ops:
  0.0 2.5 copy.16
  2.5 4.5 %all-to-all-start = ((bf16[8,4,16,1024]{3,2,1,0:T(8,128)(2,1)}), bf16[8,4,16,1024]{3,2,1,0:T(8,128)(2,1)S(1)}, u32[]{:S(2)}, u32[]{:S(2)}) async-start(bf16[8,4,16,1024]{3,2,1,0:T(8,128)(2,1)} %bitcast.40), calls=%async_computation | async-start | bytes 2097152 | tf_op jit(solution)/shard_map/all_to_all | solution.py:443
  11.4 11.5 %all-to-all-done = bf16[8,4,16,1024]{3,2,1,0:T(8,128)(2,1)S(1)} async-done(((bf16[8,4,16,1024]{3,2,1,0:T(8,128)(2,1)}), bf16[8,4,16,1024]{3,2,1,0:T(8,128)(2,1)S(1)}, u32[]{:S(2)}, u32[]{:S(2)}) %all-to-all-start) | async-done | bytes 1048608 | tf_op jit(solution)/shard_map/all_to_all | solution.py:443
  23.8 3.2 %shard_map.73 = bf16[32,136,128]{2,1,0:T(8,128)(2,1)} custom-call(s32[32]{0:T(128)} %get-tuple-element.83.index_ref, bf16[32,16,1024]{2,1,0:T(8,128)(2,1)} %bitcast.37), custom_call_target="tpu_custom_call" | custom-call | bytes 4194304 | tf_op jit(solution)/shard_map/pallas_call | solution.py:159
  27.0 41.5 %all_to_all.25.refs_0_.root_ref = bf16[32,136,128]{2,1,0:T(8,128)(2,1)} all-to-all(bf16[32,136,128]{2,1,0:T(8,128)(2,1)} %shard_map.73), channel_id=1, replica_groups=mesh['ctx'=32,'head'=8] {'ctx'}, dimensions={0} | all-to-all | bytes 2228224 | tf_op jit(solution)/shard_map/all_to_all | solution.py:460
  68.5 3.2 %shard_map.75 = bf16[32,136,128]{2,1,0:T(8,128)(2,1)} custom-call(s32[32]{0:T(128)} %get-tuple-element.82.index_ref, bf16[32,16,1024]{2,1,0:T(8,128)(2,1)} %bitcast.38, bf16[32,136,128]{2,1,0:T(8,128)(2,1)} %all_to_all.25.refs_0_.root_ref), custom_call_target="tpu_custom_call" | custom-call | bytes 4194304 | tf_op jit(solution)/shard_map/pallas_call | solution.py:159
  71.7 5.5 %all-to-all-start.2 = ((bf16[32,136,128]{2,1,0:T(8,128)(2,1)}), bf16[32,136,128]{2,1,0:T(8,128)(2,1)S(1)}, u32[]{:S(2)}, u32[]{:S(2)}) async-start(bf16[32,136,128]{2,1,0:T(8,128)(2,1)} %shard_map.75), calls=%async_computation.2 | async-start | bytes 2228224 | tf_op jit(solution)/shard_map/all_to_all | solution.py:460
  77.2 10.9 %shard_map.77 = (bf16[512,384]{1,0:T(8,128)(2,1)}, bf16[512,384]{1,0:T(8,128)(2,1)}, bf16[512,384]{1,0:T(8,128)(2,1)}, bf16[512,384]{1,0:T(8,128)(2,1)}, bf16[51...) custom-call(s32[1]{0:T(128)} %bitcast.here_ref, ...), custom_call_target="tpu_custom_call" | custom-call | flops 3221225472 | bytes 10485760 | tf_op jit(solution)/shard_map/pallas_call | solution.py:78
  90.1 2.7 collective-permute-start.19
  93.7 6.6 %collective-permute-done.16.refs_1_ = bf16[512,384]{1,0:T(8,128)(2,1)} collective-permute-done((bf16[512,384]{1,0:T(8,128)(2,1)}, bf16[512,384]{1,0:T(8,128)(2,1)}, u32[]{:S(2)}, u32[]{:S(2)}) %collective-permute-start.16) | collective-permute-done | bytes 393248 | tf_op jit(solution)/shard_map/ppermute | solution.py:107
  101.7 6.8 %collective-permute-start.22 = (bf16[512,384]{1,0:T(8,128)(2,1)}, bf16[512,384]{1,0:T(8,128)(2,1)}, u32[]{:S(2)}, u32[]{:S(2)}) collective-permute-start(bf16[512,384]{1,0:T(8,128)(2,1)} %get-tuple-element.64), channel_id=1, source_target_pairs={{0,7},{1,0},{2,1},{3,2},{4,3},{5,4},{6,5},{7,6},{8,15},{9,8},{10,9... | collective-permute-start | bytes 1179656 | tf_op jit(solution)/shard_map/ppermute | solution.py:107
  108.5 8.2 %collective-permute-done.18.refs_3_ = bf16[512,384]{1,0:T(8,128)(2,1)} collective-permute-done((bf16[512,384]{1,0:T(8,128)(2,1)}, bf16[512,384]{1,0:T(8,128)(2,1)}, u32[]{:S(2)}, u32[]{:S(2)}) %collective-permute-start.18) | collective-permute-done | bytes 393248 | tf_op jit(solution)/shard_map/ppermute | solution.py:107
  118.0 5.2 %collective-permute-done.20.refs_5_ = bf16[512,384]{1,0:T(8,128)(2,1)} collective-permute-done((bf16[512,384]{1,0:T(8,128)(2,1)}, bf16[512,384]{1,0:T(8,128)(2,1)}, u32[]{:S(2)}, u32[]{:S(2)}) %collective-permute-start.20) | collective-permute-done | bytes 393248 | tf_op jit(solution)/shard_map/ppermute | solution.py:107
  123.2 3.0 %collective-permute-done.22.refs_7_ = bf16[512,384]{1,0:T(8,128)(2,1)} collective-permute-done((bf16[512,384]{1,0:T(8,128)(2,1)}, bf16[512,384]{1,0:T(8,128)(2,1)}, u32[]{:S(2)}, u32[]{:S(2)}) %collective-permute-start.22) | collective-permute-done | bytes 393248 | tf_op jit(solution)/shard_map/ppermute | solution.py:107
  126.2 4.2 %pick_kv.1 = bf16[32,128,256]{2,1,0:T(8,128)(2,1)} custom-call(s32[32]{0:T(128)} %get-tuple-element.81.index_ref, s32[1]{0:T(128)} %bitcast.here_ref, bf16[512,384]{1,0:T(8,128)(2,1)} %get-tuple-element.57.refs_0_, bf16[512,384]{1,0:T(8,128)(2,1)} %collective-permute-done.16.refs_1_, bf16[512,384]{1,0:T(8,128)(2,1)} %collective-permute-done.17.refs_2_, ...), custom_call_target="tpu_custom_call" | custom-call | bytes 5242880 | tf_op jit(solution)/shard_map/pick_kv/pallas_call | solution.py:191
  131.5 9.9 %all-to-all-start.3 = ((bf16[32,128,256]{2,1,0:T(8,128)(2,1)}), bf16[32,128,256]{2,1,0:T(8,128)(2,1)}, u32[]{:S(2)}, u32[]{:S(2)}) async-start(bf16[32,128,256]{2,1,0:T(8,128)(2,1)} %pick_kv.1), calls=%async_computation.3 | async-start | bytes 4194304 | tf_op jit(solution)/shard_map/all_to_all | solution.py:471
  142.6 3.4 %collective-permute-start.7 = (bf16[1,16,1024]{2,1,0:T(8,128)(2,1)S(1)}, bf16[1,16,1024]{2,1,0:T(8,128)(2,1)S(1)}, u32[]{:S(2)}, u32[]{:S(2)}) collective-permute-start(bf16[1,16,1024]{2,1,0:T(8,128)(2,1)S(1)} %get-tuple-element.77), channel_id=1, source_target_pairs={{0,8},{8,16},{16,24},{24,32},{32,40},{40,48},{48,56},{56,64},{64,7... | collective-permute-start | bytes 98312 | tf_op jit(solution)/shard_map/ppermute | solution.py:453
  146.0 2.5 collective-permute-start.8
  148.5 8.9 %shard_map.74 = (bf16[512,256]{1,0:T(8,128)(2,1)}, bf16[512,256]{1,0:T(8,128)(2,1)}, bf16[512,256]{1,0:T(8,128)(2,1)}, bf16[512,256]{1,0:T(8,128)(2,1)}, bf16[51...) custom-call(s32[1]{0:T(128)} %bitcast.here_ref, ...), custom_call_target="tpu_custom_call" | custom-call | flops 2147483648 | bytes 7340032 | tf_op jit(solution)/shard_map/pallas_call | solution.py:78
  160.8 25.6 %collective-permute-done.7 = bf16[1,16,1024]{2,1,0:T(8,128)(2,1)S(1)} collective-permute-done((bf16[1,16,1024]{2,1,0:T(8,128)(2,1)S(1)}, bf16[1,16,1024]{2,1,0:T(8,128)(2,1)S(1)}, u32[]{:S(2)}, u32[]{:S(2)}) %collective-permute-start.7) | collective-permute-done | bytes 32800 | tf_op jit(solution)/shard_map/ppermute | solution.py:453
  186.4 3.4 %collective-permute-done.8 = bf16[1,16,1024]{2,1,0:T(8,128)(2,1)S(1)} collective-permute-done((bf16[1,16,1024]{2,1,0:T(8,128)(2,1)S(1)}, bf16[1,16,1024]{2,1,0:T(8,128)(2,1)S(1)}, u32[]{:S(2)}, u32[]{:S(2)}) %collective-permute-start.8) | collective-permute-done | bytes 32800 | tf_op jit(solution)/shard_map/ppermute | solution.py:454
  191.1 3.9 %collective-permute-start.3 = (bf16[512,256]{1,0:T(8,128)(2,1)}, bf16[512,256]{1,0:T(8,128)(2,1)}, u32[]{:S(2)}, u32[]{:S(2)}) collective-permute-start(bf16[512,256]{1,0:T(8,128)(2,1)} %get-tuple-element.45), channel_id=1, source_target_pairs={{0,4},{1,5},{2,6},{3,7},{4,0},{5,1},{6,2},{7,3},{8,12},{9,13},{10,... | collective-permute-start | bytes 786440 | tf_op jit(solution)/shard_map/ppermute | solution.py:107
  195.0 9.3 %shard_map.76 = (bf16[512,256]{1,0:T(8,128)(2,1)}, bf16[512,256]{1,0:T(8,128)(2,1)}, bf16[512,256]{1,0:T(8,128)(2,1)}, bf16[512,256]{1,0:T(8,128)(2,1)}, bf16[51...) custom-call(s32[1]{0:T(128)} %bitcast.here_ref, ...), custom_call_target="tpu_custom_call" | custom-call | flops 2415919104 | bytes 7733248 | tf_op jit(solution)/shard_map/pallas_call | solution.py:78
  204.6 3.1 %collective-permute-start.25 = (bf16[64,256]{1,0:T(8,128)(2,1)}, bf16[64,256]{1,0:T(8,128)(2,1)S(1)}, u32[]{:S(2)}, u32[]{:S(2)}) collective-permute-start(bf16[64,256]{1,0:T(8,128)(2,1)} %get-tuple-element.68), channel_id=1, source_target_pairs={{0,3},{1,4},{2,5},{3,6},{4,7},{5,0},{6,1},{7,2},{8,11},{9,12},{10,... | collective-permute-start | bytes 98312 | tf_op jit(solution)/shard_map/ppermute | solution.py:107
  207.7 7.4 %collective-permute-start.26 = (bf16[64,256]{1,0:T(8,128)(2,1)}, bf16[64,256]{1,0:T(8,128)(2,1)S(1)}, u32[]{:S(2)}, u32[]{:S(2)}) collective-permute-start(bf16[64,256]{1,0:T(8,128)(2,1)} %get-tuple-element.69), channel_id=1, source_target_pairs={{0,4},{1,5},{2,6},{3,7},{4,0},{5,1},{6,2},{7,3},{8,12},{9,13},{10,... | collective-permute-start | bytes 98312 | tf_op jit(solution)/shard_map/ppermute | solution.py:107
  215.4 2.6 collective-permute-start.10
  221.8 4.0 %collective-permute-done.27.refs_13_ = bf16[64,256]{1,0:T(8,128)(2,1)S(1)} collective-permute-done((bf16[64,256]{1,0:T(8,128)(2,1)}, bf16[64,256]{1,0:T(8,128)(2,1)S(1)}, u32[]{:S(2)}, u32[]{:S(2)}) %collective-permute-start.27) | collective-permute-done | bytes 32800 | tf_op jit(solution)/shard_map/ppermute | solution.py:107
  229.6 2.5 collective-permute-start.14
  233.6 17.0 %local_attention.1 = (f32[4096,128]{1,0:T(8,128)}, f32[4096,128]{1,0:T(8,128)}, f32[4096,128]{1,0:T(8,128)}, bf16[4096,128]{1,0:T(8,128)(2,1)}) custom-call(s32[3]{0:T(128)} %pad_add_fusion.place_ref, bf16[512,384]{1,0:T(8,128)(2,1)} %get-tuple-element.57.refs_0_, bf16[512,384]{1,0:T(8,128)(2,1)} %collective-permute-done.16.refs_1_, ...), custom_call_target="tpu_custom_call" | custom-call | flops 2684354560 | bytes 10485760 | tf_op jit(solution)/shard_map/local_attention/pallas_call | solution.py:292
  250.7 24.1 %random_attention.1 = bf16[4096,128]{1,0:T(8,128)(2,1)} custom-call(s32[384]{0:T(512)} %add_select_fusion.2.index_ref, s32[32]{0:T(128)} %dynamic_slice.8.count_ref, bf16[32,16,256]{2,1,0:T(8,128)(2,1)} %bitcast.50, bf16[32,16,256]{2,1,0:T(8,128)(2,1)} %bitcast.47, bf16[32,16,256]{2,1,0:T(8,128)(2,1)} %bitcast.7.refs_2_, ...), custom_call_target="tpu_custom_call" | custom-call | flops 6442450944 | bytes 14680064 | tf_op jit(solution)/shard_map/random_attention/pallas_call | solution.py:384
  274.9 20.1 %all_to_all.26 = bf16[8,512,128]{2,1,0:T(8,128)(2,1)S(1)} all-to-all(bf16[8,512,128]{2,1,0:T(8,128)(2,1)} %bitcast.42), channel_id=1, replica_groups=mesh['ctx'=32,'head'=8] {'head'}, dimensions={0} | all-to-all | bytes 2097152 | tf_op jit(solution)/shard_map/all_to_all | solution.py:478
  295.0 2.3 bitcast_convert_fusion
  (108 shorter events, 27.4 us)
Async XLA Ops:
  2.5 20.4 %all-to-all-start = ((bf16[8,4,16,1024]{3,2,1,0:T(8,128)(2,1)}), bf16[8,4,16,1024]{3,2,1,0:T(8,128)(2,1)S(1)}, u32[]{:S(2)}, u32[]{:S(2)}) async-start(bf16[8,4,16,1024]{3,2,1,0:T(8,128)(2,1)} %bitcast.40), calls=%async_computation | async-start | bytes 2097152 | tf_op jit(solution)/shard_map/all_to_all | solution.py:443
  71.7 58.7 %all-to-all-start.2 = ((bf16[32,136,128]{2,1,0:T(8,128)(2,1)}), bf16[32,136,128]{2,1,0:T(8,128)(2,1)S(1)}, u32[]{:S(2)}, u32[]{:S(2)}) async-start(bf16[32,136,128]{2,1,0:T(8,128)(2,1)} %shard_map.75), calls=%async_computation.2 | async-start | bytes 2228224 | tf_op jit(solution)/shard_map/all_to_all | solution.py:460
  88.1 12.3 %collective-permute-start.16 = (bf16[512,384]{1,0:T(8,128)(2,1)}, bf16[512,384]{1,0:T(8,128)(2,1)}, u32[]{:S(2)}, u32[]{:S(2)}) collective-permute-start(bf16[512,384]{1,0:T(8,128)(2,1)} %get-tuple-element.58), channel_id=1, source_target_pairs={{0,1},{1,2},{2,3},{3,4},{4,5},{5,6},{6,7},{7,0},{8,9},{9,10},{10,1... | collective-permute-start | bytes 1179656 | tf_op jit(solution)/shard_map/ppermute | solution.py:107
  88.1 13.6 %collective-permute-start.17 = (bf16[512,384]{1,0:T(8,128)(2,1)}, bf16[512,384]{1,0:T(8,128)(2,1)}, u32[]{:S(2)}, u32[]{:S(2)}) collective-permute-start(bf16[512,384]{1,0:T(8,128)(2,1)} %get-tuple-element.59), channel_id=1, source_target_pairs={{0,2},{1,3},{2,4},{3,5},{4,6},{5,7},{6,0},{7,1},{8,10},{9,11},{10,... | collective-permute-start | bytes 1179656 | tf_op jit(solution)/shard_map/ppermute | solution.py:107
  88.7 28.0 %collective-permute-start.18 = (bf16[512,384]{1,0:T(8,128)(2,1)}, bf16[512,384]{1,0:T(8,128)(2,1)}, u32[]{:S(2)}, u32[]{:S(2)}) collective-permute-start(bf16[512,384]{1,0:T(8,128)(2,1)} %get-tuple-element.60), channel_id=1, source_target_pairs={{0,3},{1,4},{2,5},{3,6},{4,7},{5,0},{6,1},{7,2},{8,11},{9,12},{10,... | collective-permute-start | bytes 1179656 | tf_op jit(solution)/shard_map/ppermute | solution.py:107
  90.1 27.9 %collective-permute-start.19 = (bf16[512,384]{1,0:T(8,128)(2,1)}, bf16[512,384]{1,0:T(8,128)(2,1)}, u32[]{:S(2)}, u32[]{:S(2)}) collective-permute-start(bf16[512,384]{1,0:T(8,128)(2,1)} %get-tuple-element.61), channel_id=1, source_target_pairs={{0,4},{1,5},{2,6},{3,7},{4,0},{5,1},{6,2},{7,3},{8,12},{9,13},{10,... | collective-permute-start | bytes 1179656 | tf_op jit(solution)/shard_map/ppermute | solution.py:107
  92.8 30.4 %collective-permute-start.20 = (bf16[512,384]{1,0:T(8,128)(2,1)}, bf16[512,384]{1,0:T(8,128)(2,1)}, u32[]{:S(2)}, u32[]{:S(2)}) collective-permute-start(bf16[512,384]{1,0:T(8,128)(2,1)} %get-tuple-element.62), channel_id=1, source_target_pairs={{0,5},{1,6},{2,7},{3,0},{4,1},{5,2},{6,3},{7,4},{8,13},{9,14},{10,... | collective-permute-start | bytes 1179656 | tf_op jit(solution)/shard_map/ppermute | solution.py:107
  100.4 22.8 %collective-permute-start.21 = (bf16[512,384]{1,0:T(8,128)(2,1)}, bf16[512,384]{1,0:T(8,128)(2,1)}, u32[]{:S(2)}, u32[]{:S(2)}) collective-permute-start(bf16[512,384]{1,0:T(8,128)(2,1)} %get-tuple-element.63), channel_id=1, source_target_pairs={{0,6},{1,7},{2,0},{3,1},{4,2},{5,3},{6,4},{7,5},{8,14},{9,15},{10,... | collective-permute-start | bytes 1179656 | tf_op jit(solution)/shard_map/ppermute | solution.py:107
  101.7 24.5 %collective-permute-start.22 = (bf16[512,384]{1,0:T(8,128)(2,1)}, bf16[512,384]{1,0:T(8,128)(2,1)}, u32[]{:S(2)}, u32[]{:S(2)}) collective-permute-start(bf16[512,384]{1,0:T(8,128)(2,1)} %get-tuple-element.64), channel_id=1, source_target_pairs={{0,7},{1,0},{2,1},{3,2},{4,3},{5,4},{6,5},{7,6},{8,15},{9,8},{10,9... | collective-permute-start | bytes 1179656 | tf_op jit(solution)/shard_map/ppermute | solution.py:107
  131.5 119.2 %all-to-all-start.3 = ((bf16[32,128,256]{2,1,0:T(8,128)(2,1)}), bf16[32,128,256]{2,1,0:T(8,128)(2,1)}, u32[]{:S(2)}, u32[]{:S(2)}) async-start(bf16[32,128,256]{2,1,0:T(8,128)(2,1)} %pick_kv.1), calls=%async_computation.3 | async-start | bytes 4194304 | tf_op jit(solution)/shard_map/all_to_all | solution.py:471
  142.6 43.8 %collective-permute-start.7 = (bf16[1,16,1024]{2,1,0:T(8,128)(2,1)S(1)}, bf16[1,16,1024]{2,1,0:T(8,128)(2,1)S(1)}, u32[]{:S(2)}, u32[]{:S(2)}) collective-permute-start(bf16[1,16,1024]{2,1,0:T(8,128)(2,1)S(1)} %get-tuple-element.77), channel_id=1, source_target_pairs={{0,8},{8,16},{16,24},{24,32},{32,40},{40,48},{48,56},{56,64},{64,7... | collective-permute-start | bytes 98312 | tf_op jit(solution)/shard_map/ppermute | solution.py:453
  146.0 43.8 %collective-permute-start.8 = (bf16[1,16,1024]{2,1,0:T(8,128)(2,1)S(1)}, bf16[1,16,1024]{2,1,0:T(8,128)(2,1)S(1)}, u32[]{:S(2)}, u32[]{:S(2)}) collective-permute-start(bf16[1,16,1024]{2,1,0:T(8,128)(2,1)S(1)} %get-tuple-element.78), channel_id=1, source_target_pairs={{8,0},{16,8},{24,16},{32,24},{40,32},{48,40},{56,48},{64,56},{72,6... | collective-permute-start | bytes 98312 | tf_op jit(solution)/shard_map/ppermute | solution.py:454
  157.4 33.1 %collective-permute-start.4 = (bf16[512,256]{1,0:T(8,128)(2,1)}, bf16[512,256]{1,0:T(8,128)(2,1)S(1)}, u32[]{:S(2)}, u32[]{:S(2)}) collective-permute-start(bf16[512,256]{1,0:T(8,128)(2,1)} %get-tuple-element.46), channel_id=1, source_target_pairs={{0,5},{1,6},{2,7},{3,0},{4,1},{5,2},{6,3},{7,4},{8,13},{9,14},{10,... | collective-permute-start | bytes 786440 | tf_op jit(solution)/shard_map/ppermute | solution.py:107
  157.6 33.5 %collective-permute-start.5 = (bf16[512,256]{1,0:T(8,128)(2,1)}, bf16[512,256]{1,0:T(8,128)(2,1)S(1)}, u32[]{:S(2)}, u32[]{:S(2)}) collective-permute-start(bf16[512,256]{1,0:T(8,128)(2,1)} %get-tuple-element.47), channel_id=1, source_target_pairs={{0,6},{1,7},{2,0},{3,1},{4,2},{5,3},{6,4},{7,5},{8,14},{9,15},{10,... | collective-permute-start | bytes 786440 | tf_op jit(solution)/shard_map/ppermute | solution.py:107
  160.3 44.0 %collective-permute-start.6 = (bf16[512,256]{1,0:T(8,128)(2,1)}, bf16[512,256]{1,0:T(8,128)(2,1)S(1)}, u32[]{:S(2)}, u32[]{:S(2)}) collective-permute-start(bf16[512,256]{1,0:T(8,128)(2,1)} %get-tuple-element.48), channel_id=1, source_target_pairs={{0,7},{1,0},{2,1},{3,2},{4,3},{5,4},{6,5},{7,6},{8,15},{9,8},{10,9... | collective-permute-start | bytes 786440 | tf_op jit(solution)/shard_map/ppermute | solution.py:107
  190.5 14.0 %collective-permute-start = (bf16[512,256]{1,0:T(8,128)(2,1)}, bf16[512,256]{1,0:T(8,128)(2,1)S(1)}, u32[]{:S(2)}, u32[]{:S(2)}) collective-permute-start(bf16[512,256]{1,0:T(8,128)(2,1)} %get-tuple-element.42), channel_id=1, source_target_pairs={{0,1},{1,2},{2,3},{3,4},{4,5},{5,6},{6,7},{7,0},{8,9},{9,10},{10,1... | collective-permute-start | bytes 786440 | tf_op jit(solution)/shard_map/ppermute | solution.py:107
  190.5 14.1 %collective-permute-start.1 = (bf16[512,256]{1,0:T(8,128)(2,1)}, bf16[512,256]{1,0:T(8,128)(2,1)}, u32[]{:S(2)}, u32[]{:S(2)}) collective-permute-start(bf16[512,256]{1,0:T(8,128)(2,1)} %get-tuple-element.43), channel_id=1, source_target_pairs={{0,2},{1,3},{2,4},{3,5},{4,6},{5,7},{6,0},{7,1},{8,10},{9,11},{10,... | collective-permute-start | bytes 786440 | tf_op jit(solution)/shard_map/ppermute | solution.py:107
  190.5 17.2 %collective-permute-start.2 = (bf16[512,256]{1,0:T(8,128)(2,1)}, bf16[512,256]{1,0:T(8,128)(2,1)}, u32[]{:S(2)}, u32[]{:S(2)}) collective-permute-start(bf16[512,256]{1,0:T(8,128)(2,1)} %get-tuple-element.44), channel_id=1, source_target_pairs={{0,3},{1,4},{2,5},{3,6},{4,7},{5,0},{6,1},{7,2},{8,11},{9,12},{10,... | collective-permute-start | bytes 786440 | tf_op jit(solution)/shard_map/ppermute | solution.py:107
  191.1 24.1 %collective-permute-start.3 = (bf16[512,256]{1,0:T(8,128)(2,1)}, bf16[512,256]{1,0:T(8,128)(2,1)}, u32[]{:S(2)}, u32[]{:S(2)}) collective-permute-start(bf16[512,256]{1,0:T(8,128)(2,1)} %get-tuple-element.45), channel_id=1, source_target_pairs={{0,4},{1,5},{2,6},{3,7},{4,0},{5,1},{6,2},{7,3},{8,12},{9,13},{10,... | collective-permute-start | bytes 786440 | tf_op jit(solution)/shard_map/ppermute | solution.py:107
  204.4 11.1 %collective-permute-start.23 = (bf16[64,256]{1,0:T(8,128)(2,1)}, bf16[64,256]{1,0:T(8,128)(2,1)S(1)}, u32[]{:S(2)}, u32[]{:S(2)}) collective-permute-start(bf16[64,256]{1,0:T(8,128)(2,1)} %get-tuple-element.66), channel_id=1, source_target_pairs={{0,1},{1,2},{2,3},{3,4},{4,5},{5,6},{6,7},{7,0},{8,9},{9,10},{10,1... | collective-permute-start | bytes 98312 | tf_op jit(solution)/shard_map/ppermute | solution.py:107
  204.5 13.8 %collective-permute-start.24 = (bf16[64,256]{1,0:T(8,128)(2,1)}, bf16[64,256]{1,0:T(8,128)(2,1)S(1)}, u32[]{:S(2)}, u32[]{:S(2)}) collective-permute-start(bf16[64,256]{1,0:T(8,128)(2,1)} %get-tuple-element.67), channel_id=1, source_target_pairs={{0,2},{1,3},{2,4},{3,5},{4,6},{5,7},{6,0},{7,1},{8,10},{9,11},{10,... | collective-permute-start | bytes 98312 | tf_op jit(solution)/shard_map/ppermute | solution.py:107
  204.6 15.1 %collective-permute-start.25 = (bf16[64,256]{1,0:T(8,128)(2,1)}, bf16[64,256]{1,0:T(8,128)(2,1)S(1)}, u32[]{:S(2)}, u32[]{:S(2)}) collective-permute-start(bf16[64,256]{1,0:T(8,128)(2,1)} %get-tuple-element.68), channel_id=1, source_target_pairs={{0,3},{1,4},{2,5},{3,6},{4,7},{5,0},{6,1},{7,2},{8,11},{9,12},{10,... | collective-permute-start | bytes 98312 | tf_op jit(solution)/shard_map/ppermute | solution.py:107
  207.7 13.4 %collective-permute-start.26 = (bf16[64,256]{1,0:T(8,128)(2,1)}, bf16[64,256]{1,0:T(8,128)(2,1)S(1)}, u32[]{:S(2)}, u32[]{:S(2)}) collective-permute-start(bf16[64,256]{1,0:T(8,128)(2,1)} %get-tuple-element.69), channel_id=1, source_target_pairs={{0,4},{1,5},{2,6},{3,7},{4,0},{5,1},{6,2},{7,3},{8,12},{9,13},{10,... | collective-permute-start | bytes 98312 | tf_op jit(solution)/shard_map/ppermute | solution.py:107
  215.2 14.4 %collective-permute-start.9 = (bf16[512,256]{1,0:T(8,128)(2,1)}, bf16[512,256]{1,0:T(8,128)(2,1)S(1)}, u32[]{:S(2)}, u32[]{:S(2)}) collective-permute-start(bf16[512,256]{1,0:T(8,128)(2,1)} %get-tuple-element.50), channel_id=1, source_target_pairs={{0,1},{1,2},{2,3},{3,4},{4,5},{5,6},{6,7},{7,0},{8,9},{9,10},{10,1... | collective-permute-start | bytes 786440 | tf_op jit(solution)/shard_map/ppermute | solution.py:107
  215.4 16.6 %collective-permute-start.10 = (bf16[512,256]{1,0:T(8,128)(2,1)}, bf16[512,256]{1,0:T(8,128)(2,1)S(1)}, u32[]{:S(2)}, u32[]{:S(2)}) collective-permute-start(bf16[512,256]{1,0:T(8,128)(2,1)} %get-tuple-element.51), channel_id=1, source_target_pairs={{0,2},{1,3},{2,4},{3,5},{4,6},{5,7},{6,0},{7,1},{8,10},{9,11},{10,... | collective-permute-start | bytes 786440 | tf_op jit(solution)/shard_map/ppermute | solution.py:107
  218.4 7.4 %collective-permute-start.27 = (bf16[64,256]{1,0:T(8,128)(2,1)}, bf16[64,256]{1,0:T(8,128)(2,1)S(1)}, u32[]{:S(2)}, u32[]{:S(2)}) collective-permute-start(bf16[64,256]{1,0:T(8,128)(2,1)} %get-tuple-element.70), channel_id=1, source_target_pairs={{0,5},{1,6},{2,7},{3,0},{4,1},{5,2},{6,3},{7,4},{8,13},{9,14},{10,... | collective-permute-start | bytes 98312 | tf_op jit(solution)/shard_map/ppermute | solution.py:107
  221.1 6.5 %collective-permute-start.29 = (bf16[64,256]{1,0:T(8,128)(2,1)}, bf16[64,256]{1,0:T(8,128)(2,1)S(1)}, u32[]{:S(2)}, u32[]{:S(2)}) collective-permute-start(bf16[64,256]{1,0:T(8,128)(2,1)} %get-tuple-element.72), channel_id=1, source_target_pairs={{0,7},{1,0},{2,1},{3,2},{4,3},{5,4},{6,5},{7,6},{8,15},{9,8},{10,9... | collective-permute-start | bytes 98312 | tf_op jit(solution)/shard_map/ppermute | solution.py:107
  225.8 24.9 %collective-permute-start.11 = (bf16[512,256]{1,0:T(8,128)(2,1)}, bf16[512,256]{1,0:T(8,128)(2,1)}, u32[]{:S(2)}, u32[]{:S(2)}) collective-permute-start(bf16[512,256]{1,0:T(8,128)(2,1)} %get-tuple-element.52), channel_id=1, source_target_pairs={{0,3},{1,4},{2,5},{3,6},{4,7},{5,0},{6,1},{7,2},{8,11},{9,12},{10,... | collective-permute-start | bytes 786440 | tf_op jit(solution)/shard_map/ppermute | solution.py:107
  225.8 24.9 %collective-permute-start.12 = (bf16[512,256]{1,0:T(8,128)(2,1)}, bf16[512,256]{1,0:T(8,128)(2,1)}, u32[]{:S(2)}, u32[]{:S(2)}) collective-permute-start(bf16[512,256]{1,0:T(8,128)(2,1)} %get-tuple-element.53), channel_id=1, source_target_pairs={{0,4},{1,5},{2,6},{3,7},{4,0},{5,1},{6,2},{7,3},{8,12},{9,13},{10,... | collective-permute-start | bytes 786440 | tf_op jit(solution)/shard_map/ppermute | solution.py:107
  227.7 23.0 %collective-permute-start.13 = (bf16[512,256]{1,0:T(8,128)(2,1)}, bf16[512,256]{1,0:T(8,128)(2,1)}, u32[]{:S(2)}, u32[]{:S(2)}) collective-permute-start(bf16[512,256]{1,0:T(8,128)(2,1)} %get-tuple-element.54), channel_id=1, source_target_pairs={{0,5},{1,6},{2,7},{3,0},{4,1},{5,2},{6,3},{7,4},{8,13},{9,14},{10,... | collective-permute-start | bytes 786440 | tf_op jit(solution)/shard_map/ppermute | solution.py:107
  229.6 21.2 %collective-permute-start.14 = (bf16[512,256]{1,0:T(8,128)(2,1)}, bf16[512,256]{1,0:T(8,128)(2,1)}, u32[]{:S(2)}, u32[]{:S(2)}) collective-permute-start(bf16[512,256]{1,0:T(8,128)(2,1)} %get-tuple-element.55), channel_id=1, source_target_pairs={{0,6},{1,7},{2,0},{3,1},{4,2},{5,3},{6,4},{7,5},{8,14},{9,15},{10,... | collective-permute-start | bytes 786440 | tf_op jit(solution)/shard_map/ppermute | solution.py:107
  232.1 18.7 %collective-permute-start.15 = (bf16[512,256]{1,0:T(8,128)(2,1)}, bf16[512,256]{1,0:T(8,128)(2,1)}, u32[]{:S(2)}, u32[]{:S(2)}) collective-permute-start(bf16[512,256]{1,0:T(8,128)(2,1)} %get-tuple-element.56), channel_id=1, source_target_pairs={{0,7},{1,0},{2,1},{3,2},{4,3},{5,4},{6,5},{7,6},{8,15},{9,8},{10,9... | collective-permute-start | bytes 786440 | tf_op jit(solution)/shard_map/ppermute | solution.py:107
  (19 other events, 557.5 us)

commit v7 on v6

--- a/solution.py
+++ b/solution.py
@@ -116,7 +116,7 @@
         o_ref[d, k * part : (k + 1) * part, :] = tile[:, k * lanes : (k + 1) * lanes]
 
 
-def pick_first_kernel(index_ref, x_ref, o_ref):
+def pick_kernel(index_ref, x_ref, o_ref, *, scatter):
     dests, tall, lanes = o_ref.shape
     part, width = x_ref.shape[1:]
     across = width // lanes
@@ -126,44 +126,56 @@
         return carry
 
     lax.fori_loop(0, dests, step, 0)
-    for b in range(dests):
-        row = b // across * SUB
-        lane = b % across * lanes
-        o_ref[b, tall - SUB :, :] = x_ref[
-            row // part, row % part : row % part + SUB, lane : lane + lanes
-        ]
-
-
-def pick_second_kernel(index_ref, x_ref, root_ref, o_ref):
-    dests, tall, _ = o_ref.shape
-    block = root_ref[0]
-
-    def step(d, carry):
-        pick_chunk(o_ref, d, x_ref[index_ref[d]])
-        o_ref[d, tall - SUB :, :] = block
-        return carry
-
-    lax.fori_loop(0, dests, step, 0)
-
-
-def pick_chunks(index, x, dests, got):
+    if scatter:
+        for b in range(dests):
+            row = b // across * SUB
+            lane = b % across * lanes
+            o_ref[b, tall - SUB :, :] = x_ref[
+                row // part, row % part : row % part + SUB, lane : lane + lanes
+            ]
+
+
+def pick_chunks(index, x, dests, scatter):
     _, part, width = x.shape
-    tall = part * width // LANES + SUB
-    out = (dests, tall, LANES)
+    out = (dests, part * width // LANES + SUB, LANES)
     whole = lambda shape: pl.BlockSpec(shape, lambda i, idx: (0,) * len(shape))
-    ins, specs, kernel = [x], [whole(x.shape)], pick_first_kernel
-    if got is not None:
-        ins.append(got)
-        specs.append(pl.BlockSpec((1, SUB, LANES), lambda i, idx: (0, tall // SUB - 1, 0)))
-        kernel = pick_second_kernel
     return pl.pallas_call(
-        kernel,
+        functools.partial(pick_kernel, scatter=scatter),
         grid_spec=pltpu.PrefetchScalarGridSpec(
-            num_scalar_prefetch=1, grid=(1,), in_specs=specs, out_specs=whole(out)
+            num_scalar_prefetch=1, grid=(1,), in_specs=[whole(x.shape)], out_specs=whole(out)
         ),
         out_shape=jax.ShapeDtypeStruct(out, x.dtype),
         cost_estimate=pl.CostEstimate(flops=0, transcendentals=0, bytes_accessed=4 * x.size * 2),
-    )(index, *ins)
+    )(index, x)
+
+
+def insert_kernel(got_ref, chunks_ref, o_ref, block_ref, sem):
+    _, sub, _ = block_ref.shape
+    tall = o_ref.shape[1]
+    block_ref[...] = jnp.broadcast_to(got_ref[...], block_ref.shape)
+    copy = pltpu.make_async_copy(block_ref, o_ref.at[:, tall - sub :, :], sem)
+    copy.start()
+    copy.wait()
+
+
+def insert_block(got, chunks):
+    dests, tall, lanes = chunks.shape
+    return pl.pallas_call(
+        insert_kernel,
+        grid=(1,),
+        in_specs=[
+            pl.BlockSpec((1, SUB, lanes), lambda i: (0, tall // SUB - 1, 0)),
+            pl.BlockSpec(memory_space=pl.ANY),
+        ],
+        out_specs=pl.BlockSpec(memory_space=pl.ANY),
+        out_shape=jax.ShapeDtypeStruct(chunks.shape, chunks.dtype),
+        scratch_shapes=[pltpu.VMEM((dests, SUB, lanes), chunks.dtype), pltpu.SemaphoreType.DMA],
+        input_output_aliases={1: 0},
+        cost_estimate=pl.CostEstimate(
+            flops=0, transcendentals=0, bytes_accessed=4 * dests * SUB * lanes
+        ),
+        name="insert_block",
+    )(got, chunks)
 
 
 def pick_kv_kernel(index_ref, here_ref, *refs):
@@ -312,12 +324,12 @@
     )(place, *own, *ext)
 
 
-def random_kernel(index_ref, count_ref, *refs, groups, spread):
+def random_kernel(index_ref, count_ref, *refs, groups, spread, half):
     part_refs, whole_refs = refs[: spread * groups], refs[spread * groups : spread * groups + CAP - spread]
     q_ref, m_ref, l_ref, a_ref, o_ref, kv_ref, sems = refs[spread * groups + CAP - spread :]
-    lanes = q_ref.shape[1]
+    pieces, _, piece, lanes = q_ref.shape
+    halves = index_ref.shape[0] // (RANDOM * groups * (piece // TILE))
     step = pl.program_id(0)
-    per_step = q_ref.shape[0] // TILE
     part = TILE // groups
     shards = kv_ref.shape[0] // CAP
 
@@ -336,10 +348,11 @@
         for copy in copies:
             copy.wait()
 
-    for i in range(per_step):
-        t = step * per_step + i
-        rows = pl.ds(i * TILE, TILE)
-        q2 = split_heads(q_ref[rows, :])
+    for i in range(pieces * piece // TILE):
+        home, sub = divmod(i, piece // TILE)
+        t = ((step * pieces + home) * halves + half) * (piece // TILE) + sub
+        rows = (home, 0, pl.ds(sub * TILE, TILE))
+        q2 = split_heads(q_ref[rows])
         count = count_ref[t]
         at = [index_ref[t * RANDOM + j] for j in range(RANDOM)]
         scores = []
@@ -349,7 +362,7 @@
             s = score(q2, keys)
             scores.append(s)
             top = s if top is None else jnp.maximum(top, s)
-        m_old = m_ref[rows, :]
+        m_old = m_ref[rows]
         m_old = jnp.concatenate([m_old[:, :1], m_old[:, HEAD_DIM : HEAD_DIM + 1]], axis=0)
         m_new = jnp.maximum(jnp.max(top, axis=1, keepdims=True), m_old)
         alpha = jnp.exp2((m_old - m_new) * SCALE)
@@ -366,41 +379,42 @@
         total = acc[:, lanes:]
         acc = acc[:, :lanes]
         alpha = join_heads(alpha)
-        denominator = l_ref[rows, :] * alpha + join_heads(total)
-        numerator = a_ref[rows, :] * alpha + join_heads(acc)
-        o_ref[rows, :] = (numerator / denominator).astype(jnp.bfloat16)
-
-
-def random_attention(index, count, q, parts, whole, m, l, a, per_step=8):
+        denominator = l_ref[rows] * alpha + join_heads(total)
+        numerator = a_ref[rows] * alpha + join_heads(acc)
+        o_ref[home, pl.ds(sub * TILE, TILE)] = (numerator / denominator).astype(jnp.bfloat16)
+
+
+def random_attention(index, count, q, parts, whole, m, l, a, half, halves, pieces=4):
     rows, lanes = q.shape
     groups = len(parts[0])
     spread = len(parts)
     shards = whole[0].shape[0]
     part = TILE // groups
     flat = [f.reshape(-1, part, 2 * lanes) for slot in parts for f in slot]
-    block = pl.BlockSpec((per_step * TILE, lanes), lambda i, s, c: (i, 0))
+    piece = rows // (groups * halves)
+    block = pl.BlockSpec((pieces, 1, piece, lanes), lambda i, s, c: (i, half, 0, 0))
+    views = [x.reshape(groups, halves, piece, lanes) for x in (q, m, l, a)]
     keys = RANDOM * TILE
     sources = len(flat) + len(whole)
     return pl.pallas_call(
-        functools.partial(random_kernel, groups=groups, spread=spread),
+        functools.partial(random_kernel, groups=groups, spread=spread, half=half),
         grid_spec=pltpu.PrefetchScalarGridSpec(
             num_scalar_prefetch=2,
-            grid=(rows // (per_step * TILE),),
+            grid=(groups // pieces,),
             in_specs=[pl.BlockSpec(memory_space=pl.ANY)] * sources + [block] * 4,
-            out_specs=block,
+            out_specs=pl.BlockSpec((pieces, piece, lanes), lambda i, s, c: (i, 0, 0)),
             scratch_shapes=[
                 pltpu.VMEM((CAP * shards, TILE, 2 * lanes), jnp.bfloat16),
                 pltpu.SemaphoreType.DMA((sources,)),
             ],
         ),
-        out_shape=jax.ShapeDtypeStruct((rows, lanes), jnp.bfloat16),
+        out_shape=jax.ShapeDtypeStruct((groups, piece, lanes), jnp.bfloat16),
         cost_estimate=pl.CostEstimate(
-            flops=8 * rows * keys * lanes,
-            transcendentals=2 * rows * keys,
+            flops=8 * rows * keys * lanes // halves,
+            transcendentals=2 * rows * keys // halves,
             bytes_accessed=rows * lanes * 16 + CAP * shards * TILE * lanes * 4,
         ),
-        name="random_attention",
-    )(index, count, *flat, *whole, q, m, l, a)
+    )(index, count, *flat, *whole, *views)
 
 
 def request_tables(random_tiles, random_count, shard, ctx_count, tiles_here):
@@ -456,7 +470,9 @@
 
     fetched, got = [], None
     for slot in range(CAP - 1):
-        chunks = pick_chunks(send[slot], striped, ctx_count, got)
+        chunks = pick_chunks(send[slot], striped, ctx_count, slot == 0)
+        if slot:
+            chunks = insert_block(got, chunks)
         got = lax.all_to_all(chunks, "ctx", split_axis=0, concat_axis=0, tiled=True)
         count = ctx_count * part
         if slot == 0:
@@ -473,16 +489,20 @@
     where = jnp.stack([shard, jnp.int32(tiles_here * ctx_count), here])
     m, l, a, q = local_attention(where, own, ends)
     my_count = lax.dynamic_slice_in_dim(random_count, shard * tiles_here, tiles_here, 0)
-    attended = random_attention(read, my_count, q, fetched, [whole], m, l, a)
-    attended = attended.reshape(groups, rows, -1)
-    returned = lax.all_to_all(attended, "head", split_axis=0, concat_axis=0, tiled=True)
-    out = lax.dot_general(
-        returned,
-        w_out.reshape(groups, -1, width),
-        (((0, 2), (0, 1)), ((), ())),
-        preferred_element_type=jnp.float32,
-    )
-    return out.astype(jnp.bfloat16)
+    outs = []
+    for half in range(2):
+        mixed = random_attention(
+            read, my_count, q, fetched, [whole], m, l, a, half, 2, 4 - 2 * half
+        )
+        back = lax.all_to_all(mixed, "head", split_axis=0, concat_axis=0, tiled=True)
+        out = lax.dot_general(
+            back,
+            w_out.reshape(groups, -1, width),
+            (((0, 2), (0, 1)), ((), ())),
+            preferred_element_type=jnp.float32,
+        )
+        outs.append(out.astype(jnp.bfloat16))
+    return jnp.concatenate(outs, axis=0)
 
 
 def solution(mesh):

time: 298 us -> 303 us (1.017)
  blocking collectives: 61.6 us -> 0 us
  waiting for transfers between devices: 70.2 us -> 105 us
  starting transfers between devices: 68.3 us -> 88.8 us
  Pallas kernels: 80.9 us -> 89.5 us
    all_to_all x2 -> x0, blocking collectives: 61.6 us -> none  [the longest x1 41.5 us: body(): got = lax.all_to_all(chunks, 'ctx', split_axis=0, concat_axis=0, tiled=True)]
    all_to_all x1 -> x2, waiting for transfers between devices: 0.01 us -> 26 us  [body(): got = lax.all_to_all(chunks, 'ctx', split_axis=0, concat_axis=0, tiled=True)]
    all_to_all x1 -> x2, starting transfers between devices: 5.46 us -> 17.1 us  [body(): got = lax.all_to_all(chunks, 'ctx', split_axis=0, concat_axis=0, tiled=True)]
    all_to_all x0 -> x2, starting transfers between devices: none -> 8.9 us  [body(): lax.all_to_all(mixed, 'head', split_axis=0, concat_axis=0, tiled=True)]
    all_to_all x0 -> x2, waiting for transfers between devices: none -> 8.8 us  [body(): lax.all_to_all(mixed, 'head', split_axis=0, concat_axis=0, tiled=True)]
    pallas_call x1 -> x2, Pallas kernels: 24.1 us -> 31.4 us  [random_attention(): pl.pallas_call(functools.partial(random_kernel, groups=groups, spread=spr...]
    pallas_call x2 -> x3, Pallas kernels: 6.41 us -> 7.71 us  [the longest x2 6.39 us: pick_chunks(): pl.pallas_call(functools.partial(pick_kernel, scatter=scatter), grid_spec...]
  transfers between devices with their start and end apart: 33 -> 36, of which waited for: 10 -> 12; matrix products, arithmetic and copies ran while one was open for 3% -> 4% of each run, Pallas kernels for 17% -> 23%
where the time goes in v7:
time: 303 us; the launch traced here: 302 us
  waiting for transfers between devices  105 us (35%)
  Pallas kernels  89.5 us (30%)
  starting transfers between devices  88.8 us (29%)
  local copies, waits for them, and re-layouts  10.3 us (3%)
  other arithmetic  5.6 us (2%)
    ppermute x28, starting transfers between devices, exchange(): lax.ppermute(pieces[o], axis, [(i, (i + o) % size) for i in range(size)])  42.6 us
    pallas_call x2, Pallas kernels, random_attention(): pl.pallas_call(functools.partial(random_kernel, groups=groups, spread=spr...  31.4 us
    ppermute x28, waiting for transfers between devices, exchange(): lax.ppermute(pieces[o], axis, [(i, (i + o) % size) for i in range(size)])  29.6 us
    pallas_call x3, Pallas kernels, project(): pl.pallas_call(functools.partial(project_kernel, sources=len(xs), weights...  29.2 us
    all_to_all x2, waiting for transfers between devices, body(): got = lax.all_to_all(chunks, 'ctx', split_axis=0, concat_axis=0, tiled=True)  26 us
    ppermute x1, waiting for transfers between devices, body(): before = lax.ppermute(striped[-1:], 'ctx', up)  25.6 us
    all_to_all x2, starting transfers between devices, body(): got = lax.all_to_all(chunks, 'ctx', split_axis=0, concat_axis=0, tiled=True)  17.1 us
    pallas_call x1, Pallas kernels, local_attention(): pl.pallas_call(functools.partial(local_kernel, groups=groups), grid_spec=...  17 us
  transfers between devices with their start and end apart: 36, of which 12 were waited for; matrix products, arithmetic and copies ran while one was open for 4% of the time, Pallas kernels for 23%

profile of v7, /device:TPU:6, one launch (start us, length us, event | category | flops | bytes accessed | tf_op | source)
XLA Modules:
  0.0 301.6 jit_solution(1502670014692643249)
XLA Ops:
  2.5 4.5 %all-to-all-start = ((bf16[8,4,16,1024]{3,2,1,0:T(8,128)(2,1)}), bf16[8,4,16,1024]{3,2,1,0:T(8,128)(2,1)S(1)}, u32[]{:S(2)}, u32[]{:S(2)}) async-start(bf16[8,4,16,1024]{3,2,1,0:T(8,128)(2,1)} %bitcast.60), calls=%async_computation | async-start | bytes 2097152 | tf_op jit(solution)/shard_map/all_to_all | solution.py:457
  11.4 11.4 %all-to-all-done = bf16[8,4,16,1024]{3,2,1,0:T(8,128)(2,1)S(1)} async-done(((bf16[8,4,16,1024]{3,2,1,0:T(8,128)(2,1)}), bf16[8,4,16,1024]{3,2,1,0:T(8,128)(2,1)S(1)}, u32[]{:S(2)}, u32[]{:S(2)}) %all-to-all-start) | async-done | bytes 1048608 | tf_op jit(solution)/shard_map/all_to_all | solution.py:457
  23.8 3.2 %shard_map.73 = bf16[32,136,128]{2,1,0:T(8,128)(2,1)} custom-call(s32[32]{0:T(128)} %get-tuple-element.83.index_ref, bf16[32,16,1024]{2,1,0:T(8,128)(2,1)} %bitcast.49), custom_call_target="tpu_custom_call" | custom-call | bytes 4194304 | tf_op jit(solution)/shard_map/pallas_call | solution.py:142
  27.0 11.6 %all-to-all-start.1 = ((bf16[32,136,128]{2,1,0:T(8,128)(2,1)}), bf16[32,136,128]{2,1,0:T(8,128)(2,1)S(1)}, u32[]{:S(2)}, u32[]{:S(2)}) async-start(bf16[32,136,128]{2,1,0:T(8,128)(2,1)} %shard_map.73), calls=%async_computation.1 | async-start | bytes 2228224 | tf_op jit(solution)/shard_map/all_to_all | solution.py:476
  38.6 3.2 %shard_map.75.chunks_ref = bf16[32,136,128]{2,1,0:T(8,128)(2,1)} custom-call(s32[32]{0:T(128)} %get-tuple-element.82.index_ref, bf16[32,16,1024]{2,1,0:T(8,128)(2,1)} %bitcast.50), custom_call_target="tpu_custom_call" | custom-call | bytes 4194304 | tf_op jit(solution)/shard_map/pallas_call | solution.py:142
  41.8 26.0 %all-to-all-done.1.refs_0_.got_ref = bf16[32,136,128]{2,1,0:T(8,128)(2,1)S(1)} async-done(((bf16[32,136,128]{2,1,0:T(8,128)(2,1)}), bf16[32,136,128]{2,1,0:T(8,128)(2,1)S(1)}, u32[]{:S(2)}, u32[]{:S(2)}) %all-to-all-start.1) | async-done | bytes 1114144 | tf_op jit(solution)/shard_map/all_to_all | solution.py:476
  70.1 5.6 %all-to-all-start.2 = ((bf16[32,136,128]{2,1,0:T(8,128)(2,1)}), bf16[32,136,128]{2,1,0:T(8,128)(2,1)S(1)}, u32[]{:S(2)}, u32[]{:S(2)}) async-start(bf16[32,136,128]{2,1,0:T(8,128)(2,1)} %insert_block.1), calls=%async_computation.2 | async-start | bytes 2228224 | tf_op jit(solution)/shard_map/all_to_all | solution.py:476
  75.7 10.9 %shard_map.77 = (bf16[512,384]{1,0:T(8,128)(2,1)}, bf16[512,384]{1,0:T(8,128)(2,1)}, bf16[512,384]{1,0:T(8,128)(2,1)}, bf16[512,384]{1,0:T(8,128)(2,1)}, bf16[51...) custom-call(s32[1]{0:T(128)} %bitcast.here_ref, ...), custom_call_target="tpu_custom_call" | custom-call | flops 3221225472 | bytes 10485760 | tf_op jit(solution)/shard_map/pallas_call | solution.py:78
  88.7 2.7 collective-permute-start.19
  92.3 6.6 %collective-permute-done.16.refs_1_ = bf16[512,384]{1,0:T(8,128)(2,1)} collective-permute-done((bf16[512,384]{1,0:T(8,128)(2,1)}, bf16[512,384]{1,0:T(8,128)(2,1)}, u32[]{:S(2)}, u32[]{:S(2)}) %collective-permute-start.16) | collective-permute-done | bytes 393248 | tf_op jit(solution)/shard_map/ppermute | solution.py:107
  100.3 6.8 %collective-permute-start.22 = (bf16[512,384]{1,0:T(8,128)(2,1)}, bf16[512,384]{1,0:T(8,128)(2,1)}, u32[]{:S(2)}, u32[]{:S(2)}) collective-permute-start(bf16[512,384]{1,0:T(8,128)(2,1)} %get-tuple-element.64), channel_id=1, source_target_pairs={{0,7},{1,0},{2,1},{3,2},{4,3},{5,4},{6,5},{7,6},{8,15},{9,8},{10,9... | collective-permute-start | bytes 1179656 | tf_op jit(solution)/shard_map/ppermute | solution.py:107
  107.1 8.2 %collective-permute-done.18.refs_3_ = bf16[512,384]{1,0:T(8,128)(2,1)} collective-permute-done((bf16[512,384]{1,0:T(8,128)(2,1)}, bf16[512,384]{1,0:T(8,128)(2,1)}, u32[]{:S(2)}, u32[]{:S(2)}) %collective-permute-start.18) | collective-permute-done | bytes 393248 | tf_op jit(solution)/shard_map/ppermute | solution.py:107
  116.6 5.2 %collective-permute-done.20.refs_5_ = bf16[512,384]{1,0:T(8,128)(2,1)} collective-permute-done((bf16[512,384]{1,0:T(8,128)(2,1)}, bf16[512,384]{1,0:T(8,128)(2,1)}, u32[]{:S(2)}, u32[]{:S(2)}) %collective-permute-start.20) | collective-permute-done | bytes 393248 | tf_op jit(solution)/shard_map/ppermute | solution.py:107
  121.8 3.0 %collective-permute-done.22.refs_7_ = bf16[512,384]{1,0:T(8,128)(2,1)} collective-permute-done((bf16[512,384]{1,0:T(8,128)(2,1)}, bf16[512,384]{1,0:T(8,128)(2,1)}, u32[]{:S(2)}, u32[]{:S(2)}) %collective-permute-start.22) | collective-permute-done | bytes 393248 | tf_op jit(solution)/shard_map/ppermute | solution.py:107
  124.8 4.2 %pick_kv.1 = bf16[32,128,256]{2,1,0:T(8,128)(2,1)} custom-call(s32[32]{0:T(128)} %get-tuple-element.81.index_ref, s32[1]{0:T(128)} %bitcast.here_ref, bf16[512,384]{1,0:T(8,128)(2,1)} %get-tuple-element.57.refs_0_, bf16[512,384]{1,0:T(8,128)(2,1)} %collective-permute-done.16.refs_1_, bf16[512,384]{1,0:T(8,128)(2,1)} %collective-permute-done.17.refs_2_, ...), custom_call_target="tpu_custom_call" | custom-call | bytes 5242880 | tf_op jit(solution)/shard_map/pick_kv/pallas_call | solution.py:203
  130.1 9.8 %all-to-all-start.3 = ((bf16[32,128,256]{2,1,0:T(8,128)(2,1)}), bf16[32,128,256]{2,1,0:T(8,128)(2,1)}, u32[]{:S(2)}, u32[]{:S(2)}) async-start(bf16[32,128,256]{2,1,0:T(8,128)(2,1)} %pick_kv.1), calls=%async_computation.3 | async-start | bytes 4194304 | tf_op jit(solution)/shard_map/all_to_all | solution.py:487
  141.2 3.4 %collective-permute-start.7 = (bf16[1,16,1024]{2,1,0:T(8,128)(2,1)S(1)}, bf16[1,16,1024]{2,1,0:T(8,128)(2,1)S(1)}, u32[]{:S(2)}, u32[]{:S(2)}) collective-permute-start(bf16[1,16,1024]{2,1,0:T(8,128)(2,1)S(1)} %get-tuple-element.77), channel_id=1, source_target_pairs={{0,8},{8,16},{16,24},{24,32},{32,40},{40,48},{48,56},{56,64},{64,7... | collective-permute-start | bytes 98312 | tf_op jit(solution)/shard_map/ppermute | solution.py:467
  147.0 8.9 %shard_map.74 = (bf16[512,256]{1,0:T(8,128)(2,1)}, bf16[512,256]{1,0:T(8,128)(2,1)}, bf16[512,256]{1,0:T(8,128)(2,1)}, bf16[512,256]{1,0:T(8,128)(2,1)}, bf16[51...) custom-call(s32[1]{0:T(128)} %bitcast.here_ref, ...), custom_call_target="tpu_custom_call" | custom-call | flops 2147483648 | bytes 7340032 | tf_op jit(solution)/shard_map/pallas_call | solution.py:78
  159.3 25.6 %collective-permute-done.7 = bf16[1,16,1024]{2,1,0:T(8,128)(2,1)S(1)} collective-permute-done((bf16[1,16,1024]{2,1,0:T(8,128)(2,1)S(1)}, bf16[1,16,1024]{2,1,0:T(8,128)(2,1)S(1)}, u32[]{:S(2)}, u32[]{:S(2)}) %collective-permute-start.7) | collective-permute-done | bytes 32800 | tf_op jit(solution)/shard_map/ppermute | solution.py:467
  185.0 3.4 %collective-permute-done.8 = bf16[1,16,1024]{2,1,0:T(8,128)(2,1)S(1)} collective-permute-done((bf16[1,16,1024]{2,1,0:T(8,128)(2,1)S(1)}, bf16[1,16,1024]{2,1,0:T(8,128)(2,1)S(1)}, u32[]{:S(2)}, u32[]{:S(2)}) %collective-permute-start.8) | collective-permute-done | bytes 32800 | tf_op jit(solution)/shard_map/ppermute | solution.py:468
  189.6 3.9 %collective-permute-start.3 = (bf16[512,256]{1,0:T(8,128)(2,1)}, bf16[512,256]{1,0:T(8,128)(2,1)}, u32[]{:S(2)}, u32[]{:S(2)}) collective-permute-start(bf16[512,256]{1,0:T(8,128)(2,1)} %get-tuple-element.45), channel_id=1, source_target_pairs={{0,4},{1,5},{2,6},{3,7},{4,0},{5,1},{6,2},{7,3},{8,12},{9,13},{10,... | collective-permute-start | bytes 786440 | tf_op jit(solution)/shard_map/ppermute | solution.py:107
  193.5 9.3 %shard_map.76 = (bf16[512,256]{1,0:T(8,128)(2,1)}, bf16[512,256]{1,0:T(8,128)(2,1)}, bf16[512,256]{1,0:T(8,128)(2,1)}, bf16[512,256]{1,0:T(8,128)(2,1)}, bf16[51...) custom-call(s32[1]{0:T(128)} %bitcast.here_ref, ...), custom_call_target="tpu_custom_call" | custom-call | flops 2415919104 | bytes 7733248 | tf_op jit(solution)/shard_map/pallas_call | solution.py:78
  203.1 3.1 %collective-permute-start.25 = (bf16[64,256]{1,0:T(8,128)(2,1)}, bf16[64,256]{1,0:T(8,128)(2,1)}, u32[]{:S(2)}, u32[]{:S(2)}) collective-permute-start(bf16[64,256]{1,0:T(8,128)(2,1)} %get-tuple-element.68), channel_id=1, source_target_pairs={{0,3},{1,4},{2,5},{3,6},{4,7},{5,0},{6,1},{7,2},{8,11},{9,12},{10,... | collective-permute-start | bytes 98312 | tf_op jit(solution)/shard_map/ppermute | solution.py:107
  206.2 7.5 %collective-permute-start.26 = (bf16[64,256]{1,0:T(8,128)(2,1)}, bf16[64,256]{1,0:T(8,128)(2,1)}, u32[]{:S(2)}, u32[]{:S(2)}) collective-permute-start(bf16[64,256]{1,0:T(8,128)(2,1)} %get-tuple-element.69), channel_id=1, source_target_pairs={{0,4},{1,5},{2,6},{3,7},{4,0},{5,1},{6,2},{7,3},{8,12},{9,13},{10,... | collective-permute-start | bytes 98312 | tf_op jit(solution)/shard_map/ppermute | solution.py:107
  213.9 2.5 collective-permute-start.10
  220.2 3.9 %collective-permute-done.27.refs_13_ = bf16[64,256]{1,0:T(8,128)(2,1)S(1)} collective-permute-done((bf16[64,256]{1,0:T(8,128)(2,1)}, bf16[64,256]{1,0:T(8,128)(2,1)S(1)}, u32[]{:S(2)}, u32[]{:S(2)}) %collective-permute-start.27) | collective-permute-done | bytes 32800 | tf_op jit(solution)/shard_map/ppermute | solution.py:107
  232.1 17.0 %local_attention.1 = (f32[4096,128]{1,0:T(8,128)}, f32[4096,128]{1,0:T(8,128)}, f32[4096,128]{1,0:T(8,128)}, bf16[4096,128]{1,0:T(8,128)(2,1)}) custom-call(s32[3]{0:T(128)} %pad_add_fusion.place_ref, bf16[512,384]{1,0:T(8,128)(2,1)} %get-tuple-element.57.refs_0_, bf16[512,384]{1,0:T(8,128)(2,1)} %collective-permute-done.16.refs_1_, ...), custom_call_target="tpu_custom_call" | custom-call | flops 2684354560 | bytes 10485760 | tf_op jit(solution)/shard_map/local_attention/pallas_call | solution.py:304
  249.3 15.0 %shard_map.78 = bf16[8,256,128]{2,1,0:T(8,128)(2,1)} custom-call(s32[384]{0:T(512)} %add_select_fusion.2.index_ref, s32[32]{0:T(128)} %dynamic_slice.8.count_ref, bf16[32,16,256]{2,1,0:T(8,128)(2,1)} %bitcast.61, bf16[32,16,256]{2,1,0:T(8,128)(2,1)} %bitcast.69, bf16[32,16,256]{2,1,0:T(8,128)(2,1)} %bitcast.71, bf16[32,16,256]{2,1,0:T(8,128)(2,1)} %bitcast.8.refs_3_, ...), custom_call_target="tpu_custom_call" | custom-call | flops 3221225472 | bytes 14680064 | tf_op jit(solution)/shard_map/pallas_call | solution.py:399
  264.3 4.1 %all-to-all-start.4 = ((bf16[8,256,128]{2,1,0:T(8,128)(2,1)}), bf16[8,256,128]{2,1,0:T(8,128)(2,1)S(1)}, u32[]{:S(2)}, u32[]{:S(2)}) async-start(bf16[8,256,128]{2,1,0:T(8,128)(2,1)} %shard_map.78), calls=%async_computation.4 | async-start | bytes 1048576 | tf_op jit(solution)/shard_map/all_to_all | solution.py:497
  268.4 16.4 %shard_map.79 = bf16[8,256,128]{2,1,0:T(8,128)(2,1)} custom-call(s32[384]{0:T(512)} %add_select_fusion.2.index_ref, s32[32]{0:T(128)} %dynamic_slice.8.count_ref, bf16[32,16,256]{2,1,0:T(8,128)(2,1)} %bitcast.62, bf16[32,16,256]{2,1,0:T(8,128)(2,1)} %bitcast.70, bf16[32,16,256]{2,1,0:T(8,128)(2,1)} %bitcast.72, bf16[32,16,256]{2,1,0:T(8,128)(2,1)} %bitcast.8.refs_3_, ...), custom_call_target="tpu_custom_call" | custom-call | flops 3221225472 | bytes 14680064 | tf_op jit(solution)/shard_map/pallas_call | solution.py:399
  284.7 4.8 %all-to-all-start.5 = ((bf16[8,256,128]{2,1,0:T(8,128)(2,1)}), bf16[8,256,128]{2,1,0:T(8,128)(2,1)S(1)}, u32[]{:S(2)}, u32[]{:S(2)}) async-start(bf16[8,256,128]{2,1,0:T(8,128)(2,1)} %shard_map.79), calls=%async_computation.5 | async-start | bytes 1048576 | tf_op jit(solution)/shard_map/all_to_all | solution.py:497
  291.1 8.8 %all-to-all-done.5 = bf16[8,256,128]{2,1,0:T(8,128)(2,1)S(1)} async-done(((bf16[8,256,128]{2,1,0:T(8,128)(2,1)}), bf16[8,256,128]{2,1,0:T(8,128)(2,1)S(1)}, u32[]{:S(2)}, u32[]{:S(2)}) %all-to-all-start.5) | async-done | bytes 524320 | tf_op jit(solution)/shard_map/all_to_all | solution.py:497
  (118 shorter events, 40.7 us)
Async XLA Ops:
  2.5 20.4 %all-to-all-start = ((bf16[8,4,16,1024]{3,2,1,0:T(8,128)(2,1)}), bf16[8,4,16,1024]{3,2,1,0:T(8,128)(2,1)S(1)}, u32[]{:S(2)}, u32[]{:S(2)}) async-start(bf16[8,4,16,1024]{3,2,1,0:T(8,128)(2,1)} %bitcast.60), calls=%async_computation | async-start | bytes 2097152 | tf_op jit(solution)/shard_map/all_to_all | solution.py:457
  27.0 40.7 %all-to-all-start.1 = ((bf16[32,136,128]{2,1,0:T(8,128)(2,1)}), bf16[32,136,128]{2,1,0:T(8,128)(2,1)S(1)}, u32[]{:S(2)}, u32[]{:S(2)}) async-start(bf16[32,136,128]{2,1,0:T(8,128)(2,1)} %shard_map.73), calls=%async_computation.1 | async-start | bytes 2228224 | tf_op jit(solution)/shard_map/all_to_all | solution.py:476
  70.1 58.9 %all-to-all-start.2 = ((bf16[32,136,128]{2,1,0:T(8,128)(2,1)}), bf16[32,136,128]{2,1,0:T(8,128)(2,1)S(1)}, u32[]{:S(2)}, u32[]{:S(2)}) async-start(bf16[32,136,128]{2,1,0:T(8,128)(2,1)} %insert_block.1), calls=%async_computation.2 | async-start | bytes 2228224 | tf_op jit(solution)/shard_map/all_to_all | solution.py:476
  86.7 12.3 %collective-permute-start.16 = (bf16[512,384]{1,0:T(8,128)(2,1)}, bf16[512,384]{1,0:T(8,128)(2,1)}, u32[]{:S(2)}, u32[]{:S(2)}) collective-permute-start(bf16[512,384]{1,0:T(8,128)(2,1)} %get-tuple-element.58), channel_id=1, source_target_pairs={{0,1},{1,2},{2,3},{3,4},{4,5},{5,6},{6,7},{7,0},{8,9},{9,10},{10,1... | collective-permute-start | bytes 1179656 | tf_op jit(solution)/shard_map/ppermute | solution.py:107
  86.7 13.6 %collective-permute-start.17 = (bf16[512,384]{1,0:T(8,128)(2,1)}, bf16[512,384]{1,0:T(8,128)(2,1)}, u32[]{:S(2)}, u32[]{:S(2)}) collective-permute-start(bf16[512,384]{1,0:T(8,128)(2,1)} %get-tuple-element.59), channel_id=1, source_target_pairs={{0,2},{1,3},{2,4},{3,5},{4,6},{5,7},{6,0},{7,1},{8,10},{9,11},{10,... | collective-permute-start | bytes 1179656 | tf_op jit(solution)/shard_map/ppermute | solution.py:107
  87.3 28.0 %collective-permute-start.18 = (bf16[512,384]{1,0:T(8,128)(2,1)}, bf16[512,384]{1,0:T(8,128)(2,1)}, u32[]{:S(2)}, u32[]{:S(2)}) collective-permute-start(bf16[512,384]{1,0:T(8,128)(2,1)} %get-tuple-element.60), channel_id=1, source_target_pairs={{0,3},{1,4},{2,5},{3,6},{4,7},{5,0},{6,1},{7,2},{8,11},{9,12},{10,... | collective-permute-start | bytes 1179656 | tf_op jit(solution)/shard_map/ppermute | solution.py:107
  88.7 27.9 %collective-permute-start.19 = (bf16[512,384]{1,0:T(8,128)(2,1)}, bf16[512,384]{1,0:T(8,128)(2,1)}, u32[]{:S(2)}, u32[]{:S(2)}) collective-permute-start(bf16[512,384]{1,0:T(8,128)(2,1)} %get-tuple-element.61), channel_id=1, source_target_pairs={{0,4},{1,5},{2,6},{3,7},{4,0},{5,1},{6,2},{7,3},{8,12},{9,13},{10,... | collective-permute-start | bytes 1179656 | tf_op jit(solution)/shard_map/ppermute | solution.py:107
  91.4 30.4 %collective-permute-start.20 = (bf16[512,384]{1,0:T(8,128)(2,1)}, bf16[512,384]{1,0:T(8,128)(2,1)}, u32[]{:S(2)}, u32[]{:S(2)}) collective-permute-start(bf16[512,384]{1,0:T(8,128)(2,1)} %get-tuple-element.62), channel_id=1, source_target_pairs={{0,5},{1,6},{2,7},{3,0},{4,1},{5,2},{6,3},{7,4},{8,13},{9,14},{10,... | collective-permute-start | bytes 1179656 | tf_op jit(solution)/shard_map/ppermute | solution.py:107
  99.0 22.8 %collective-permute-start.21 = (bf16[512,384]{1,0:T(8,128)(2,1)}, bf16[512,384]{1,0:T(8,128)(2,1)}, u32[]{:S(2)}, u32[]{:S(2)}) collective-permute-start(bf16[512,384]{1,0:T(8,128)(2,1)} %get-tuple-element.63), channel_id=1, source_target_pairs={{0,6},{1,7},{2,0},{3,1},{4,2},{5,3},{6,4},{7,5},{8,14},{9,15},{10,... | collective-permute-start | bytes 1179656 | tf_op jit(solution)/shard_map/ppermute | solution.py:107
  100.3 24.5 %collective-permute-start.22 = (bf16[512,384]{1,0:T(8,128)(2,1)}, bf16[512,384]{1,0:T(8,128)(2,1)}, u32[]{:S(2)}, u32[]{:S(2)}) collective-permute-start(bf16[512,384]{1,0:T(8,128)(2,1)} %get-tuple-element.64), channel_id=1, source_target_pairs={{0,7},{1,0},{2,1},{3,2},{4,3},{5,4},{6,5},{7,6},{8,15},{9,8},{10,9... | collective-permute-start | bytes 1179656 | tf_op jit(solution)/shard_map/ppermute | solution.py:107
  130.1 119.1 %all-to-all-start.3 = ((bf16[32,128,256]{2,1,0:T(8,128)(2,1)}), bf16[32,128,256]{2,1,0:T(8,128)(2,1)}, u32[]{:S(2)}, u32[]{:S(2)}) async-start(bf16[32,128,256]{2,1,0:T(8,128)(2,1)} %pick_kv.1), calls=%async_computation.3 | async-start | bytes 4194304 | tf_op jit(solution)/shard_map/all_to_all | solution.py:487
  141.2 43.8 %collective-permute-start.7 = (bf16[1,16,1024]{2,1,0:T(8,128)(2,1)S(1)}, bf16[1,16,1024]{2,1,0:T(8,128)(2,1)S(1)}, u32[]{:S(2)}, u32[]{:S(2)}) collective-permute-start(bf16[1,16,1024]{2,1,0:T(8,128)(2,1)S(1)} %get-tuple-element.77), channel_id=1, source_target_pairs={{0,8},{8,16},{16,24},{24,32},{32,40},{40,48},{48,56},{56,64},{64,7... | collective-permute-start | bytes 98312 | tf_op jit(solution)/shard_map/ppermute | solution.py:467
  144.5 43.8 %collective-permute-start.8 = (bf16[1,16,1024]{2,1,0:T(8,128)(2,1)S(1)}, bf16[1,16,1024]{2,1,0:T(8,128)(2,1)S(1)}, u32[]{:S(2)}, u32[]{:S(2)}) collective-permute-start(bf16[1,16,1024]{2,1,0:T(8,128)(2,1)S(1)} %get-tuple-element.78), channel_id=1, source_target_pairs={{8,0},{16,8},{24,16},{32,24},{40,32},{48,40},{56,48},{64,56},{72,6... | collective-permute-start | bytes 98312 | tf_op jit(solution)/shard_map/ppermute | solution.py:468
  155.9 33.1 %collective-permute-start.4 = (bf16[512,256]{1,0:T(8,128)(2,1)}, bf16[512,256]{1,0:T(8,128)(2,1)S(1)}, u32[]{:S(2)}, u32[]{:S(2)}) collective-permute-start(bf16[512,256]{1,0:T(8,128)(2,1)} %get-tuple-element.46), channel_id=1, source_target_pairs={{0,5},{1,6},{2,7},{3,0},{4,1},{5,2},{6,3},{7,4},{8,13},{9,14},{10,... | collective-permute-start | bytes 786440 | tf_op jit(solution)/shard_map/ppermute | solution.py:107
  156.1 33.5 %collective-permute-start.5 = (bf16[512,256]{1,0:T(8,128)(2,1)}, bf16[512,256]{1,0:T(8,128)(2,1)S(1)}, u32[]{:S(2)}, u32[]{:S(2)}) collective-permute-start(bf16[512,256]{1,0:T(8,128)(2,1)} %get-tuple-element.47), channel_id=1, source_target_pairs={{0,6},{1,7},{2,0},{3,1},{4,2},{5,3},{6,4},{7,5},{8,14},{9,15},{10,... | collective-permute-start | bytes 786440 | tf_op jit(solution)/shard_map/ppermute | solution.py:107
  158.9 44.0 %collective-permute-start.6 = (bf16[512,256]{1,0:T(8,128)(2,1)}, bf16[512,256]{1,0:T(8,128)(2,1)S(1)}, u32[]{:S(2)}, u32[]{:S(2)}) collective-permute-start(bf16[512,256]{1,0:T(8,128)(2,1)} %get-tuple-element.48), channel_id=1, source_target_pairs={{0,7},{1,0},{2,1},{3,2},{4,3},{5,4},{6,5},{7,6},{8,15},{9,8},{10,9... | collective-permute-start | bytes 786440 | tf_op jit(solution)/shard_map/ppermute | solution.py:107
  189.0 14.0 %collective-permute-start = (bf16[512,256]{1,0:T(8,128)(2,1)}, bf16[512,256]{1,0:T(8,128)(2,1)S(1)}, u32[]{:S(2)}, u32[]{:S(2)}) collective-permute-start(bf16[512,256]{1,0:T(8,128)(2,1)} %get-tuple-element.42), channel_id=1, source_target_pairs={{0,1},{1,2},{2,3},{3,4},{4,5},{5,6},{6,7},{7,0},{8,9},{9,10},{10,1... | collective-permute-start | bytes 786440 | tf_op jit(solution)/shard_map/ppermute | solution.py:107
  189.0 14.1 %collective-permute-start.1 = (bf16[512,256]{1,0:T(8,128)(2,1)}, bf16[512,256]{1,0:T(8,128)(2,1)S(1)}, u32[]{:S(2)}, u32[]{:S(2)}) collective-permute-start(bf16[512,256]{1,0:T(8,128)(2,1)} %get-tuple-element.43), channel_id=1, source_target_pairs={{0,2},{1,3},{2,4},{3,5},{4,6},{5,7},{6,0},{7,1},{8,10},{9,11},{10,... | collective-permute-start | bytes 786440 | tf_op jit(solution)/shard_map/ppermute | solution.py:107
  189.1 17.2 %collective-permute-start.2 = (bf16[512,256]{1,0:T(8,128)(2,1)}, bf16[512,256]{1,0:T(8,128)(2,1)}, u32[]{:S(2)}, u32[]{:S(2)}) collective-permute-start(bf16[512,256]{1,0:T(8,128)(2,1)} %get-tuple-element.44), channel_id=1, source_target_pairs={{0,3},{1,4},{2,5},{3,6},{4,7},{5,0},{6,1},{7,2},{8,11},{9,12},{10,... | collective-permute-start | bytes 786440 | tf_op jit(solution)/shard_map/ppermute | solution.py:107
  189.6 24.1 %collective-permute-start.3 = (bf16[512,256]{1,0:T(8,128)(2,1)}, bf16[512,256]{1,0:T(8,128)(2,1)}, u32[]{:S(2)}, u32[]{:S(2)}) collective-permute-start(bf16[512,256]{1,0:T(8,128)(2,1)} %get-tuple-element.45), channel_id=1, source_target_pairs={{0,4},{1,5},{2,6},{3,7},{4,0},{5,1},{6,2},{7,3},{8,12},{9,13},{10,... | collective-permute-start | bytes 786440 | tf_op jit(solution)/shard_map/ppermute | solution.py:107
  203.0 13.8 %collective-permute-start.24 = (bf16[64,256]{1,0:T(8,128)(2,1)}, bf16[64,256]{1,0:T(8,128)(2,1)S(1)}, u32[]{:S(2)}, u32[]{:S(2)}) collective-permute-start(bf16[64,256]{1,0:T(8,128)(2,1)} %get-tuple-element.67), channel_id=1, source_target_pairs={{0,2},{1,3},{2,4},{3,5},{4,6},{5,7},{6,0},{7,1},{8,10},{9,11},{10,... | collective-permute-start | bytes 98312 | tf_op jit(solution)/shard_map/ppermute | solution.py:107
  203.1 15.1 %collective-permute-start.25 = (bf16[64,256]{1,0:T(8,128)(2,1)}, bf16[64,256]{1,0:T(8,128)(2,1)}, u32[]{:S(2)}, u32[]{:S(2)}) collective-permute-start(bf16[64,256]{1,0:T(8,128)(2,1)} %get-tuple-element.68), channel_id=1, source_target_pairs={{0,3},{1,4},{2,5},{3,6},{4,7},{5,0},{6,1},{7,2},{8,11},{9,12},{10,... | collective-permute-start | bytes 98312 | tf_op jit(solution)/shard_map/ppermute | solution.py:107
  206.2 13.4 %collective-permute-start.26 = (bf16[64,256]{1,0:T(8,128)(2,1)}, bf16[64,256]{1,0:T(8,128)(2,1)}, u32[]{:S(2)}, u32[]{:S(2)}) collective-permute-start(bf16[64,256]{1,0:T(8,128)(2,1)} %get-tuple-element.69), channel_id=1, source_target_pairs={{0,4},{1,5},{2,6},{3,7},{4,0},{5,1},{6,2},{7,3},{8,12},{9,13},{10,... | collective-permute-start | bytes 98312 | tf_op jit(solution)/shard_map/ppermute | solution.py:107
  213.7 14.4 %collective-permute-start.9 = (bf16[512,256]{1,0:T(8,128)(2,1)}, bf16[512,256]{1,0:T(8,128)(2,1)S(1)}, u32[]{:S(2)}, u32[]{:S(2)}) collective-permute-start(bf16[512,256]{1,0:T(8,128)(2,1)} %get-tuple-element.50), channel_id=1, source_target_pairs={{0,1},{1,2},{2,3},{3,4},{4,5},{5,6},{6,7},{7,0},{8,9},{9,10},{10,1... | collective-permute-start | bytes 786440 | tf_op jit(solution)/shard_map/ppermute | solution.py:107
  213.9 16.5 %collective-permute-start.10 = (bf16[512,256]{1,0:T(8,128)(2,1)}, bf16[512,256]{1,0:T(8,128)(2,1)S(1)}, u32[]{:S(2)}, u32[]{:S(2)}) collective-permute-start(bf16[512,256]{1,0:T(8,128)(2,1)} %get-tuple-element.51), channel_id=1, source_target_pairs={{0,2},{1,3},{2,4},{3,5},{4,6},{5,7},{6,0},{7,1},{8,10},{9,11},{10,... | collective-permute-start | bytes 786440 | tf_op jit(solution)/shard_map/ppermute | solution.py:107
  224.2 25.0 %collective-permute-start.11 = (bf16[512,256]{1,0:T(8,128)(2,1)}, bf16[512,256]{1,0:T(8,128)(2,1)}, u32[]{:S(2)}, u32[]{:S(2)}) collective-permute-start(bf16[512,256]{1,0:T(8,128)(2,1)} %get-tuple-element.52), channel_id=1, source_target_pairs={{0,3},{1,4},{2,5},{3,6},{4,7},{5,0},{6,1},{7,2},{8,11},{9,12},{10,... | collective-permute-start | bytes 786440 | tf_op jit(solution)/shard_map/ppermute | solution.py:107
  224.2 25.0 %collective-permute-start.12 = (bf16[512,256]{1,0:T(8,128)(2,1)}, bf16[512,256]{1,0:T(8,128)(2,1)}, u32[]{:S(2)}, u32[]{:S(2)}) collective-permute-start(bf16[512,256]{1,0:T(8,128)(2,1)} %get-tuple-element.53), channel_id=1, source_target_pairs={{0,4},{1,5},{2,6},{3,7},{4,0},{5,1},{6,2},{7,3},{8,12},{9,13},{10,... | collective-permute-start | bytes 786440 | tf_op jit(solution)/shard_map/ppermute | solution.py:107
  226.1 23.1 %collective-permute-start.13 = (bf16[512,256]{1,0:T(8,128)(2,1)}, bf16[512,256]{1,0:T(8,128)(2,1)}, u32[]{:S(2)}, u32[]{:S(2)}) collective-permute-start(bf16[512,256]{1,0:T(8,128)(2,1)} %get-tuple-element.54), channel_id=1, source_target_pairs={{0,5},{1,6},{2,7},{3,0},{4,1},{5,2},{6,3},{7,4},{8,13},{9,14},{10,... | collective-permute-start | bytes 786440 | tf_op jit(solution)/shard_map/ppermute | solution.py:107
  228.1 21.2 %collective-permute-start.14 = (bf16[512,256]{1,0:T(8,128)(2,1)}, bf16[512,256]{1,0:T(8,128)(2,1)}, u32[]{:S(2)}, u32[]{:S(2)}) collective-permute-start(bf16[512,256]{1,0:T(8,128)(2,1)} %get-tuple-element.55), channel_id=1, source_target_pairs={{0,6},{1,7},{2,0},{3,1},{4,2},{5,3},{6,4},{7,5},{8,14},{9,15},{10,... | collective-permute-start | bytes 786440 | tf_op jit(solution)/shard_map/ppermute | solution.py:107
  230.5 18.8 %collective-permute-start.15 = (bf16[512,256]{1,0:T(8,128)(2,1)}, bf16[512,256]{1,0:T(8,128)(2,1)}, u32[]{:S(2)}, u32[]{:S(2)}) collective-permute-start(bf16[512,256]{1,0:T(8,128)(2,1)} %get-tuple-element.56), channel_id=1, source_target_pairs={{0,7},{1,0},{2,1},{3,2},{4,3},{5,4},{6,5},{7,6},{8,15},{9,8},{10,9... | collective-permute-start | bytes 786440 | tf_op jit(solution)/shard_map/ppermute | solution.py:107
  264.3 20.5 %all-to-all-start.4 = ((bf16[8,256,128]{2,1,0:T(8,128)(2,1)}), bf16[8,256,128]{2,1,0:T(8,128)(2,1)S(1)}, u32[]{:S(2)}, u32[]{:S(2)}) async-start(bf16[8,256,128]{2,1,0:T(8,128)(2,1)} %shard_map.78), calls=%async_computation.4 | async-start | bytes 1048576 | tf_op jit(solution)/shard_map/all_to_all | solution.py:497
  284.7 15.1 %all-to-all-start.5 = ((bf16[8,256,128]{2,1,0:T(8,128)(2,1)}), bf16[8,256,128]{2,1,0:T(8,128)(2,1)S(1)}, u32[]{:S(2)}, u32[]{:S(2)}) async-start(bf16[8,256,128]{2,1,0:T(8,128)(2,1)} %shard_map.79), calls=%async_computation.5 | async-start | bytes 1048576 | tf_op jit(solution)/shard_map/all_to_all | solution.py:497
  (23 other events, 604.4 us)

commit v8 on v7

--- a/solution.py
+++ b/solution.py
@@ -324,12 +324,12 @@
     )(place, *own, *ext)
 
 
-def random_kernel(index_ref, count_ref, *refs, groups, spread, half):
+def random_kernel(index_ref, count_ref, *refs, groups, spread):
     part_refs, whole_refs = refs[: spread * groups], refs[spread * groups : spread * groups + CAP - spread]
     q_ref, m_ref, l_ref, a_ref, o_ref, kv_ref, sems = refs[spread * groups + CAP - spread :]
-    pieces, _, piece, lanes = q_ref.shape
-    halves = index_ref.shape[0] // (RANDOM * groups * (piece // TILE))
+    lanes = q_ref.shape[1]
     step = pl.program_id(0)
+    per_step = q_ref.shape[0] // TILE
     part = TILE // groups
     shards = kv_ref.shape[0] // CAP
 
@@ -348,11 +348,10 @@
         for copy in copies:
             copy.wait()
 
-    for i in range(pieces * piece // TILE):
-        home, sub = divmod(i, piece // TILE)
-        t = ((step * pieces + home) * halves + half) * (piece // TILE) + sub
-        rows = (home, 0, pl.ds(sub * TILE, TILE))
-        q2 = split_heads(q_ref[rows])
+    for i in range(per_step):
+        t = step * per_step + i
+        rows = pl.ds(i * TILE, TILE)
+        q2 = split_heads(q_ref[rows, :])
         count = count_ref[t]
         at = [index_ref[t * RANDOM + j] for j in range(RANDOM)]
         scores = []
@@ -362,7 +361,7 @@
             s = score(q2, keys)
             scores.append(s)
             top = s if top is None else jnp.maximum(top, s)
-        m_old = m_ref[rows]
+        m_old = m_ref[rows, :]
         m_old = jnp.concatenate([m_old[:, :1], m_old[:, HEAD_DIM : HEAD_DIM + 1]], axis=0)
         m_new = jnp.maximum(jnp.max(top, axis=1, keepdims=True), m_old)
         alpha = jnp.exp2((m_old - m_new) * SCALE)
@@ -379,42 +378,41 @@
         total = acc[:, lanes:]
         acc = acc[:, :lanes]
         alpha = join_heads(alpha)
-        denominator = l_ref[rows] * alpha + join_heads(total)
-        numerator = a_ref[rows] * alpha + join_heads(acc)
-        o_ref[home, pl.ds(sub * TILE, TILE)] = (numerator / denominator).astype(jnp.bfloat16)
-
-
-def random_attention(index, count, q, parts, whole, m, l, a, half, halves, pieces=4):
+        denominator = l_ref[rows, :] * alpha + join_heads(total)
+        numerator = a_ref[rows, :] * alpha + join_heads(acc)
+        o_ref[rows, :] = (numerator / denominator).astype(jnp.bfloat16)
+
+
+def random_attention(index, count, q, parts, whole, m, l, a, per_step=8):
     rows, lanes = q.shape
     groups = len(parts[0])
     spread = len(parts)
     shards = whole[0].shape[0]
     part = TILE // groups
     flat = [f.reshape(-1, part, 2 * lanes) for slot in parts for f in slot]
-    piece = rows // (groups * halves)
-    block = pl.BlockSpec((pieces, 1, piece, lanes), lambda i, s, c: (i, half, 0, 0))
-    views = [x.reshape(groups, halves, piece, lanes) for x in (q, m, l, a)]
+    block = pl.BlockSpec((per_step * TILE, lanes), lambda i, s, c: (i, 0))
     keys = RANDOM * TILE
     sources = len(flat) + len(whole)
     return pl.pallas_call(
-        functools.partial(random_kernel, groups=groups, spread=spread, half=half),
+        functools.partial(random_kernel, groups=groups, spread=spread),
         grid_spec=pltpu.PrefetchScalarGridSpec(
             num_scalar_prefetch=2,
-            grid=(groups // pieces,),
+            grid=(rows // (per_step * TILE),),
             in_specs=[pl.BlockSpec(memory_space=pl.ANY)] * sources + [block] * 4,
-            out_specs=pl.BlockSpec((pieces, piece, lanes), lambda i, s, c: (i, 0, 0)),
+            out_specs=block,
             scratch_shapes=[
                 pltpu.VMEM((CAP * shards, TILE, 2 * lanes), jnp.bfloat16),
                 pltpu.SemaphoreType.DMA((sources,)),
             ],
         ),
-        out_shape=jax.ShapeDtypeStruct((groups, piece, lanes), jnp.bfloat16),
+        out_shape=jax.ShapeDtypeStruct((rows, lanes), jnp.bfloat16),
         cost_estimate=pl.CostEstimate(
-            flops=8 * rows * keys * lanes // halves,
-            transcendentals=2 * rows * keys // halves,
+            flops=8 * rows * keys * lanes,
+            transcendentals=2 * rows * keys,
             bytes_accessed=rows * lanes * 16 + CAP * shards * TILE * lanes * 4,
         ),
-    )(index, count, *flat, *whole, *views)
+        name="random_attention",
+    )(index, count, *flat, *whole, q, m, l, a)
 
 
 def request_tables(random_tiles, random_count, shard, ctx_count, tiles_here):
@@ -489,20 +487,16 @@
     where = jnp.stack([shard, jnp.int32(tiles_here * ctx_count), here])
     m, l, a, q = local_attention(where, own, ends)
     my_count = lax.dynamic_slice_in_dim(random_count, shard * tiles_here, tiles_here, 0)
-    outs = []
-    for half in range(2):
-        mixed = random_attention(
-            read, my_count, q, fetched, [whole], m, l, a, half, 2, 4 - 2 * half
-        )
-        back = lax.all_to_all(mixed, "head", split_axis=0, concat_axis=0, tiled=True)
-        out = lax.dot_general(
-            back,
-            w_out.reshape(groups, -1, width),
-            (((0, 2), (0, 1)), ((), ())),
-            preferred_element_type=jnp.float32,
-        )
-        outs.append(out.astype(jnp.bfloat16))
-    return jnp.concatenate(outs, axis=0)
+    attended = random_attention(read, my_count, q, fetched, [whole], m, l, a)
+    attended = attended.reshape(groups, rows, -1)
+    returned = lax.all_to_all(attended, "head", split_axis=0, concat_axis=0, tiled=True)
+    out = lax.dot_general(
+        returned,
+        w_out.reshape(groups, -1, width),
+        (((0, 2), (0, 1)), ((), ())),
+        preferred_element_type=jnp.float32,
+    )
+    return out.astype(jnp.bfloat16)
 
 
 def solution(mesh):

time: 303 us -> 297 us (0.980)
  blocking collectives: 0 us -> 20.2 us
  waiting for transfers between devices: 105 us -> 96.1 us
  starting transfers between devices: 88.8 us -> 80 us
  Pallas kernels: 89.5 us -> 82.2 us
    all_to_all x0 -> x1, blocking collectives: none -> 20.2 us  [body(): lax.all_to_all(attended, 'head', split_axis=0, concat_axis=0, tiled=True)]
    all_to_all x2 -> x0, starting transfers between devices: 8.9 us -> none  [body(): lax.all_to_all(mixed, 'head', split_axis=0, concat_axis=0, tiled=True)]
    all_to_all x2 -> x0, waiting for transfers between devices: 8.8 us -> none  [body(): lax.all_to_all(mixed, 'head', split_axis=0, concat_axis=0, tiled=True)]
    pallas_call x2 -> x1, Pallas kernels: 31.4 us -> 24.1 us  [random_attention(): pl.pallas_call(functools.partial(random_kernel, groups=groups, spread=spr...]
  transfers between devices with their start and end apart: 36 -> 34, of which waited for: 12 -> 11; matrix products, arithmetic and copies ran while one was open for 4% -> 3% of each run, Pallas kernels for 23% -> 18%
where the time goes in v8:
time: 297 us; the launch traced here: 296 us
  waiting for transfers between devices  96.1 us (32%)
  Pallas kernels  82.2 us (28%)
  starting transfers between devices  80 us (27%)
  blocking collectives  20.2 us (7%)
  local copies, waits for them, and re-layouts  10.2 us (3%)
  other arithmetic  4.51 us (2%)
    ppermute x28, starting transfers between devices, exchange(): lax.ppermute(pieces[o], axis, [(i, (i + o) % size) for i in range(size)])  42.6 us
    ppermute x28, waiting for transfers between devices, exchange(): lax.ppermute(pieces[o], axis, [(i, (i + o) % size) for i in range(size)])  29.7 us
    pallas_call x3, Pallas kernels, project(): pl.pallas_call(functools.partial(project_kernel, sources=len(xs), weights...  29.1 us
    all_to_all x2, waiting for transfers between devices, body(): got = lax.all_to_all(chunks, 'ctx', split_axis=0, concat_axis=0, tiled=True)  26 us
    ppermute x1, waiting for transfers between devices, body(): before = lax.ppermute(striped[-1:], 'ctx', up)  25.6 us
    pallas_call x1, Pallas kernels, random_attention(): pl.pallas_call(functools.partial(random_kernel, groups=groups, spread=spr...  24.1 us
    all_to_all x1, blocking collectives, body(): lax.all_to_all(attended, 'head', split_axis=0, concat_axis=0, tiled=True)  20.2 us
    all_to_all x2, starting transfers between devices, body(): got = lax.all_to_all(chunks, 'ctx', split_axis=0, concat_axis=0, tiled=True)  17.1 us
  transfers between devices with their start and end apart: 34, of which 11 were waited for; matrix products, arithmetic and copies ran while one was open for 3% of the time, Pallas kernels for 18%

profile of v8, /device:TPU:6, one launch (start us, length us, event | category | flops | bytes accessed | tf_op | source)
XLA Modules:
  0.0 295.9 jit_solution(11646904151990502131)
XLA Ops:
  0.0 2.5 copy.17
  2.5 4.6 %all-to-all-start = ((bf16[8,4,16,1024]{3,2,1,0:T(8,128)(2,1)}), bf16[8,4,16,1024]{3,2,1,0:T(8,128)(2,1)S(1)}, u32[]{:S(2)}, u32[]{:S(2)}) async-start(bf16[8,4,16,1024]{3,2,1,0:T(8,128)(2,1)} %bitcast.40), calls=%async_computation | async-start | bytes 2097152 | tf_op jit(solution)/shard_map/all_to_all | solution.py:455
  11.5 11.5 %all-to-all-done = bf16[8,4,16,1024]{3,2,1,0:T(8,128)(2,1)S(1)} async-done(((bf16[8,4,16,1024]{3,2,1,0:T(8,128)(2,1)}), bf16[8,4,16,1024]{3,2,1,0:T(8,128)(2,1)S(1)}, u32[]{:S(2)}, u32[]{:S(2)}) %all-to-all-start) | async-done | bytes 1048608 | tf_op jit(solution)/shard_map/all_to_all | solution.py:455
  24.0 3.2 %shard_map.73 = bf16[32,136,128]{2,1,0:T(8,128)(2,1)} custom-call(s32[32]{0:T(128)} %get-tuple-element.83.index_ref, bf16[32,16,1024]{2,1,0:T(8,128)(2,1)} %bitcast.37), custom_call_target="tpu_custom_call" | custom-call | bytes 4194304 | tf_op jit(solution)/shard_map/pallas_call | solution.py:142
  27.2 11.6 %all-to-all-start.1 = ((bf16[32,136,128]{2,1,0:T(8,128)(2,1)}), bf16[32,136,128]{2,1,0:T(8,128)(2,1)S(1)}, u32[]{:S(2)}, u32[]{:S(2)}) async-start(bf16[32,136,128]{2,1,0:T(8,128)(2,1)} %shard_map.73), calls=%async_computation.1 | async-start | bytes 2228224 | tf_op jit(solution)/shard_map/all_to_all | solution.py:474
  38.7 3.2 %shard_map.75.chunks_ref = bf16[32,136,128]{2,1,0:T(8,128)(2,1)} custom-call(s32[32]{0:T(128)} %get-tuple-element.82.index_ref, bf16[32,16,1024]{2,1,0:T(8,128)(2,1)} %bitcast.38), custom_call_target="tpu_custom_call" | custom-call | bytes 4194304 | tf_op jit(solution)/shard_map/pallas_call | solution.py:142
  42.0 26.0 %all-to-all-done.1.refs_0_.got_ref = bf16[32,136,128]{2,1,0:T(8,128)(2,1)S(1)} async-done(((bf16[32,136,128]{2,1,0:T(8,128)(2,1)}), bf16[32,136,128]{2,1,0:T(8,128)(2,1)S(1)}, u32[]{:S(2)}, u32[]{:S(2)}) %all-to-all-start.1) | async-done | bytes 1114144 | tf_op jit(solution)/shard_map/all_to_all | solution.py:474
  70.3 5.6 %all-to-all-start.2 = ((bf16[32,136,128]{2,1,0:T(8,128)(2,1)}), bf16[32,136,128]{2,1,0:T(8,128)(2,1)S(1)}, u32[]{:S(2)}, u32[]{:S(2)}) async-start(bf16[32,136,128]{2,1,0:T(8,128)(2,1)} %insert_block.1), calls=%async_computation.2 | async-start | bytes 2228224 | tf_op jit(solution)/shard_map/all_to_all | solution.py:474
  75.9 10.9 %shard_map.77 = (bf16[512,384]{1,0:T(8,128)(2,1)}, bf16[512,384]{1,0:T(8,128)(2,1)}, bf16[512,384]{1,0:T(8,128)(2,1)}, bf16[512,384]{1,0:T(8,128)(2,1)}, bf16[51...) custom-call(s32[1]{0:T(128)} %bitcast.here_ref, ...), custom_call_target="tpu_custom_call" | custom-call | flops 3221225472 | bytes 10485760 | tf_op jit(solution)/shard_map/pallas_call | solution.py:78
  88.8 2.7 collective-permute-start.19
  92.4 6.6 %collective-permute-done.16.refs_1_ = bf16[512,384]{1,0:T(8,128)(2,1)} collective-permute-done((bf16[512,384]{1,0:T(8,128)(2,1)}, bf16[512,384]{1,0:T(8,128)(2,1)}, u32[]{:S(2)}, u32[]{:S(2)}) %collective-permute-start.16) | collective-permute-done | bytes 393248 | tf_op jit(solution)/shard_map/ppermute | solution.py:107
  100.3 6.8 %collective-permute-start.22 = (bf16[512,384]{1,0:T(8,128)(2,1)}, bf16[512,384]{1,0:T(8,128)(2,1)}, u32[]{:S(2)}, u32[]{:S(2)}) collective-permute-start(bf16[512,384]{1,0:T(8,128)(2,1)} %get-tuple-element.64), channel_id=1, source_target_pairs={{0,7},{1,0},{2,1},{3,2},{4,3},{5,4},{6,5},{7,6},{8,15},{9,8},{10,9... | collective-permute-start | bytes 1179656 | tf_op jit(solution)/shard_map/ppermute | solution.py:107
  107.1 8.2 %collective-permute-done.18.refs_3_ = bf16[512,384]{1,0:T(8,128)(2,1)} collective-permute-done((bf16[512,384]{1,0:T(8,128)(2,1)}, bf16[512,384]{1,0:T(8,128)(2,1)}, u32[]{:S(2)}, u32[]{:S(2)}) %collective-permute-start.18) | collective-permute-done | bytes 393248 | tf_op jit(solution)/shard_map/ppermute | solution.py:107
  116.7 5.2 %collective-permute-done.20.refs_5_ = bf16[512,384]{1,0:T(8,128)(2,1)} collective-permute-done((bf16[512,384]{1,0:T(8,128)(2,1)}, bf16[512,384]{1,0:T(8,128)(2,1)}, u32[]{:S(2)}, u32[]{:S(2)}) %collective-permute-start.20) | collective-permute-done | bytes 393248 | tf_op jit(solution)/shard_map/ppermute | solution.py:107
  121.8 3.0 %collective-permute-done.22.refs_7_ = bf16[512,384]{1,0:T(8,128)(2,1)} collective-permute-done((bf16[512,384]{1,0:T(8,128)(2,1)}, bf16[512,384]{1,0:T(8,128)(2,1)}, u32[]{:S(2)}, u32[]{:S(2)}) %collective-permute-start.22) | collective-permute-done | bytes 393248 | tf_op jit(solution)/shard_map/ppermute | solution.py:107
  124.9 4.2 %pick_kv.1 = bf16[32,128,256]{2,1,0:T(8,128)(2,1)} custom-call(s32[32]{0:T(128)} %get-tuple-element.81.index_ref, s32[1]{0:T(128)} %bitcast.here_ref, bf16[512,384]{1,0:T(8,128)(2,1)} %get-tuple-element.57.refs_0_, bf16[512,384]{1,0:T(8,128)(2,1)} %collective-permute-done.16.refs_1_, bf16[512,384]{1,0:T(8,128)(2,1)} %collective-permute-done.17.refs_2_, ...), custom_call_target="tpu_custom_call" | custom-call | bytes 5242880 | tf_op jit(solution)/shard_map/pick_kv/pallas_call | solution.py:203
  130.1 9.8 %all-to-all-start.3 = ((bf16[32,128,256]{2,1,0:T(8,128)(2,1)}), bf16[32,128,256]{2,1,0:T(8,128)(2,1)}, u32[]{:S(2)}, u32[]{:S(2)}) async-start(bf16[32,128,256]{2,1,0:T(8,128)(2,1)} %pick_kv.1), calls=%async_computation.3 | async-start | bytes 4194304 | tf_op jit(solution)/shard_map/all_to_all | solution.py:485
  141.2 3.4 %collective-permute-start.7 = (bf16[1,16,1024]{2,1,0:T(8,128)(2,1)S(1)}, bf16[1,16,1024]{2,1,0:T(8,128)(2,1)S(1)}, u32[]{:S(2)}, u32[]{:S(2)}) collective-permute-start(bf16[1,16,1024]{2,1,0:T(8,128)(2,1)S(1)} %get-tuple-element.77), channel_id=1, source_target_pairs={{0,8},{8,16},{16,24},{24,32},{32,40},{40,48},{48,56},{56,64},{64,7... | collective-permute-start | bytes 98312 | tf_op jit(solution)/shard_map/ppermute | solution.py:465
  144.6 2.5 collective-permute-start.8
  147.1 8.9 %shard_map.74 = (bf16[512,256]{1,0:T(8,128)(2,1)}, bf16[512,256]{1,0:T(8,128)(2,1)}, bf16[512,256]{1,0:T(8,128)(2,1)}, bf16[512,256]{1,0:T(8,128)(2,1)}, bf16[51...) custom-call(s32[1]{0:T(128)} %bitcast.here_ref, ...), custom_call_target="tpu_custom_call" | custom-call | flops 2147483648 | bytes 7340032 | tf_op jit(solution)/shard_map/pallas_call | solution.py:78
  159.4 25.6 %collective-permute-done.7 = bf16[1,16,1024]{2,1,0:T(8,128)(2,1)S(1)} collective-permute-done((bf16[1,16,1024]{2,1,0:T(8,128)(2,1)S(1)}, bf16[1,16,1024]{2,1,0:T(8,128)(2,1)S(1)}, u32[]{:S(2)}, u32[]{:S(2)}) %collective-permute-start.7) | collective-permute-done | bytes 32800 | tf_op jit(solution)/shard_map/ppermute | solution.py:465
  185.0 3.4 %collective-permute-done.8 = bf16[1,16,1024]{2,1,0:T(8,128)(2,1)S(1)} collective-permute-done((bf16[1,16,1024]{2,1,0:T(8,128)(2,1)S(1)}, bf16[1,16,1024]{2,1,0:T(8,128)(2,1)S(1)}, u32[]{:S(2)}, u32[]{:S(2)}) %collective-permute-start.8) | collective-permute-done | bytes 32800 | tf_op jit(solution)/shard_map/ppermute | solution.py:466
  189.6 3.9 %collective-permute-start.3 = (bf16[512,256]{1,0:T(8,128)(2,1)}, bf16[512,256]{1,0:T(8,128)(2,1)}, u32[]{:S(2)}, u32[]{:S(2)}) collective-permute-start(bf16[512,256]{1,0:T(8,128)(2,1)} %get-tuple-element.45), channel_id=1, source_target_pairs={{0,4},{1,5},{2,6},{3,7},{4,0},{5,1},{6,2},{7,3},{8,12},{9,13},{10,... | collective-permute-start | bytes 786440 | tf_op jit(solution)/shard_map/ppermute | solution.py:107
  193.5 9.3 %shard_map.76 = (bf16[512,256]{1,0:T(8,128)(2,1)}, bf16[512,256]{1,0:T(8,128)(2,1)}, bf16[512,256]{1,0:T(8,128)(2,1)}, bf16[512,256]{1,0:T(8,128)(2,1)}, bf16[51...) custom-call(s32[1]{0:T(128)} %bitcast.here_ref, ...), custom_call_target="tpu_custom_call" | custom-call | flops 2415919104 | bytes 7733248 | tf_op jit(solution)/shard_map/pallas_call | solution.py:78
  203.2 3.1 %collective-permute-start.25 = (bf16[64,256]{1,0:T(8,128)(2,1)}, bf16[64,256]{1,0:T(8,128)(2,1)S(1)}, u32[]{:S(2)}, u32[]{:S(2)}) collective-permute-start(bf16[64,256]{1,0:T(8,128)(2,1)} %get-tuple-element.68), channel_id=1, source_target_pairs={{0,3},{1,4},{2,5},{3,6},{4,7},{5,0},{6,1},{7,2},{8,11},{9,12},{10,... | collective-permute-start | bytes 98312 | tf_op jit(solution)/shard_map/ppermute | solution.py:107
  206.2 7.5 %collective-permute-start.26 = (bf16[64,256]{1,0:T(8,128)(2,1)}, bf16[64,256]{1,0:T(8,128)(2,1)S(1)}, u32[]{:S(2)}, u32[]{:S(2)}) collective-permute-start(bf16[64,256]{1,0:T(8,128)(2,1)} %get-tuple-element.69), channel_id=1, source_target_pairs={{0,4},{1,5},{2,6},{3,7},{4,0},{5,1},{6,2},{7,3},{8,12},{9,13},{10,... | collective-permute-start | bytes 98312 | tf_op jit(solution)/shard_map/ppermute | solution.py:107
  214.0 2.6 collective-permute-start.10
  220.3 4.0 %collective-permute-done.27.refs_13_ = bf16[64,256]{1,0:T(8,128)(2,1)S(1)} collective-permute-done((bf16[64,256]{1,0:T(8,128)(2,1)}, bf16[64,256]{1,0:T(8,128)(2,1)S(1)}, u32[]{:S(2)}, u32[]{:S(2)}) %collective-permute-start.27) | collective-permute-done | bytes 32800 | tf_op jit(solution)/shard_map/ppermute | solution.py:107
  228.1 2.5 collective-permute-start.14
  232.3 17.0 %local_attention.1 = (f32[4096,128]{1,0:T(8,128)}, f32[4096,128]{1,0:T(8,128)}, f32[4096,128]{1,0:T(8,128)}, bf16[4096,128]{1,0:T(8,128)(2,1)}) custom-call(s32[3]{0:T(128)} %pad_add_fusion.place_ref, bf16[512,384]{1,0:T(8,128)(2,1)} %get-tuple-element.57.refs_0_, bf16[512,384]{1,0:T(8,128)(2,1)} %collective-permute-done.16.refs_1_, ...), custom_call_target="tpu_custom_call" | custom-call | flops 2684354560 | bytes 10485760 | tf_op jit(solution)/shard_map/local_attention/pallas_call | solution.py:304
  249.4 24.1 %random_attention.1 = bf16[4096,128]{1,0:T(8,128)(2,1)} custom-call(s32[384]{0:T(512)} %add_select_fusion.2.index_ref, s32[32]{0:T(128)} %dynamic_slice.8.count_ref, bf16[32,16,256]{2,1,0:T(8,128)(2,1)} %bitcast.50, bf16[32,16,256]{2,1,0:T(8,128)(2,1)} %bitcast.47, bf16[32,16,256]{2,1,0:T(8,128)(2,1)} %bitcast.7.refs_2_, ...), custom_call_target="tpu_custom_call" | custom-call | flops 6442450944 | bytes 14680064 | tf_op jit(solution)/shard_map/random_attention/pallas_call | solution.py:396
  273.5 20.2 %all_to_all.25 = bf16[8,512,128]{2,1,0:T(8,128)(2,1)S(1)} all-to-all(bf16[8,512,128]{2,1,0:T(8,128)(2,1)} %bitcast.42), channel_id=1, replica_groups=mesh['ctx'=32,'head'=8] {'head'}, dimensions={0} | all-to-all | bytes 2097152 | tf_op jit(solution)/shard_map/all_to_all | solution.py:492
  (112 shorter events, 32.0 us)
Async XLA Ops:
  2.5 20.5 %all-to-all-start = ((bf16[8,4,16,1024]{3,2,1,0:T(8,128)(2,1)}), bf16[8,4,16,1024]{3,2,1,0:T(8,128)(2,1)S(1)}, u32[]{:S(2)}, u32[]{:S(2)}) async-start(bf16[8,4,16,1024]{3,2,1,0:T(8,128)(2,1)} %bitcast.40), calls=%async_computation | async-start | bytes 2097152 | tf_op jit(solution)/shard_map/all_to_all | solution.py:455
  27.2 40.7 %all-to-all-start.1 = ((bf16[32,136,128]{2,1,0:T(8,128)(2,1)}), bf16[32,136,128]{2,1,0:T(8,128)(2,1)S(1)}, u32[]{:S(2)}, u32[]{:S(2)}) async-start(bf16[32,136,128]{2,1,0:T(8,128)(2,1)} %shard_map.73), calls=%async_computation.1 | async-start | bytes 2228224 | tf_op jit(solution)/shard_map/all_to_all | solution.py:474
  70.3 58.8 %all-to-all-start.2 = ((bf16[32,136,128]{2,1,0:T(8,128)(2,1)}), bf16[32,136,128]{2,1,0:T(8,128)(2,1)S(1)}, u32[]{:S(2)}, u32[]{:S(2)}) async-start(bf16[32,136,128]{2,1,0:T(8,128)(2,1)} %insert_block.1), calls=%async_computation.2 | async-start | bytes 2228224 | tf_op jit(solution)/shard_map/all_to_all | solution.py:474
  86.7 12.3 %collective-permute-start.16 = (bf16[512,384]{1,0:T(8,128)(2,1)}, bf16[512,384]{1,0:T(8,128)(2,1)}, u32[]{:S(2)}, u32[]{:S(2)}) collective-permute-start(bf16[512,384]{1,0:T(8,128)(2,1)} %get-tuple-element.58), channel_id=1, source_target_pairs={{0,1},{1,2},{2,3},{3,4},{4,5},{5,6},{6,7},{7,0},{8,9},{9,10},{10,1... | collective-permute-start | bytes 1179656 | tf_op jit(solution)/shard_map/ppermute | solution.py:107
  86.7 13.6 %collective-permute-start.17 = (bf16[512,384]{1,0:T(8,128)(2,1)}, bf16[512,384]{1,0:T(8,128)(2,1)}, u32[]{:S(2)}, u32[]{:S(2)}) collective-permute-start(bf16[512,384]{1,0:T(8,128)(2,1)} %get-tuple-element.59), channel_id=1, source_target_pairs={{0,2},{1,3},{2,4},{3,5},{4,6},{5,7},{6,0},{7,1},{8,10},{9,11},{10,... | collective-permute-start | bytes 1179656 | tf_op jit(solution)/shard_map/ppermute | solution.py:107
  87.4 28.0 %collective-permute-start.18 = (bf16[512,384]{1,0:T(8,128)(2,1)}, bf16[512,384]{1,0:T(8,128)(2,1)}, u32[]{:S(2)}, u32[]{:S(2)}) collective-permute-start(bf16[512,384]{1,0:T(8,128)(2,1)} %get-tuple-element.60), channel_id=1, source_target_pairs={{0,3},{1,4},{2,5},{3,6},{4,7},{5,0},{6,1},{7,2},{8,11},{9,12},{10,... | collective-permute-start | bytes 1179656 | tf_op jit(solution)/shard_map/ppermute | solution.py:107
  88.8 27.9 %collective-permute-start.19 = (bf16[512,384]{1,0:T(8,128)(2,1)}, bf16[512,384]{1,0:T(8,128)(2,1)}, u32[]{:S(2)}, u32[]{:S(2)}) collective-permute-start(bf16[512,384]{1,0:T(8,128)(2,1)} %get-tuple-element.61), channel_id=1, source_target_pairs={{0,4},{1,5},{2,6},{3,7},{4,0},{5,1},{6,2},{7,3},{8,12},{9,13},{10,... | collective-permute-start | bytes 1179656 | tf_op jit(solution)/shard_map/ppermute | solution.py:107
  91.4 30.4 %collective-permute-start.20 = (bf16[512,384]{1,0:T(8,128)(2,1)}, bf16[512,384]{1,0:T(8,128)(2,1)}, u32[]{:S(2)}, u32[]{:S(2)}) collective-permute-start(bf16[512,384]{1,0:T(8,128)(2,1)} %get-tuple-element.62), channel_id=1, source_target_pairs={{0,5},{1,6},{2,7},{3,0},{4,1},{5,2},{6,3},{7,4},{8,13},{9,14},{10,... | collective-permute-start | bytes 1179656 | tf_op jit(solution)/shard_map/ppermute | solution.py:107
  99.0 22.8 %collective-permute-start.21 = (bf16[512,384]{1,0:T(8,128)(2,1)}, bf16[512,384]{1,0:T(8,128)(2,1)}, u32[]{:S(2)}, u32[]{:S(2)}) collective-permute-start(bf16[512,384]{1,0:T(8,128)(2,1)} %get-tuple-element.63), channel_id=1, source_target_pairs={{0,6},{1,7},{2,0},{3,1},{4,2},{5,3},{6,4},{7,5},{8,14},{9,15},{10,... | collective-permute-start | bytes 1179656 | tf_op jit(solution)/shard_map/ppermute | solution.py:107
  100.3 24.5 %collective-permute-start.22 = (bf16[512,384]{1,0:T(8,128)(2,1)}, bf16[512,384]{1,0:T(8,128)(2,1)}, u32[]{:S(2)}, u32[]{:S(2)}) collective-permute-start(bf16[512,384]{1,0:T(8,128)(2,1)} %get-tuple-element.64), channel_id=1, source_target_pairs={{0,7},{1,0},{2,1},{3,2},{4,3},{5,4},{6,5},{7,6},{8,15},{9,8},{10,9... | collective-permute-start | bytes 1179656 | tf_op jit(solution)/shard_map/ppermute | solution.py:107
  130.1 119.2 %all-to-all-start.3 = ((bf16[32,128,256]{2,1,0:T(8,128)(2,1)}), bf16[32,128,256]{2,1,0:T(8,128)(2,1)}, u32[]{:S(2)}, u32[]{:S(2)}) async-start(bf16[32,128,256]{2,1,0:T(8,128)(2,1)} %pick_kv.1), calls=%async_computation.3 | async-start | bytes 4194304 | tf_op jit(solution)/shard_map/all_to_all | solution.py:485
  141.2 43.8 %collective-permute-start.7 = (bf16[1,16,1024]{2,1,0:T(8,128)(2,1)S(1)}, bf16[1,16,1024]{2,1,0:T(8,128)(2,1)S(1)}, u32[]{:S(2)}, u32[]{:S(2)}) collective-permute-start(bf16[1,16,1024]{2,1,0:T(8,128)(2,1)S(1)} %get-tuple-element.77), channel_id=1, source_target_pairs={{0,8},{8,16},{16,24},{24,32},{32,40},{40,48},{48,56},{56,64},{64,7... | collective-permute-start | bytes 98312 | tf_op jit(solution)/shard_map/ppermute | solution.py:465
  144.6 43.8 %collective-permute-start.8 = (bf16[1,16,1024]{2,1,0:T(8,128)(2,1)S(1)}, bf16[1,16,1024]{2,1,0:T(8,128)(2,1)S(1)}, u32[]{:S(2)}, u32[]{:S(2)}) collective-permute-start(bf16[1,16,1024]{2,1,0:T(8,128)(2,1)S(1)} %get-tuple-element.78), channel_id=1, source_target_pairs={{8,0},{16,8},{24,16},{32,24},{40,32},{48,40},{56,48},{64,56},{72,6... | collective-permute-start | bytes 98312 | tf_op jit(solution)/shard_map/ppermute | solution.py:466
  156.0 33.1 %collective-permute-start.4 = (bf16[512,256]{1,0:T(8,128)(2,1)}, bf16[512,256]{1,0:T(8,128)(2,1)S(1)}, u32[]{:S(2)}, u32[]{:S(2)}) collective-permute-start(bf16[512,256]{1,0:T(8,128)(2,1)} %get-tuple-element.46), channel_id=1, source_target_pairs={{0,5},{1,6},{2,7},{3,0},{4,1},{5,2},{6,3},{7,4},{8,13},{9,14},{10,... | collective-permute-start | bytes 786440 | tf_op jit(solution)/shard_map/ppermute | solution.py:107
  156.2 33.4 %collective-permute-start.5 = (bf16[512,256]{1,0:T(8,128)(2,1)}, bf16[512,256]{1,0:T(8,128)(2,1)S(1)}, u32[]{:S(2)}, u32[]{:S(2)}) collective-permute-start(bf16[512,256]{1,0:T(8,128)(2,1)} %get-tuple-element.47), channel_id=1, source_target_pairs={{0,6},{1,7},{2,0},{3,1},{4,2},{5,3},{6,4},{7,5},{8,14},{9,15},{10,... | collective-permute-start | bytes 786440 | tf_op jit(solution)/shard_map/ppermute | solution.py:107
  158.9 44.0 %collective-permute-start.6 = (bf16[512,256]{1,0:T(8,128)(2,1)}, bf16[512,256]{1,0:T(8,128)(2,1)S(1)}, u32[]{:S(2)}, u32[]{:S(2)}) collective-permute-start(bf16[512,256]{1,0:T(8,128)(2,1)} %get-tuple-element.48), channel_id=1, source_target_pairs={{0,7},{1,0},{2,1},{3,2},{4,3},{5,4},{6,5},{7,6},{8,15},{9,8},{10,9... | collective-permute-start | bytes 786440 | tf_op jit(solution)/shard_map/ppermute | solution.py:107
  189.0 14.0 %collective-permute-start = (bf16[512,256]{1,0:T(8,128)(2,1)}, bf16[512,256]{1,0:T(8,128)(2,1)S(1)}, u32[]{:S(2)}, u32[]{:S(2)}) collective-permute-start(bf16[512,256]{1,0:T(8,128)(2,1)} %get-tuple-element.42), channel_id=1, source_target_pairs={{0,1},{1,2},{2,3},{3,4},{4,5},{5,6},{6,7},{7,0},{8,9},{9,10},{10,1... | collective-permute-start | bytes 786440 | tf_op jit(solution)/shard_map/ppermute | solution.py:107
  189.0 14.1 %collective-permute-start.1 = (bf16[512,256]{1,0:T(8,128)(2,1)}, bf16[512,256]{1,0:T(8,128)(2,1)}, u32[]{:S(2)}, u32[]{:S(2)}) collective-permute-start(bf16[512,256]{1,0:T(8,128)(2,1)} %get-tuple-element.43), channel_id=1, source_target_pairs={{0,2},{1,3},{2,4},{3,5},{4,6},{5,7},{6,0},{7,1},{8,10},{9,11},{10,... | collective-permute-start | bytes 786440 | tf_op jit(solution)/shard_map/ppermute | solution.py:107
  189.1 17.2 %collective-permute-start.2 = (bf16[512,256]{1,0:T(8,128)(2,1)}, bf16[512,256]{1,0:T(8,128)(2,1)}, u32[]{:S(2)}, u32[]{:S(2)}) collective-permute-start(bf16[512,256]{1,0:T(8,128)(2,1)} %get-tuple-element.44), channel_id=1, source_target_pairs={{0,3},{1,4},{2,5},{3,6},{4,7},{5,0},{6,1},{7,2},{8,11},{9,12},{10,... | collective-permute-start | bytes 786440 | tf_op jit(solution)/shard_map/ppermute | solution.py:107
  189.6 24.1 %collective-permute-start.3 = (bf16[512,256]{1,0:T(8,128)(2,1)}, bf16[512,256]{1,0:T(8,128)(2,1)}, u32[]{:S(2)}, u32[]{:S(2)}) collective-permute-start(bf16[512,256]{1,0:T(8,128)(2,1)} %get-tuple-element.45), channel_id=1, source_target_pairs={{0,4},{1,5},{2,6},{3,7},{4,0},{5,1},{6,2},{7,3},{8,12},{9,13},{10,... | collective-permute-start | bytes 786440 | tf_op jit(solution)/shard_map/ppermute | solution.py:107
  202.9 11.1 %collective-permute-start.23 = (bf16[64,256]{1,0:T(8,128)(2,1)}, bf16[64,256]{1,0:T(8,128)(2,1)S(1)}, u32[]{:S(2)}, u32[]{:S(2)}) collective-permute-start(bf16[64,256]{1,0:T(8,128)(2,1)} %get-tuple-element.66), channel_id=1, source_target_pairs={{0,1},{1,2},{2,3},{3,4},{4,5},{5,6},{6,7},{7,0},{8,9},{9,10},{10,1... | collective-permute-start | bytes 98312 | tf_op jit(solution)/shard_map/ppermute | solution.py:107
  203.1 13.9 %collective-permute-start.24 = (bf16[64,256]{1,0:T(8,128)(2,1)}, bf16[64,256]{1,0:T(8,128)(2,1)S(1)}, u32[]{:S(2)}, u32[]{:S(2)}) collective-permute-start(bf16[64,256]{1,0:T(8,128)(2,1)} %get-tuple-element.67), channel_id=1, source_target_pairs={{0,2},{1,3},{2,4},{3,5},{4,6},{5,7},{6,0},{7,1},{8,10},{9,11},{10,... | collective-permute-start | bytes 98312 | tf_op jit(solution)/shard_map/ppermute | solution.py:107
  203.2 15.1 %collective-permute-start.25 = (bf16[64,256]{1,0:T(8,128)(2,1)}, bf16[64,256]{1,0:T(8,128)(2,1)S(1)}, u32[]{:S(2)}, u32[]{:S(2)}) collective-permute-start(bf16[64,256]{1,0:T(8,128)(2,1)} %get-tuple-element.68), channel_id=1, source_target_pairs={{0,3},{1,4},{2,5},{3,6},{4,7},{5,0},{6,1},{7,2},{8,11},{9,12},{10,... | collective-permute-start | bytes 98312 | tf_op jit(solution)/shard_map/ppermute | solution.py:107
  206.2 13.4 %collective-permute-start.26 = (bf16[64,256]{1,0:T(8,128)(2,1)}, bf16[64,256]{1,0:T(8,128)(2,1)S(1)}, u32[]{:S(2)}, u32[]{:S(2)}) collective-permute-start(bf16[64,256]{1,0:T(8,128)(2,1)} %get-tuple-element.69), channel_id=1, source_target_pairs={{0,4},{1,5},{2,6},{3,7},{4,0},{5,1},{6,2},{7,3},{8,12},{9,13},{10,... | collective-permute-start | bytes 98312 | tf_op jit(solution)/shard_map/ppermute | solution.py:107
  213.7 14.4 %collective-permute-start.9 = (bf16[512,256]{1,0:T(8,128)(2,1)}, bf16[512,256]{1,0:T(8,128)(2,1)S(1)}, u32[]{:S(2)}, u32[]{:S(2)}) collective-permute-start(bf16[512,256]{1,0:T(8,128)(2,1)} %get-tuple-element.50), channel_id=1, source_target_pairs={{0,1},{1,2},{2,3},{3,4},{4,5},{5,6},{6,7},{7,0},{8,9},{9,10},{10,1... | collective-permute-start | bytes 786440 | tf_op jit(solution)/shard_map/ppermute | solution.py:107
  214.0 16.6 %collective-permute-start.10 = (bf16[512,256]{1,0:T(8,128)(2,1)}, bf16[512,256]{1,0:T(8,128)(2,1)S(1)}, u32[]{:S(2)}, u32[]{:S(2)}) collective-permute-start(bf16[512,256]{1,0:T(8,128)(2,1)} %get-tuple-element.51), channel_id=1, source_target_pairs={{0,2},{1,3},{2,4},{3,5},{4,6},{5,7},{6,0},{7,1},{8,10},{9,11},{10,... | collective-permute-start | bytes 786440 | tf_op jit(solution)/shard_map/ppermute | solution.py:107
  216.9 7.4 %collective-permute-start.27 = (bf16[64,256]{1,0:T(8,128)(2,1)}, bf16[64,256]{1,0:T(8,128)(2,1)S(1)}, u32[]{:S(2)}, u32[]{:S(2)}) collective-permute-start(bf16[64,256]{1,0:T(8,128)(2,1)} %get-tuple-element.70), channel_id=1, source_target_pairs={{0,5},{1,6},{2,7},{3,0},{4,1},{5,2},{6,3},{7,4},{8,13},{9,14},{10,... | collective-permute-start | bytes 98312 | tf_op jit(solution)/shard_map/ppermute | solution.py:107
  224.3 25.0 %collective-permute-start.11 = (bf16[512,256]{1,0:T(8,128)(2,1)}, bf16[512,256]{1,0:T(8,128)(2,1)}, u32[]{:S(2)}, u32[]{:S(2)}) collective-permute-start(bf16[512,256]{1,0:T(8,128)(2,1)} %get-tuple-element.52), channel_id=1, source_target_pairs={{0,3},{1,4},{2,5},{3,6},{4,7},{5,0},{6,1},{7,2},{8,11},{9,12},{10,... | collective-permute-start | bytes 786440 | tf_op jit(solution)/shard_map/ppermute | solution.py:107
  224.3 25.0 %collective-permute-start.12 = (bf16[512,256]{1,0:T(8,128)(2,1)}, bf16[512,256]{1,0:T(8,128)(2,1)}, u32[]{:S(2)}, u32[]{:S(2)}) collective-permute-start(bf16[512,256]{1,0:T(8,128)(2,1)} %get-tuple-element.53), channel_id=1, source_target_pairs={{0,4},{1,5},{2,6},{3,7},{4,0},{5,1},{6,2},{7,3},{8,12},{9,13},{10,... | collective-permute-start | bytes 786440 | tf_op jit(solution)/shard_map/ppermute | solution.py:107
  226.2 23.1 %collective-permute-start.13 = (bf16[512,256]{1,0:T(8,128)(2,1)}, bf16[512,256]{1,0:T(8,128)(2,1)}, u32[]{:S(2)}, u32[]{:S(2)}) collective-permute-start(bf16[512,256]{1,0:T(8,128)(2,1)} %get-tuple-element.54), channel_id=1, source_target_pairs={{0,5},{1,6},{2,7},{3,0},{4,1},{5,2},{6,3},{7,4},{8,13},{9,14},{10,... | collective-permute-start | bytes 786440 | tf_op jit(solution)/shard_map/ppermute | solution.py:107
  228.1 21.3 %collective-permute-start.14 = (bf16[512,256]{1,0:T(8,128)(2,1)}, bf16[512,256]{1,0:T(8,128)(2,1)}, u32[]{:S(2)}, u32[]{:S(2)}) collective-permute-start(bf16[512,256]{1,0:T(8,128)(2,1)} %get-tuple-element.55), channel_id=1, source_target_pairs={{0,6},{1,7},{2,0},{3,1},{4,2},{5,3},{6,4},{7,5},{8,14},{9,15},{10,... | collective-permute-start | bytes 786440 | tf_op jit(solution)/shard_map/ppermute | solution.py:107
  230.6 18.8 %collective-permute-start.15 = (bf16[512,256]{1,0:T(8,128)(2,1)}, bf16[512,256]{1,0:T(8,128)(2,1)}, u32[]{:S(2)}, u32[]{:S(2)}) collective-permute-start(bf16[512,256]{1,0:T(8,128)(2,1)} %get-tuple-element.56), channel_id=1, source_target_pairs={{0,7},{1,0},{2,1},{3,2},{4,3},{5,4},{6,5},{7,6},{8,15},{9,8},{10,9... | collective-permute-start | bytes 786440 | tf_op jit(solution)/shard_map/ppermute | solution.py:107
  (21 other events, 560.0 us)
